TPU v7x, 32 devices: a whole 2x2x4 slice. The times are simulated.
32 devices in a mesh: groups: 2 (over y), ctx: 4 (over z), heads: 4 (over x, core).
Axes of the slice: x: 2, y: 2, z: 4, core: 2. Of those that a mesh axis runs over, the one named last changes fastest.
Arguments:
- ssm_input: bfloat16 [2048, 8192], P(('groups', 'ctx'), 'heads'), parts along dimension 0, may hold values from -6 to 6
- decay_log: float32 [2048, 128], P(('groups', 'ctx'), 'heads'), parts along dimension 0
- state_write: bfloat16 [2048, 128], P(('groups', 'ctx')), parts along dimension 0, may hold values from -2 to 2
- state_read: bfloat16 [2048, 128], P(('groups', 'ctx')), parts along dimension 0, may hold values from -2 to 2
- skip_scale: float32 [128], P('heads'), may hold values from 0.5 to 3
- gate_input: bfloat16 [2048, 8192], P(('groups', 'ctx'), 'heads'), parts along dimension 0, may hold values from -6 to 6
- ssm_gain: float32 [8192], P('heads'), may hold values from 0.1 to 1.9
- out_weight: bfloat16 [8192, 4096], P('heads', 'ctx'), may hold values from -0.0625 to 0.0625
- residual_in: bfloat16 [2048, 4096], P(('groups', 'ctx'), 'heads'), parts along dimension 0, may hold values from -24 to 24
- moe_gain: float32 [4096], P('heads'), may hold values from 0.1 to 1.9
- down_latent: bfloat16 [4096, 1024], P('heads'), may hold values from -0.09375 to 0.09375
- expert_up: bfloat16 [8, 1024, 2688], P('ctx', None, 'heads'), may hold values from -0.1875 to 0.1875
- expert_down: bfloat16 [8, 2688, 1024], P('ctx', 'heads'), may hold values from -0.125 to 0.125
- up_latent: bfloat16 [1024, 4096], P(None, 'heads'), may hold values from -0.1875 to 0.1875
- expert_ids: int32 [2048, 22], P(('groups', 'ctx')), parts along dimension 0, may hold values from 0 to 511, as said below
- combine_fixed: int32 [2048, 22], P(('groups', 'ctx')), parts along dimension 0, may hold values from 1 to 65535
Outputs:
- layer_out: bfloat16 [2048, 4096], P(('groups', 'ctx'), 'heads'), parts along dimension 0
There are 2 independent parts, one for each index of `groups`. A program takes and returns all parts, laid end to end along the dimension named above; an argument that names none is the same for every part. Nothing has to cross between parts.
Inputs may be any that keep to these rules, and one draw needn't show every extreme that they name: `expert_ids`: each row names 22 different experts. No expert below 8 is named by more than 16 of the 256 tokens of one block, and in every block some expert below 8 is named by exactly 16 of them.
All inputs are finite; a program needn't handle non-finite values.
Results may differ from a plain program's by a relative error of at most 0.014.
Values may be sent and summed in bfloat16 or wider, within the bound.
No kernel may reach another device: no remote copies, remote signals or barrier semaphores. Data moves between devices by JAX's collectives and lax.ppermute only.
A program may use at most 128 MiB of HBM per device.

v0:
```python
import jax
import jax.numpy as jnp
from jax import lax
from jax.sharding import PartitionSpec as P

D = 4096
GRP = 1024
LAT = 1024
CAP = 16


epsilon = 1e-05


def prefix(value, axis, combine, identity):
    length, here = (lax.axis_size(axis), lax.axis_index(axis))
    everything = jax.tree.map(
        lambda part, kind: lax.all_gather(part.astype(kind), axis),
        value,
        (jnp.bfloat16, jnp.bfloat16),
    )
    start = jax.tree.map(
        lambda part, zero: jnp.broadcast_to(jnp.asarray(zero, part.dtype), part.shape),
        value,
        identity,
    )

    def step(k, before):
        reached = k < here
        new = combine(
            before, jax.tree.map(lambda part, own: part[k].astype(own.dtype), everything, value)
        )
        return jax.tree.map(lambda a, b: jnp.where(reached, a, b), new, before)

    return lax.fori_loop(0, length, step, start)


def state_link(previous, current):
    return (previous[0] * current[0], current[0][:, None, None] * previous[1] + current[1])


def expert_apply(incoming, expert_up, expert_down):
    hidden = jnp.einsum("secl,elf->secf", incoming, expert_up, preferred_element_type=jnp.float32)
    hidden = (jnp.maximum(hidden, 0.0) ** 2).astype(jnp.bfloat16)
    return jnp.einsum("secf,efl->secl", hidden, expert_down, preferred_element_type=jnp.float32)


def local(
    ssm_input,
    decay_log,
    state_write,
    state_read,
    skip_scale,
    gate_input,
    ssm_gain,
    out_weight,
    residual_in,
    moe_gain,
    down_latent,
    expert_up,
    expert_down,
    up_latent,
    expert_ids,
    combine_fixed,
):
    row_count = ssm_input.shape[0]
    head_count = decay_log.shape[1]
    inputs = ssm_input.astype(jnp.float32).reshape(row_count, head_count, -1)
    writes = state_write.astype(jnp.float32)
    reads = state_read.astype(jnp.float32)
    cumulative = jnp.cumsum(decay_log, axis=0)
    causal = jnp.arange(row_count)[:, None] >= jnp.arange(row_count)[None, :]
    spread = jnp.where(causal[:, :, None], cumulative[:, None, :] - cumulative[None, :, :], 0.0)
    intersection = jnp.dot(state_read, state_write.T, preferred_element_type=jnp.float32)
    mixing = jnp.where(causal[:, :, None], jnp.exp(-spread), 0.0) * intersection[:, :, None]
    within = jnp.einsum("tsh,shp->thp", mixing, inputs, precision=lax.Precision.HIGHEST)
    tail_decay = jnp.exp(cumulative - cumulative[-1][None, :])
    local_state = jnp.einsum(
        "sn,sh,shp->hnp", writes, tail_decay, inputs, precision=lax.Precision.HIGHEST
    )
    local_decay = jnp.exp(-cumulative[-1])
    identity = (jnp.ones_like(local_decay), jnp.zeros_like(local_state))
    prior_decay, prior_state = prefix((local_decay, local_state), "ctx", state_link, identity)
    carried = (
        jnp.einsum("tn,hnp->thp", reads, prior_state, precision=lax.Precision.HIGHEST)
        * jnp.exp(-cumulative)[:, :, None]
    )
    mixed = within + carried + skip_scale[None, :, None] * inputs
    gated = mixed.reshape(row_count, -1) * jax.nn.silu(gate_input.astype(jnp.float32))
    grouped = gated.reshape(row_count, -1, GRP)
    group_rms = lax.rsqrt(jnp.mean(grouped * grouped, axis=2, keepdims=True) + epsilon)
    normed = ((grouped * group_rms).reshape(gated.shape) * ssm_gain).astype(jnp.bfloat16)
    partial_value = jnp.dot(
        normed,
        lax.all_gather(out_weight, "ctx", axis=1, tiled=True),
        preferred_element_type=jnp.float32,
    )
    mamba_out = lax.psum_scatter(
        partial_value.astype(jnp.bfloat16), "heads", scatter_dimension=1, tiled=True
    ).astype(jnp.float32)
    residual = residual_in.astype(jnp.float32) + mamba_out
    scaled = (residual * moe_gain).astype(jnp.bfloat16)
    latent_part = jnp.dot(scaled, down_latent, preferred_element_type=jnp.float32)
    squares = jnp.sum(residual * residual, axis=1)
    latent_sum, square_sum = (
        lax.psum(latent_part.astype(jnp.bfloat16), "heads").astype(jnp.float32),
        lax.psum(squares.astype(jnp.bfloat16), "heads").astype(jnp.float32),
    )
    inv_rms = lax.rsqrt(square_sum / D + epsilon)
    latent = (latent_sum * inv_rms[:, None]).astype(jnp.bfloat16)
    ctx_count = lax.axis_size("ctx")
    experts_here = expert_up.shape[0]
    wave_size = experts_here * ctx_count
    matches = expert_ids[:, :, None] == jnp.arange(wave_size)[None, None, :]
    chosen = jnp.any(matches, axis=1).astype(jnp.int32)
    weight_fixed = jnp.sum(jnp.where(matches, combine_fixed[:, :, None], 0), axis=1)
    slot_index = jnp.cumsum(chosen, axis=0) - 1
    placed = (chosen[:, :, None] == 1) & (slot_index[:, :, None] == jnp.arange(CAP)[None, None, :])
    route_weight = (weight_fixed.astype(jnp.float32) / 65536.0).astype(jnp.bfloat16)
    combine_table = jnp.where(placed, route_weight[:, :, None], jnp.zeros((), jnp.bfloat16))
    outgoing = jnp.einsum(
        "tk,tl->kl",
        placed.astype(jnp.bfloat16).reshape(row_count, wave_size * CAP),
        latent,
        preferred_element_type=jnp.float32,
    )
    outgoing = outgoing.astype(jnp.bfloat16).reshape(ctx_count, experts_here, CAP, LAT)
    incoming = lax.all_to_all(outgoing, "ctx", split_axis=0, concat_axis=0, tiled=True)
    expert_out = lax.psum(
        expert_apply(incoming, expert_up, expert_down).astype(jnp.bfloat16), "heads"
    )
    returned = lax.all_to_all(expert_out, "ctx", split_axis=0, concat_axis=0, tiled=True).reshape(
        wave_size * CAP, LAT
    )
    combined = jnp.einsum(
        "tk,kl->tl",
        combine_table.reshape(row_count, wave_size * CAP),
        returned,
        preferred_element_type=jnp.float32,
    )
    moe_out = jnp.dot(combined.astype(jnp.bfloat16), up_latent, preferred_element_type=jnp.float32)
    return (residual + moe_out).astype(jnp.bfloat16)


def solution(mesh):
    placed = (
        P(("groups", "ctx"), "heads"),
        P(("groups", "ctx"), "heads"),
        P(("groups", "ctx"), None),
        P(("groups", "ctx"), None),
        P("heads"),
        P(("groups", "ctx"), "heads"),
        P("heads"),
        P("heads", "ctx"),
        P(("groups", "ctx"), "heads"),
        P("heads"),
        P("heads", None),
        P("ctx", None, "heads"),
        P("ctx", "heads", None),
        P(None, "heads"),
        P(("groups", "ctx"), None),
        P(("groups", "ctx"), None),
    )
    return jax.shard_map(
        local, mesh=mesh, in_specs=placed, out_specs=P(("groups", "ctx"), "heads"), check_vma=False
    )
```

profile of v0, /device:TPU:0, one launch (start us, length us, event | category | flops | bytes accessed | tf_op | source)
XLA Modules:
  0.0 502.4 jit_solution(15376862244414403239)
XLA Ops:
  6.5 0.9 copy_bitcast_fusion
  7.5 0.6 reduce-window.14
  8.0 0.2 slice_reduce_fusion
  8.2 0.1 bitcast_bitcast_fusion
  8.3 0.2 slice_reduce_fusion.1
  8.5 0.1 negate_exponential_fusion
  8.6 2.3 copy.76
  10.9 3.2 fusion.28
  14.1 0.0 all-gather.7.cloned.1.call-update
  14.1 0.0 all-gather.5.cloned.1.call-start
  14.2 0.7 all-gather.5.cloned.1.call-update
  14.9 0.0 reduce-scatter.2.cloned.1.call-start
  14.9 0.2 fusion.63
  15.1 12.6 %all-gather.1 = bf16[4,1,32]{2,1,0:T(2,128)(2,1)S(1)} all-gather(bf16[1,1,32]{2,1,0:T(2,128)(2,1)S(1)} %bitcast.123), channel_id=1, replica_groups=mesh['groups'=2,'ctx'=4,'heads'=4] {'ctx'}, dimensions={0}, use_global_device_ids=true | all-gather | bytes 320 | tf_op jit(solution)/shard_map/all_gather | solution.py:18
  27.8 0.9 fusion.68
  28.7 33.9 %all-gather.7.cloned.1.call-done = bf16[128,128,64]{1,2,0:T(8,128)(2,1)} async-done(((bf16[32,128,64]{1,2,0:T(8,128)(2,1)}), bf16[128,128,64]{1,2,0:T(8,128)(2,1)}) %all-gather.7.cloned.1.call-update) | async-done | bytes 2097168 | tf_op jit(solution)/shard_map/all_gather | solution.py:18
  62.7 24.2 %while.14 = (s32[]{:T(128)}, f32[32,128,64]{2,1,0:T(8,128)}, s32[]{:T(128)}, bf16[4,32]{1,0:T(4,128)(2,1)S(1)}, bf16[4,32,128,64]{2,3,1,0:T(8,128)(2,1)}, /*index=5*/s32[]{:T(128)}, s32[]{:T(128)}) while((s32[]{:T(128)}, f32[32,128,64]{2,1,0:T(8,128)}, s32[]{:T(128)}, bf16[4,32]{1,0:T(4,128)(2,1)S(1)}, ...), condition=%wide.region_3.4_spmd.clone, body=%wide.region_2.3_spmd.clone.sunk | while | flops 1310756 | bytes 4719017 | solution.py:35
  62.7 1.1 constant_dynamic-slice_fusion.2
  63.7 1.4 copy.105
  65.1 2.9 fusion.81
  68.0 1.1 constant_dynamic-slice_fusion.2
  69.1 1.4 copy.105
  70.5 4.0 fusion.81
  74.5 1.1 constant_dynamic-slice_fusion.2
  75.7 1.4 copy.105
  77.0 3.8 fusion.81
  80.8 1.1 constant_dynamic-slice_fusion.2
  82.0 1.4 copy.105
  83.3 3.5 fusion.81
  86.9 3.6 fusion.60
  90.5 7.9 %fusion.18 = f32[256,32,64]{0,2,1:T(8,128)} fusion(bf16[256,32,64]{0,2,1:T(8,128)(2,1)S(1)} %bitcast.116, f32[32,64,256]{2,1,0:T(8,128)S(1)} %fusion.60, f32[256,256]{1,0:T(8,128)S(1)} %copy-done.4, f32[256,32]{0,1:T(8,128)S(1)} %bitcast_bitcast_fusion, pred[256,256]{1,0:T(8,128)(4,1)S(1)} %iota_compare_fusion, f32[32]{0:T(128)S(1)} %copy-done.10, ...), kind=kOutput, calls=%fused_computation.26 | convolution fusion | flops 1623719936 | bytes 5636224 | tf_op jit(solution)/shard_map/tsh,shp->thp/dot_general | solution.py:76
  98.4 2.9 copy.79
  101.4 3.7 fusion.67
  105.1 4.0 mul.106
  109.1 2.2 reduce_sum.27
  111.4 0.6 mul.107
  112.0 2.2 copy.91
  114.2 235.6 %all-gather.5.cloned.1.call-done = bf16[2048,4096]{1,0:T(8,128)(2,1)} async-done(((bf16[2048,1024]{1,0:T(8,128)(2,1)}), bf16[2048,4096]{1,0:T(8,128)(2,1)}) %all-gather.5.cloned.1.call-update) | async-done | bytes 16777232 | tf_op jit(solution)/shard_map/all_gather | solution.py:95
  349.8 13.4 %convolution_convert_fusion = bf16[256,4096]{1,0:T(8,128)(2,1)} fusion(bf16[2048,4096]{1,0:T(8,128)(2,1)} %all-gather.5.cloned.1.call-done, f32[256,2048]{1,0:T(8,128)} %bitcast.119, f32[2048]{0:T(1024)S(1)} %copy-done.8, f32[256,2048]{1,0:T(8,128)} %copy.79, bf16[256,2048]{1,0:T(8,128)(2,1)} %param.23), kind=kOutput, calls=%fused_computation.11 | convolution fusion | flops 4300734464 | bytes 24125440 | tf_op jit(solution)/shard_map/dot_general | solution.py:93
  363.2 0.0 reduce-scatter.2.cloned.1.call-update
  363.3 0.2 all-reduce.3.cloned.1.call-start
  363.5 0.5 copy-done.6
  364.0 0.6 reduce-window.16
  364.6 0.2 slice_reduce_fusion.2
  364.9 0.1 eq.66
  365.0 0.1 add_bitcast_fusion.1
  365.0 0.1 fusion.59
  365.1 27.6 %reduce-scatter.2.cloned.1.call-done = bf16[256,1024]{1,0:T(8,128)(2,1)} async-done(((bf16[256,4096]{1,0:T(8,128)(2,1)}), bf16[256,1024]{1,0:T(8,128)(2,1)}) %reduce-scatter.2.cloned.1.call-update) | async-done | bytes 524304 | tf_op jit(solution)/shard_map/reduce_scatter | solution.py:98
  392.8 3.3 convolution_convert_fusion.1
  396.1 0.0 all-reduce.3.cloned.1.call-update
  396.1 0.0 all-reduce.5.cloned.1.call-start
  396.1 1.3 multiply_reduce_fusion
  397.4 5.8 %psum.22 = bf16[256]{0:T(256)(128)(2,1)S(1)} all-reduce(bf16[256]{0:T(256)(128)(2,1)S(1)} %multiply_reduce_fusion), channel_id=1, replica_groups=mesh['groups'=2,'ctx'=4,'heads'=4] {'heads'}, use_global_device_ids=true, to_apply=%region_12.13 | all-reduce | flops 256 | bytes 1024 | tf_op jit(solution)/shard_map/psum | solution.py:107
  403.2 26.4 %all-reduce.3.cloned.1.call-done = bf16[256,1024]{1,0:T(8,128)(2,1)} async-done(((bf16[256,1024]{1,0:T(8,128)(2,1)}), bf16[256,1024]{1,0:T(8,128)(2,1)}) %all-reduce.3.cloned.1.call-update) | async-done | bytes 524304 | tf_op jit(solution)/shard_map/psum | solution.py:106
  429.7 1.4 convolution_convert_fusion.3
  431.0 12.3 %all_to_all.10 = bf16[4,2,16,1024]{3,2,1,0:T(8,128)(2,1)S(1)} all-to-all(bf16[4,2,16,1024]{3,2,1,0:T(8,128)(2,1)S(1)} %bitcast.120), channel_id=1, replica_groups=mesh['groups'=2,'ctx'=4,'heads'=4] {'ctx'}, dimensions={0} | all-to-all | bytes 524288 | tf_op jit(solution)/shard_map/all_to_all | solution.py:128
  443.3 3.9 fusion.41
  447.3 0.8 select_reduce_fusion
  448.1 30.2 %all-reduce.5.cloned.1.call-done = bf16[4,2,16,1024]{3,2,0,1:T(8,128)(2,1)} async-done(((bf16[4,2,16,1024]{3,2,0,1:T(8,128)(2,1)}), bf16[4,2,16,1024]{3,2,0,1:T(8,128)(2,1)}) %all-reduce.5.cloned.1.call-update) | async-done | bytes 262160 | tf_op jit(solution)/shard_map/psum | solution.py:129
  478.3 1.7 copy.83
  480.0 4.6 all-to-all-start.1
  484.6 1.3 fusion.58
  485.9 6.6 %all-to-all-done.1 = bf16[4,2,16,1024]{3,2,1,0:T(8,128)(2,1)S(1)} async-done(((bf16[4,2,16,1024]{3,2,1,0:T(8,128)(2,1)}), bf16[4,2,16,1024]{3,2,1,0:T(8,128)(2,1)S(1)}, u32[]{:S(2)}, u32[]{:S(2)}) %all-to-all-start.1) | async-done | bytes 262176 | tf_op jit(solution)/shard_map/all_to_all | solution.py:132
  492.5 3.3 fusion.27
  (40 shorter events, 0.3 us)
Async XLA Ops:
  6.5 436.8 %copy-start = (bf16[2,672,1024]{2,1,0:T(8,128)(2,1)S(1)}, bf16[2,672,1024]{2,1,0:T(8,128)(2,1)}, u32[]{:S(2)}) copy-start(bf16[2,672,1024]{2,1,0:T(8,128)(2,1)} %param.30) | copy-start | bytes 8257540
  6.5 4.4 copy-start.5
  6.5 56.1 %all-gather.7.cloned.1.call-start = ((), (), s32[]{:S(2)}) async-start(), calls=%async_computation.7 | async-start | bytes 2621440 | tf_op jit(solution)/shard_map/all_gather | solution.py:18
  14.1 13.7 %copy-start.3 = (bf16[256,128]{1,0:T(8,128)(2,1)S(1)}, bf16[256,128]{1,0:T(8,128)(2,1)}, u32[]{:S(2)}) copy-start(bf16[256,128]{1,0:T(8,128)(2,1)} %param.21) | copy-start | bytes 196612
  14.1 335.7 %all-gather.5.cloned.1.call-start = ((), (), s32[]{:S(2)}) async-start(), calls=%async_computation.3 | async-start | bytes 20971520 | tf_op jit(solution)/shard_map/all_gather | solution.py:95
  14.9 377.9 %reduce-scatter.2.cloned.1.call-start = ((), (), s32[]{:S(2)}) async-start(), calls=%async_computation.4 | async-start | bytes 2621440 | tf_op jit(solution)/shard_map/reduce_scatter | solution.py:98
  86.9 3.6 copy-start.1
  86.9 3.6 copy-start.4
  86.9 3.6 copy-start.10
  112.0 237.8 %copy-start.8 = (f32[2048]{0:T(1024)S(1)}, f32[2048]{0:T(1024)}, u32[]{:S(2)}) copy-start(f32[2048]{0:T(1024)} %param.24) | copy-start | bytes 24580
  363.2 0.7 copy-start.6
  363.2 29.5 %copy-start.2 = (bf16[256,1024]{1,0:T(8,128)(2,1)S(1)}, bf16[256,1024]{1,0:T(8,128)(2,1)}, u32[]{:S(2)}) copy-start(bf16[256,1024]{1,0:T(8,128)(2,1)} %param.26) | copy-start | bytes 1572868
  363.2 29.5 %copy-start.9 = (f32[1024]{0:T(1024)S(1)}, f32[1024]{0:T(1024)}, u32[]{:S(2)}) copy-start(f32[1024]{0:T(1024)} %param.27) | copy-start | bytes 12292
  363.3 66.4 %all-reduce.3.cloned.1.call-start = ((), (), s32[]{:S(2)}) async-start(), calls=%async_computation.5 | async-start | bytes 1048576 | tf_op jit(solution)/shard_map/psum | solution.py:106
  364.0 32.1 %copy-start.7 = (pred[256,8]{0,1:T(8,128)(4,1)}, pred[256,8]{0,1:T(8,128)(4,1)S(1)}, u32[]{:S(2)}) copy-start(pred[256,8]{0,1:T(8,128)(4,1)S(1)} %get-tuple-element.165) | copy-start | bytes 6148
  396.1 82.2 %all-reduce.5.cloned.1.call-start = ((), (), s32[]{:S(2)}) async-start(), calls=%async_computation.6 | async-start | bytes 524288 | tf_op jit(solution)/shard_map/psum | solution.py:129
  480.0 12.5 %all-to-all-start.1 = ((bf16[4,2,16,1024]{3,2,1,0:T(8,128)(2,1)}), bf16[4,2,16,1024]{3,2,1,0:T(8,128)(2,1)S(1)}, u32[]{:S(2)}, u32[]{:S(2)}) async-start(bf16[4,2,16,1024]{3,2,1,0:T(8,128)(2,1)} %copy.83), calls=%async_computation.2 | async-start | bytes 524288 | tf_op jit(solution)/shard_map/all_to_all | solution.py:132
Sparse Core Ops, SparseCore 0:
  14.2 48.3 all-gather.6
  64.2 285.5 all-gather.4
  363.4 29.3 reduce-scatter.1
  396.2 33.4 all-reduce.2
  447.4 30.8 all-reduce.4
where the time goes:
time: 503 us; the launch traced here: 502 us
  waiting for transfers between devices  361 us (72%)
  matrix products  40.9 us (8%)
  blocking collectives  30.7 us (6%)
  local copies, waits for them, and re-layouts  25.7 us (5%)
  other arithmetic  25.5 us (5%)
  between operations  13.3 us (3%)
    all_gather x1, waiting for transfers between devices, local(): lax.all_gather(out_weight, 'ctx', axis=1, tiled=True)  236 us
    all_gather x1, waiting for transfers between devices, prefix(): lax.all_gather(part.astype(kind), axis)  33.9 us
    psum x1, waiting for transfers between devices, local(): lax.psum(expert_apply(incoming, expert_up, expert_down).astype(jnp.bfloat...  30.2 us
    reduce_scatter x1, waiting for transfers between devices, local(): lax.psum_scatter(partial_value.astype(jnp.bfloat16), 'heads', scatter_dim...  27.6 us
    psum x1, waiting for transfers between devices, local(): lax.psum(latent_part.astype(jnp.bfloat16), 'heads').astype(jnp.float32)  26.4 us
    select_n x4, other arithmetic, step(): return jax.tree.map(lambda a, b: jnp.where(reached, a, b), new, before)  14.3 us
    dot_general x1, matrix products, local(): jnp.dot(normed, lax.all_gather(out_weight, 'ctx', axis=1, tiled=True), pr...  13.4 us
    all_gather x1, blocking collectives, prefix(): lax.all_gather(part.astype(kind), axis)  12.6 us
  transfers between devices with their start and end apart: 6, of which 6 were waited for; matrix products, arithmetic and copies ran while one was open for 11% of the time, Pallas kernels for 0%

commit v1 on v0

v1 whole, which is shorter than its diff:
```python
import functools

import jax
import jax.numpy as jnp
from jax import lax
from jax.experimental import pallas as pl
from jax.experimental.pallas import tpu as pltpu
from jax.sharding import PartitionSpec as P


GRP = 1024
CAP = 16
EPS = 1e-05
PAD = 16
SQL = 128
LANES = 128
BF = jnp.bfloat16
F32 = jnp.float32

VM = pl.BlockSpec(memory_space=pltpu.VMEM)
LIMIT = 14 * 2**20


def sds(shape, dtype=BF):
    return pltpu.VMEM(shape, dtype)


def call(body, args, outs, scratch=()):
    args = [pltpu.with_memory_space_constraint(a, pltpu.VMEM) for a in args]
    return pl.pallas_call(
        body,
        in_specs=[VM] * len(args),
        out_specs=[VM] * len(outs),
        out_shape=outs,
        scratch_shapes=scratch,
        compiler_params=pltpu.CompilerParams(vmem_limit_bytes=LIMIT),
    )(*args)


def pick(table, index):
    value = jnp.int32(table[0])
    for i, entry in enumerate(table[1:], 1):
        if entry != table[0]:
            value = jnp.where(index == i, jnp.int32(entry), value)
    return value


def dot(a, b):
    return jnp.dot(a, b, preferred_element_type=F32)


def split(v, terms):
    out = []
    for _ in range(terms):
        part = v.astype(BF)
        out.append(part)
        v = v - part.astype(F32)
    return out


def iota(shape, dim):
    return lax.broadcasted_iota(jnp.int32, shape, dim)


def plan_of(rows, shares):
    units = rows // shares // LANES
    sizes = (1, 2, 1, 2, 2)
    if units % sum(sizes) == 0:
        return tuple(size * units // sum(sizes) * LANES for size in sizes)
    return (LANES,) * units


def tasks(n):
    table = []
    for c in range(n):
        row = [("O", 0, c)]
        for s in range(1, n - 1):
            if c - s >= 0:
                row.append(("R", s, c - s))
            if c + s < n:
                row.append(("L", s, c + s))
        if len(row) < n:
            row.insert(n - 2, None)
        table.append(row)
    return table


def state_kernel(n, heads, width, x_ref, decay_ref, write_ref, scale_ref, cume_ref, cumt_ref, skip_ref, *rest):
    outs, pieces = rest[:n], rest[n]
    rows = x_ref.shape[0]
    cols = heads * width
    piece = cols // n
    c = lax.axis_index("ctx")
    upper = (iota((rows, rows), 0) <= iota((rows, rows), 1)).astype(F32).astype(BF)
    cumt = sum(dot(part, upper) for part in split(decay_ref[...], 3))
    cumt_ref[...] = cumt
    cum = cumt.T
    spread = (iota((heads, cols), 1) // width == iota((heads, cols), 0)).astype(F32).astype(BF)
    cume = sum(dot(part, spread) for part in split(cum, 3))
    cume_ref[...] = cume
    skip_ref[...] = sum(dot(part, spread) for part in split(scale_ref[...], 3))
    last = cume[rows - 1 : rows, :]
    weighted = (jnp.exp(cume - last) * x_ref[...].astype(F32)).astype(BF)
    state = lax.dot_general(
        write_ref[...], weighted, (((0,), (0,)), ((), ())), preferred_element_type=F32
    ).astype(BF)
    size = state.shape[0]
    high, low = split(jnp.exp(-last), 2)
    row = iota((PAD, cols), 0)
    tail = jnp.where(row == 0, high.astype(F32), jnp.where(row == 1, low.astype(F32), 0.0)).astype(BF)
    for q in range(n):
        pieces[q, 0:size, :] = state[:, q * piece : (q + 1) * piece]
        pieces[q, size : size + PAD, :] = tail[:, q * piece : (q + 1) * piece]
    for k in range(n):
        outs[k][...] = pieces[c ^ k]


def prefix_kernel(n, *refs):
    ins, outs, got, made = refs[:n], refs[n : 2 * n], refs[2 * n], refs[2 * n + 1]
    c = lax.axis_index("ctx")
    size = outs[0].shape[0]
    for k in range(n):
        got[c ^ k] = ins[k][...]
    total = jnp.zeros(outs[0].shape, F32)
    for j in range(n):
        made[j] = total.astype(BF)
        if j < n - 1:
            keep = got[j, size : size + PAD, :].astype(F32)
            keep = keep[0:1, :] + keep[1:2, :]
            total = total * keep + got[j, 0:size, :].astype(F32)
    for k in range(n):
        outs[k][...] = made[c ^ k]


def within_kernel(first, steps, count, width, x_ref, cume_ref, cumt_ref, write_ref, read_ref, skip_ref, out_ref):
    rows = x_ref.shape[0]
    half = rows // 2
    inter = lax.dot_general(
        read_ref[...], write_ref[...], (((1,), (1,)), ((), ())), preferred_element_type=F32
    )
    causal = iota((half, half), 0) >= iota((half, half), 1)
    block = count * width

    def step(i, carry):
        start = pl.multiple_of((first + i) * block, block)
        x_all = x_ref[:, pl.ds(start, block)]
        cume = cume_ref[:, pl.ds(start, block)]
        skip_all = skip_ref[:, pl.ds(start, block)]
        results = []
        for j in range(count):
            lanes = slice(j * width, (j + 1) * width)
            x = x_all[:, lanes]
            col = cume[:, j * width : j * width + 1]
            line = cumt_ref[pl.ds((first + i) * count + j, 1), :]
            top, bottom = col[0:half], col[half:rows]
            left, right = line[:, 0:half], line[:, half:rows]
            m00 = jnp.exp(jnp.where(causal, left - top, 0.0))
            m00 = jnp.where(causal, m00 * inter[0:half, 0:half], 0.0).astype(BF)
            m10 = (jnp.exp(left - bottom) * inter[half:rows, 0:half]).astype(BF)
            m11 = jnp.exp(jnp.where(causal, right - bottom, 0.0))
            m11 = jnp.where(causal, m11 * inter[half:rows, half:rows], 0.0).astype(BF)
            upper = dot(m00, x[0:half])
            lower = dot(m10, x[0:half]) + dot(m11, x[half:rows])
            results.append(jnp.concatenate([upper, lower], axis=0))
        result = results[0] if count == 1 else jnp.concatenate(results, axis=1)
        at = pl.ds(pl.multiple_of(i * block, block), block)
        out_ref[:, at] = result + skip_all * x_all.astype(F32)
        return carry

    lax.fori_loop(0, steps, step, 0)


def gate_kernel(n, base, per, base_ref, cume_ref, gate_ref, gain_ref, read_ref, *refs):
    ins, out_ref, prior = refs[:n], refs[n], refs[n + 1]
    c = lax.axis_index("ctx")
    at = slice(base * (GRP // per), (base + per) * (GRP // per))
    for k in range(n):
        prior[c ^ k] = ins[k][...]
    reads = read_ref[...]
    carried = [dot(reads, prior[base + q]) for q in range(per)]
    carried = carried[0] if per == 1 else jnp.concatenate(carried, axis=1)
    mixed = base_ref[...] + carried * jnp.exp(-cume_ref[:, at])
    gate = gate_ref[:, at].astype(F32)
    gated = mixed * (gate / (1.0 + jnp.exp(-gate)))
    mean = jnp.mean(gated * gated, axis=1, keepdims=True)
    out_ref[...] = (gated * lax.rsqrt(mean + EPS) * gain_ref[:, at]).astype(BF)


def load_rows(choice, index, options, groups, cands, a):
    grp = a.shape[1] // groups
    sel = pick(choice, index)
    for o in range(options):

        def copy(o=o):
            for g in range(groups):
                a[:, g * grp : (g + 1) * grp] = cands[o * groups + g][...]

        if len(set(choice)) == 1:
            if o == choice[0]:
                copy()
        else:
            pl.when(sel == o)(copy)


def store_parts(total, outs):
    total = total.astype(BF)
    if len(outs) == 2:
        half = total.shape[0] // 2
        first = lax.rem(lax.axis_index("heads") // 2, 2) == 0
        outs[0][...] = jnp.where(first, total[:half], total[half:])
        outs[1][...] = jnp.where(first, total[half:], total[:half])
    else:
        outs[0][...] = total


def project_kernel(choice, options, groups, fold, parts, *refs):
    cands, refs = refs[: options * groups], refs[options * groups :]
    w_ref, refs = refs[0], refs[1:]
    if fold:
        add_ref, refs = refs[0], refs[1:]
    outs, a = refs[:parts], refs[parts]
    place = lax.axis_index("ctx") * 2 + lax.rem(lax.axis_index("heads"), 2)
    load_rows(choice, place, options, groups, cands, a)
    total = dot(a[...], w_ref[...])
    if fold:
        total = total + add_ref[...].astype(F32)
    store_parts(total, outs)


def final_kernel(choice, options, groups, far_core, shares, chunks, fold, parts, *refs):
    cands, refs = refs[: options * groups], refs[options * groups :]
    w_ref, refs = refs[0], refs[1:]
    far, refs = refs[: shares * chunks], refs[shares * chunks :]
    if fold:
        add_ref, refs = refs[0], refs[1:]
    outs, a, acc = refs[:parts], refs[parts], refs[parts + 1]
    place = lax.axis_index("ctx") * 2 + lax.rem(lax.axis_index("heads"), 2)
    load_rows(choice, place, options, groups, cands, a)
    core = lax.rem(lax.axis_index("heads"), 2)
    plan = [far[j].shape[0] for j in range(chunks)]

    @pl.when(core == far_core)
    def _():
        total = None
        for k in range(shares):
            share = lax.axis_index("groups") ^ k
            for j in range(chunks):
                start = pl.multiple_of(share * sum(plan) + sum(plan[:j]), LANES)
                part = dot(a[:, pl.ds(start, plan[j])], far[k * chunks + j][...])
                total = part if total is None else total + part
        acc[...] = total

    @pl.when(core != far_core)
    def _():
        acc[...] = dot(a[...], w_ref[...])

    total = acc[...]
    if fold:
        total = total + add_ref[...].astype(F32)
    store_parts(total, outs)


def project(choice, cands, weight, add, parts):
    options, groups = len(cands), len(cands[0])
    rows, grp = cands[0][0].shape
    args = [a for cand in cands for a in cand] + [weight]
    if add is not None:
        args.append(add)
    return call(
        functools.partial(project_kernel, choice, options, groups, add is not None, parts),
        args,
        [sds((rows // parts, weight.shape[1]))] * parts,
        [pltpu.VMEM((rows, groups * grp), BF)],
    )


def project_final(choice, cands, weight, far, far_core, add, parts):
    options, groups = len(cands), len(cands[0])
    rows, grp = cands[0][0].shape
    args = [a for cand in cands for a in cand] + [weight] + [a for share in far for a in share]
    if add is not None:
        args.append(add)
    return call(
        functools.partial(
            final_kernel, choice, options, groups, far_core, len(far), len(far[0]), add is not None, parts
        ),
        args,
        [sds((rows // parts, weight.shape[1]))] * parts,
        [pltpu.VMEM((rows, groups * grp), BF), pltpu.VMEM((rows, weight.shape[1]), F32)],
    )


def fold_kernel(own_ref, add_ref, *outs):
    store_parts(own_ref[...].astype(F32) + add_ref[...].astype(F32), outs)


def fold(own, add, parts):
    shape = (own.shape[0] // parts, own.shape[1])
    return call(fold_kernel, [own, add], [sds(shape)] * parts)


def cut_kernel(plan, picks, w_ref, *refs):
    outs, sem = refs[:-1], refs[-1]
    share = lax.axis_index("groups") * sum(plan)
    copies = []
    for i, (j, out) in enumerate(zip(picks, outs)):
        start = pl.multiple_of(share + sum(plan[:j]), LANES)
        copies.append(
            pltpu.make_async_copy(w_ref.at[pl.ds(start, plan[j]), :], out, sem.at[i])
        )
    for copy in copies:
        copy.start()
    for copy in copies:
        copy.wait()


def cut(weight, space, plan, picks):
    return pl.pallas_call(
        functools.partial(cut_kernel, plan, picks),
        in_specs=[pl.BlockSpec(memory_space=space)],
        out_specs=[VM] * len(picks),
        out_shape=[sds((plan[j], weight.shape[1])) for j in picks],
        scratch_shapes=[pltpu.SemaphoreType.DMA((len(picks),))],
        compiler_params=pltpu.CompilerParams(vmem_limit_bytes=LIMIT),
        name="cut",
    )(pltpu.with_memory_space_constraint(weight, space))


def route_kernel(owners, owned, ids_ref, fixed_ref, placed_ref, table_ref):
    named, rows = ids_ref.shape
    wave = owners * owned
    ids, fixed = ids_ref[...], fixed_ref[...]
    line = iota((wave, rows), 0)
    chosen = jnp.zeros((wave, rows), jnp.int32)
    weight = jnp.zeros((wave, rows), jnp.int32)
    for k in range(named):
        match = ids[k : k + 1, :] == line
        chosen = jnp.where(match, 1, chosen)
        weight = weight + jnp.where(match, fixed[k : k + 1, :], 0)
    chosen = chosen.astype(F32)
    upper = (iota((rows, rows), 0) <= iota((rows, rows), 1)).astype(F32).astype(BF)
    slot = dot(chosen.astype(BF), upper) - 1.0
    slot = jnp.where(chosen > 0.5, slot, -1.0).astype(BF)
    route = (weight.astype(F32) / 65536.0).astype(BF)
    slots = wave * CAP
    per = owned // 2
    s = iota((slots, wave), 0) // CAP
    expert = (s // per % owners) * owned + s // (per * owners) * per + s % per
    spread = (expert == iota((slots, wave), 1)).astype(F32).astype(BF)
    placed = dot(spread, slot) == (iota((slots, rows), 0) % CAP).astype(F32)
    table_ref[...] = jnp.where(placed, dot(spread, route), 0.0).T.astype(BF)
    placed_ref[...] = jnp.where(placed, 1.0, 0.0).astype(BF)


def by_core(value):
    half = value.shape[0] // 2
    first = lax.rem(lax.axis_index("heads"), 2) == 0
    mine = jnp.where(first, value[:half], value[half:])
    other = jnp.where(first, value[half:], value[:half])
    return mine, other


def squares_block(value):
    high, low = split(value, 2)
    lane = iota((value.shape[0], SQL), 1)
    high, low = high.astype(F32), low.astype(F32)
    return jnp.where(lane == 0, high, jnp.where(lane == 1, low, 0.0)).astype(BF)


def latent_kernel(where_to, resin_ref, gain_ref, down_ref, placed_ref, *refs):
    count = len(where_to)
    ins = refs[:count]
    res_ref, same_ref, other_ref = refs[count:]
    done = set()
    for (r0, c0), ref in zip(where_to, ins):
        at = (slice(r0, r0 + ref.shape[0]), slice(c0, c0 + ref.shape[1]))
        value = ref[...].astype(F32)
        if (r0, c0) in done:
            res_ref[at] += value
        else:
            res_ref[at] = value + resin_ref[at].astype(F32)
            done.add((r0, c0))
    residual = res_ref[...]
    placed = placed_ref[...]
    scaled = dot(placed, (residual * gain_ref[...]).astype(BF)).astype(BF)
    squares = jnp.sum(residual * residual, axis=1, keepdims=True)
    squares = dot(placed, squares_block(squares)).astype(BF)
    lat = down_ref.shape[1]
    mine, other = by_core(dot(scaled, down_ref[...]))
    same_ref[:, :lat] = mine.astype(BF)
    other_ref[:, :lat] = other.astype(BF)
    mine, other = by_core(squares)
    same_ref[:, lat:] = mine
    other_ref[:, lat:] = other


def add_up(ins, total):
    lat = total.shape[1] - SQL
    total[:, :lat] = sum(ref[:, :lat].astype(F32) for ref in ins).astype(BF)
    squares = sum(ref[:, lat:].astype(F32) for ref in ins)
    total[:, lat:] = squares_block(squares[:, 0:1] + squares[:, 1:2])


def merge_kernel(own_ref, recv_ref, out_ref):
    add_up((own_ref, recv_ref), out_ref)


def dispatch_kernel(n, count, *refs):
    ins, outs, total = refs[:count], refs[count : count + n], refs[count + n]
    c = lax.axis_index("ctx")
    rows = outs[0].shape[0]
    add_up(ins, total)
    for k in range(n):
        start = pl.multiple_of((c ^ k) * rows, rows)
        outs[k][...] = total[pl.ds(start, rows), :]


def expert_kernel(n, per, features, *refs):
    ins = refs[:n]
    up_ref, down_ref, up_other_ref, down_other_ref = refs[n : n + 4]
    outs = refs[n + 4 :]
    lat = outs[0].shape[1]
    contract = (((1,), (1,)), ((), ()))
    for j in range(per):
        rows = jnp.concatenate([ref[j * CAP : (j + 1) * CAP, :] for ref in ins], axis=0)
        square = rows[:, lat : lat + 1].astype(F32) + rows[:, lat + 1 : lat + 2].astype(F32)
        rows = (rows[:, :lat].astype(F32) * lax.rsqrt(square / features + EPS)).astype(BF)
        result = None
        for up, down in (
            (up_ref[j], down_ref[j]),
            (up_other_ref[j], down_other_ref[j]),
        ):
            hidden = lax.dot_general(rows, up, contract, preferred_element_type=F32)
            hidden = jnp.maximum(hidden, 0.0)
            part = dot((hidden * hidden).astype(BF), down)
            result = part if result is None else result + part
        result = result.astype(BF)
        for k in range(n):
            outs[k][j * CAP : (j + 1) * CAP, :] = result[k * CAP : (k + 1) * CAP, :]


def share_kernel(per, *refs):
    count = (len(refs) - 1) // 3
    ins, outs, sem = refs[:count], refs[count : 3 * count], refs[3 * count]
    core = lax.rem(lax.axis_index("heads"), 2)
    copies = []
    for i, ref in enumerate(ins):
        for k, start in enumerate((core * per, (1 - core) * per)):
            copies.append(
                pltpu.make_async_copy(
                    ref.at[pl.ds(start, per)], outs[i + k * count], sem.at[i + k * count]
                )
            )
    for copy in copies:
        copy.start()
    for copy in copies:
        copy.wait()


def share_experts(per, *arrays):
    outs = pl.pallas_call(
        functools.partial(share_kernel, per),
        in_specs=[pl.BlockSpec(memory_space=pl.ANY)] * len(arrays),
        out_specs=[VM] * (2 * len(arrays)),
        out_shape=[sds((per, *a.shape[1:])) for a in arrays] * 2,
        scratch_shapes=[pltpu.SemaphoreType.DMA((2 * len(arrays),))],
        compiler_params=pltpu.CompilerParams(vmem_limit_bytes=LIMIT),
        name="share",
    )(*arrays)
    return outs[: len(arrays)], outs[len(arrays) :]


def returned_kernel(n, *refs):
    ins, out_ref = refs[:n], refs[n]
    c = lax.axis_index("ctx")
    rows = ins[0].shape[0]
    for k in range(n):
        out_ref[pl.ds(pl.multiple_of((c ^ k) * rows, rows), rows), :] = ins[k][...]


def sum_kernel(*refs):
    refs[-1][...] = sum(ref[...].astype(F32) for ref in refs[:-1]).astype(BF)


def combine_kernel(mine_ref, other_ref, table_ref, res_ref, up_ref, out_ref):
    mine, other = mine_ref[...], other_ref[...]
    first = lax.rem(lax.axis_index("heads"), 2) == 0
    table = table_ref[...]
    half = table.shape[1] // 2
    combined = dot(table[:, :half], jnp.where(first, mine, other))
    combined = combined + dot(table[:, half:], jnp.where(first, other, mine))
    out_ref[...] = (res_ref[...] + dot(combined.astype(BF), up_ref[...])).astype(BF)


def local(
    ssm_input,
    decay_log,
    state_write,
    state_read,
    skip_scale,
    gate_input,
    ssm_gain,
    out_weight,
    residual_in,
    moe_gain,
    down_latent,
    expert_up,
    expert_down,
    up_latent,
    expert_ids,
    combine_fixed,
):
    n, nh = lax.axis_size("ctx"), lax.axis_size("heads")
    nx, ny = nh // 2, lax.axis_size("groups")
    both = ("ctx", "heads")
    rows, cols = ssm_input.shape
    heads = decay_log.shape[1]
    width = cols // heads
    size = state_write.shape[1]
    groups = cols // GRP
    piece = cols // n
    feats = residual_in.shape[1]
    owned = expert_up.shape[0]
    per = owned // 2
    slots = owned * n * CAP
    lat = down_latent.shape[1]
    swap = [(i, i ^ 1) for i in range(nh)]

    def exchange(arrays, senders=range(n), receivers=range(n)):
        out = [arrays[0]]
        for k in range(1, n):
            perm = [(i, i ^ k) for i in senders if i ^ k in receivers]
            out.append(lax.ppermute(arrays[k], "ctx", perm))
        return out

    def across(a):
        out = [a]
        for k in range(1, nx):
            out.append(lax.ppermute(a, "heads", [(i, i ^ (2 * k)) for i in range(nh)]))
        return out

    plan = plan_of(out_weight.shape[0], ny)
    chunks = cut(out_weight, pltpu.HBM, plan, range(1))
    chunks = chunks + cut(out_weight, pl.ANY, plan, range(1, len(plan)))
    far = [[] for _ in range(ny)]
    for j, chunk in enumerate(chunks):
        far[0].append(lax.ppermute(chunk, "ctx", [(0, 1), (n - 1, n - 2)]))
        for k in range(1, ny):
            perm = []
            for y in range(ny):
                perm += [(y * n + c, (y ^ k) * n + c) for c in (1, n - 2)]
            far[k].append(lax.ppermute(far[0][j], ("groups", "ctx"), perm))

    outs = call(
        functools.partial(state_kernel, n, heads, width),
        [ssm_input, decay_log.T, state_write, skip_scale[None, :]],
        [sds((rows, cols), F32), sds((heads, rows), F32), sds((1, cols), F32)]
        + [sds((size + PAD, piece))] * n,
        [pltpu.VMEM((n, size + PAD, piece), BF)],
    )
    cume, cumt, skip, sends = outs[0], outs[1], outs[2], outs[3:]
    got = exchange(sends, senders=range(n - 1))
    count = min(heads // groups, 8)
    base = []
    for g in range(groups):
        steps = heads // groups // count
        base += call(
            functools.partial(within_kernel, g * steps, steps, count, width),
            [ssm_input, cume, cumt, state_write, state_read, skip],
            [sds((rows, GRP), F32)],
        )
    prior = call(
        functools.partial(prefix_kernel, n),
        got,
        [sds((size, piece))] * n,
        [pltpu.VMEM((n, size + PAD, piece), BF), pltpu.VMEM((n, size, piece), BF)],
    )
    prior = exchange(prior, receivers=range(1, n))
    placed, table = call(
        functools.partial(route_kernel, n, owned),
        [expert_ids.T, combine_fixed.T],
        [sds((slots, rows)), sds((rows, slots))],
    )
    per_group = GRP // piece
    normed = []
    for g in range(groups):
        normed += call(
            functools.partial(gate_kernel, n, g * per_group, per_group),
            [base[g], cume, gate_input, ssm_gain[None, :], state_read, *prior],
            [sds((rows, GRP))],
            [pltpu.VMEM((n, size, piece), BF)],
        )

    kept, given = share_experts(per, jnp.swapaxes(expert_up, 1, 2), expert_down)
    taken = [lax.ppermute(a, "heads", swap) for a in given]

    table_of = tasks(n)
    blocks = {("O", 0): normed}
    feat_block = out_weight.shape[1]
    ratio = n // nh
    got, where_to = [], []

    right = left = normed
    for s in range(1, n - 1):
        for name, line, perm in (
            ("R", right, [(i, i + 1) for i in range(s - 1, n - 1)]),
            ("L", left, [(i, i - 1) for i in range(1, n - s + 1)]),
        ):
            out = []
            for a in line:
                out.append(lax.ppermute(a, "ctx", perm))
            blocks[name, s] = out
        right, left = blocks["R", s], blocks["L", s]

    def options(slot_of_core):
        keys, choice = [], []
        for i in range(2 * n):
            task = table_of[i // 2][slot_of_core(i % 2)]
            if task is None:
                choice.append(0)
                continue
            if task[:2] not in keys:
                keys.append(task[:2])
            choice.append(keys.index(task[:2]))
        return tuple(choice), [blocks[k] for k in keys]

    def rest(held, entries):
        for xi in range(nx):
            for rr in range(ratio):
                perm = [
                    (cc * nh + 2 * xi + core, to * nh + f // ratio)
                    for cc, core, f, to in entries
                    if f % ratio == rr
                ]
                if perm:
                    got.append(lax.ppermute(held, both, perm))
                    where_to.append((0, rr * feat_block))

    def entries_of(slot_of_core, cores):
        return [
            (cc, k, cc, table_of[cc][slot_of_core(k)][2])
            for cc in range(n)
            for k in cores
            if table_of[cc][slot_of_core(k)] is not None
        ]

    for p in range((n - 2) // 2):
        choice, cands = options(lambda k: 2 * p + 1 - k)
        (sent,) = project(choice, cands, out_weight, None, 1)
        recv = lax.ppermute(sent, "heads", swap)
        choice, cands = options(lambda k: 2 * p + k)
        (held,) = project(choice, cands, out_weight, recv, 1)
        rest(held, entries_of(lambda k: 2 * p + k, (0, 1)))
    choice, cands = options(lambda k: n - 2)
    (own,) = project(choice, cands, out_weight, None, 1)
    perm = [(c * nh + i, c * nh + i - 1) for c in range(1, n - 1) for i in range(1, nh, 2)]
    recv = lax.ppermute(own, both, perm)
    (held,) = fold(own, recv, 1)
    rest(held, entries_of(lambda k: n - 2, (0,)))
    choice, cands = options(lambda k: n - 1)
    (sent,) = project_final(choice, cands, out_weight, far, 0, None, 1)
    recv = lax.ppermute(sent, "heads", swap)
    (held,) = project_final(choice, cands, out_weight, far, 1, recv, 1)
    rest(held, entries_of(lambda k: n - 1, (0,)) + [(1, 1, 0, n - 1), (n - 2, 1, n - 1, 0)])

    wide = lat + SQL
    residual, same, apart = call(
        functools.partial(latent_kernel, tuple(where_to)),
        [residual_in, moe_gain[None, :], down_latent, placed, *got],
        [sds((rows, feats), F32), sds((slots // 2, wide)), sds((slots // 2, wide))],
    )
    recv = lax.ppermute(apart, "heads", swap)
    (total,) = call(merge_kernel, [same, recv], [sds((slots // 2, wide))])
    sends = call(
        functools.partial(dispatch_kernel, n, nx),
        across(total),
        [sds((per * CAP, wide))] * n,
        [pltpu.VMEM((slots // 2, wide), BF)],
    )
    sends = call(
        functools.partial(expert_kernel, n, per, float(feats * nh)),
        [*exchange(sends), *kept, *taken],
        [sds((per * CAP, lat))] * n,
    )
    (mine,) = call(functools.partial(returned_kernel, n), exchange(sends), [sds((slots // 2, lat))])
    (mine,) = call(sum_kernel, across(mine), [sds((slots // 2, lat))])
    other = lax.ppermute(mine, "heads", swap)
    (out,) = call(
        combine_kernel,
        [mine, other, table, residual, up_latent],
        [jax.ShapeDtypeStruct((rows, feats), BF)],
    )
    return out


def solution(mesh):
    placed = (
        P(("groups", "ctx"), "heads"),
        P(("groups", "ctx"), "heads"),
        P(("groups", "ctx"), None),
        P(("groups", "ctx"), None),
        P("heads"),
        P(("groups", "ctx"), "heads"),
        P("heads"),
        P("heads", "ctx"),
        P(("groups", "ctx"), "heads"),
        P("heads"),
        P("heads", None),
        P("ctx", None, "heads"),
        P("ctx", "heads", None),
        P(None, "heads"),
        P(("groups", "ctx"), None),
        P(("groups", "ctx"), None),
    )
    return jax.shard_map(
        local, mesh=mesh, in_specs=placed, out_specs=P(("groups", "ctx"), "heads"), check_vma=False
    )
```

time: 503 us -> 214 us (0.43)
  waiting for transfers between devices: 361 us -> 74.9 us
  starting transfers between devices: 4.94 us -> 111 us
  matrix products: 40.9 us -> 0 us
  blocking collectives: 30.7 us -> 0 us
  other arithmetic: 25.5 us -> 0 us
  Pallas kernels: 0 us -> 21.1 us
  local copies, waits for them, and re-layouts: 25.7 us -> 5.74 us
  between operations: 13.3 us -> 0.81 us
    all_gather x2 -> x0, waiting for transfers between devices: 270 us -> none  [the longest x1 236 us: local(): lax.all_gather(out_weight, 'ctx', axis=1, tiled=True)]
    ppermute x0 -> x45, starting transfers between devices: none -> 111 us  [the longest x12 35 us: exchange(): out.append(lax.ppermute(arrays[k], 'ctx', perm))]
    ppermute x0 -> x45, waiting for transfers between devices: none -> 74.9 us  [the longest x8 22.1 us: local(): out.append(lax.ppermute(a, 'ctx', perm))]
    psum x2 -> x0, waiting for transfers between devices: 56.7 us -> none  [the longest x1 30.2 us: local(): lax.psum(expert_apply(incoming, expert_up, expert_down).astype(jnp.bfloat...]
    dot_general x9 -> x0, matrix products: 40.9 us -> none  [the longest x1 13.4 us: local(): jnp.dot(normed, lax.all_gather(out_weight, 'ctx', axis=1, tiled=True), pr...]
    reduce_scatter x1 -> x0, waiting for transfers between devices: 27.6 us -> none  [local(): lax.psum_scatter(partial_value.astype(jnp.bfloat16), 'heads', scatter_dim...]
    pallas_call x0 -> x23, Pallas kernels: none -> 21.1 us  [the longest x20 19.2 us: call(): pl.pallas_call(body, in_specs=[VM] * len(args), out_specs=[VM] * len(outs...]
    select_n x5 -> x0, other arithmetic: 15.6 us -> none  [the longest x4 14.3 us: step(): return jax.tree.map(lambda a, b: jnp.where(reached, a, b), new, before)]
  transfers between devices with their start and end apart: 6 -> 45, of which waited for: 6 -> 16; matrix products, arithmetic and copies ran while one was open for 11% -> 0% of each run, Pallas kernels for 0% -> 7%
where the time goes in v1:
time: 214 us; the launch traced here: 213 us
  starting transfers between devices  111 us (52%)
  waiting for transfers between devices  74.9 us (35%)
  Pallas kernels  21.1 us (10%)
  local copies, waits for them, and re-layouts  5.74 us (3%)
    ppermute x12, starting transfers between devices, exchange(): out.append(lax.ppermute(arrays[k], 'ctx', perm))  35 us
    ppermute x8, waiting for transfers between devices, local(): out.append(lax.ppermute(a, 'ctx', perm))  22.1 us
    ppermute x5, waiting for transfers between devices, local(): far[0].append(lax.ppermute(chunk, 'ctx', [(0, 1), (n - 1, n - 2)]))  21 us
    ppermute x8, starting transfers between devices, local(): out.append(lax.ppermute(a, 'ctx', perm))  20.1 us
    pallas_call x20, Pallas kernels, call(): pl.pallas_call(body, in_specs=[VM] * len(args), out_specs=[VM] * len(outs...  19.2 us
    ppermute x6, starting transfers between devices, rest(): got.append(lax.ppermute(held, both, perm))  17.1 us
    ppermute x12, waiting for transfers between devices, exchange(): out.append(lax.ppermute(arrays[k], 'ctx', perm))  14.6 us
    ppermute x2, starting transfers between devices, local(): taken = [lax.ppermute(a, 'heads', swap) for a in given]  13.4 us
  transfers between devices with their start and end apart: 45, of which 16 were waited for; matrix products, arithmetic and copies ran while one was open for 0% of the time, Pallas kernels for 7%

profile of v1, /device:TPU:0, one launch (start us, length us, event | category | flops | bytes accessed | tf_op | source)
XLA Modules:
  0.0 213.5 jit_solution(14397272869956710562)
XLA Ops:
  0.0 1.2 copy-done.2
  1.2 0.8 copy-done.10
  2.1 0.8 copy-done.14
  3.5 1.9 shard_map.155
  5.3 5.0 %collective-permute-start = (bf16[144,512]{1,0:T(8,128)(2,1)S(1)}, bf16[144,512]{1,0:T(8,128)(2,1)S(1)}, u32[]{:S(2)}, u32[]{:S(2)}) collective-permute-start(bf16[144,512]{1,0:T(8,128)(2,1)S(1)} %get-tuple-element.42), channel_id=1, source_target_pairs={{0,4},{4,0},{8,12},{1,5},{5,1},{9,13},{2,6},{6,2},{10,14},{3,7},{7... | collective-permute-start | bytes 442376 | tf_op jit(solution)/shard_map/ppermute | solution.py:533
  10.3 4.5 %collective-permute-start.1 = (bf16[144,512]{1,0:T(8,128)(2,1)S(1)}, bf16[144,512]{1,0:T(8,128)(2,1)S(1)}, u32[]{:S(2)}, u32[]{:S(2)}) collective-permute-start(bf16[144,512]{1,0:T(8,128)(2,1)S(1)} %get-tuple-element.43), channel_id=1, source_target_pairs={{0,8},{4,12},{8,0},{1,9},{5,13},{9,1},{2,10},{6,14},{10,2},{3,11},... | collective-permute-start | bytes 442376 | tf_op jit(solution)/shard_map/ppermute | solution.py:533
  14.8 1.3 collective-permute-start.2
  16.2 2.2 %copy-done = bf16[2048,1024]{1,0:T(8,128)(2,1)S(1)} copy-done((bf16[2048,1024]{1,0:T(8,128)(2,1)S(1)}, bf16[2048,1024]{1,0:T(8,128)(2,1)}, u32[]{:S(2)}) %copy-start) | copy-done | bytes 4194328
  18.5 3.6 %collective-permute-start.21 = (bf16[256,1024]{1,0:T(8,128)(2,1)S(1)}, bf16[256,1024]{1,0:T(8,128)(2,1)S(1)}, u32[]{:S(2)}, u32[]{:S(2)}) collective-permute-start(bf16[256,1024]{1,0:T(8,128)(2,1)S(1)} %get-tuple-element.49), channel_id=1, source_target_pairs={{0,4},{12,8},{1,5},{13,9},{2,6},{14,10},{3,7},{15,11},{16,20},{28,... | collective-permute-start | bytes 1572872 | tf_op jit(solution)/shard_map/ppermute | solution.py:547
  22.1 1.0 cut.2
  23.1 1.3 collective-permute-start.20
  24.7 4.3 %collective-permute-start.3 = (bf16[128,512]{1,0:T(8,128)(2,1)S(1)}, bf16[128,512]{1,0:T(8,128)(2,1)S(1)}, u32[]{:S(2)}, u32[]{:S(2)}) collective-permute-start(bf16[128,512]{1,0:T(8,128)(2,1)S(1)} %get-tuple-element.46), channel_id=1, source_target_pairs={{0,4},{8,12},{12,8},{1,5},{9,13},{13,9},{2,6},{10,14},{14,10},{3,7... | collective-permute-start | bytes 393224 | tf_op jit(solution)/shard_map/ppermute | solution.py:533
  29.0 3.8 %collective-permute-start.4 = (bf16[128,512]{1,0:T(8,128)(2,1)S(1)}, bf16[128,512]{1,0:T(8,128)(2,1)S(1)}, u32[]{:S(2)}, u32[]{:S(2)}) collective-permute-start(bf16[128,512]{1,0:T(8,128)(2,1)S(1)} %get-tuple-element.47), channel_id=1, source_target_pairs={{0,8},{4,12},{12,4},{1,9},{5,13},{13,5},{2,10},{6,14},{14,6},{3,11... | collective-permute-start | bytes 393224 | tf_op jit(solution)/shard_map/ppermute | solution.py:533
  32.8 3.4 %collective-permute-start.5 = (bf16[128,512]{1,0:T(8,128)(2,1)S(1)}, bf16[128,512]{1,0:T(8,128)(2,1)S(1)}, u32[]{:S(2)}, u32[]{:S(2)}) collective-permute-start(bf16[128,512]{1,0:T(8,128)(2,1)S(1)} %get-tuple-element.48), channel_id=1, source_target_pairs={{0,12},{4,8},{8,4},{1,13},{5,9},{9,5},{2,14},{6,10},{10,6},{3,15},... | collective-permute-start | bytes 393224 | tf_op jit(solution)/shard_map/ppermute | solution.py:533
  36.2 6.6 %collective-permute-done.3.refs_1_ = bf16[128,512]{1,0:T(8,128)(2,1)S(1)} collective-permute-done((bf16[128,512]{1,0:T(8,128)(2,1)S(1)}, bf16[128,512]{1,0:T(8,128)(2,1)S(1)}, u32[]{:S(2)}, u32[]{:S(2)}) %collective-permute-start.3) | collective-permute-done | bytes 131104 | tf_op jit(solution)/shard_map/ppermute | solution.py:533
  42.8 4.4 %collective-permute-start.23 = (bf16[256,1024]{1,0:T(8,128)(2,1)S(1)}, bf16[256,1024]{1,0:T(8,128)(2,1)S(1)}, u32[]{:S(2)}, u32[]{:S(2)}) collective-permute-start(bf16[256,1024]{1,0:T(8,128)(2,1)S(1)} %get-tuple-element.51), channel_id=1, source_target_pairs={{0,4},{12,8},{1,5},{13,9},{2,6},{14,10},{3,7},{15,11},{16,20},{28,... | collective-permute-start | bytes 1572872 | tf_op jit(solution)/shard_map/ppermute | solution.py:547
  47.2 1.3 collective-permute-start.24
  48.6 1.5 shard_map.156.base_ref
  50.1 1.3 collective-permute-start.22
  51.5 0.8 shard_map.158.refs_2_.refs_0_
  52.3 1.3 collective-permute-start.6
  53.6 21.0 %collective-permute-done.22.refs_7_ = bf16[128,1024]{1,0:T(8,128)(2,1)S(1)} collective-permute-done((bf16[128,1024]{1,0:T(8,128)(2,1)S(1)}, bf16[128,1024]{1,0:T(8,128)(2,1)S(1)}, u32[]{:S(2)}, u32[]{:S(2)}) %collective-permute-start.22) | collective-permute-done | bytes 262176 | tf_op jit(solution)/shard_map/ppermute | solution.py:547
  75.9 1.5 shard_map.159.base_ref
  77.4 0.8 shard_map.160.refs_3_.refs_1_
  78.3 1.4 collective-permute-start.7
  79.7 9.5 %collective-permute-start.8 = (bf16[256,1024]{1,0:T(8,128)(2,1)S(1)}, bf16[256,1024]{1,0:T(8,128)(2,1)S(1)}, u32[]{:S(2)}, u32[]{:S(2)}) collective-permute-start(bf16[256,1024]{1,0:T(8,128)(2,1)S(1)} %shard_map.158.refs_2_.refs_0_), channel_id=1, source_target_pairs={{0,4},{4,8},{8,12},{1,5},{5,9},{9,13},{2,6},{6,10},{10,14},{3,7},{... | collective-permute-start | bytes 1572872 | tf_op jit(solution)/shard_map/ppermute | solution.py:611
  89.3 3.9 %collective-permute-start.9 = (bf16[256,1024]{1,0:T(8,128)(2,1)S(1)}, bf16[256,1024]{1,0:T(8,128)(2,1)S(1)}, u32[]{:S(2)}, u32[]{:S(2)}) collective-permute-start(bf16[256,1024]{1,0:T(8,128)(2,1)S(1)} %shard_map.160.refs_3_.refs_1_), channel_id=1, source_target_pairs={{0,4},{4,8},{8,12},{1,5},{5,9},{9,13},{2,6},{6,10},{10,14},{3,7},{... | collective-permute-start | bytes 1572872 | tf_op jit(solution)/shard_map/ppermute | solution.py:611
  93.2 0.7 collective-permute-start.26
  94.6 2.3 %collective-permute-done.7.refs_1_.refs_3_ = bf16[256,1024]{1,0:T(8,128)(2,1)S(1)} collective-permute-done((bf16[256,1024]{1,0:T(8,128)(2,1)S(1)}, bf16[256,1024]{1,0:T(8,128)(2,1)S(1)}, u32[]{:S(2)}, u32[]{:S(2)}) %collective-permute-start.7) | collective-permute-done | bytes 524320 | tf_op jit(solution)/shard_map/ppermute | solution.py:611
  97.6 3.9 %collective-permute-done.8.refs_4_ = bf16[256,1024]{1,0:T(8,128)(2,1)S(1)} collective-permute-done((bf16[256,1024]{1,0:T(8,128)(2,1)S(1)}, bf16[256,1024]{1,0:T(8,128)(2,1)S(1)}, u32[]{:S(2)}, u32[]{:S(2)}) %collective-permute-start.8) | collective-permute-done | bytes 524320 | tf_op jit(solution)/shard_map/ppermute | solution.py:611
  101.5 1.3 collective-permute-start.16
  102.8 6.6 %collective-permute-done.9.refs_5_ = bf16[256,1024]{1,0:T(8,128)(2,1)S(1)} collective-permute-done((bf16[256,1024]{1,0:T(8,128)(2,1)S(1)}, bf16[256,1024]{1,0:T(8,128)(2,1)S(1)}, u32[]{:S(2)}, u32[]{:S(2)}) %collective-permute-start.9) | collective-permute-done | bytes 524320 | tf_op jit(solution)/shard_map/ppermute | solution.py:611
  109.4 1.3 collective-permute-start.17
  110.7 0.7 collective-permute-start.18
  112.1 1.3 shard_map.161
  113.5 1.2 shard_map.163.own_ref
  114.8 1.2 collective-permute-done.16.refs_0_
  116.6 8.2 %collective-permute-done.17.refs_1_ = bf16[256,1024]{1,0:T(8,128)(2,1)S(1)} collective-permute-done((bf16[256,1024]{1,0:T(8,128)(2,1)S(1)}, bf16[256,1024]{1,0:T(8,128)(2,1)S(1)}, u32[]{:S(2)}, u32[]{:S(2)}) %collective-permute-start.17) | collective-permute-done | bytes 524320 | tf_op jit(solution)/shard_map/ppermute | solution.py:611
  124.9 1.7 shard_map.165
  126.6 1.5 shard_map.162
  128.2 0.8 collective-permute-start.11
  129.0 1.3 collective-permute-start.12
  130.4 0.7 collective-permute-start.14
  131.2 0.8 share.1
  131.9 13.3 %collective-permute-start.38 = (bf16[1,672,1024]{2,1,0:T(8,128)(2,1)S(1)}, bf16[1,672,1024]{2,1,0:T(8,128)(2,1)S(1)}, u32[]{:S(2)}, u32[]{:S(2)}) collective-permute-start(bf16[1,672,1024]{2,1,0:T(8,128)(2,1)S(1)} %get-tuple-element.61), channel_id=1, source_target_pairs={{0,1},{1,0},{2,3},{3,2},{4,5},{5,4},{6,7},{7,6},{8,9},{9,8},{10,11... | collective-permute-start | bytes 4128776 | tf_op jit(solution)/shard_map/ppermute | solution.py:595
  145.3 1.4 shard_map.166
  147.5 12.9 %collective-permute-start.31 = (bf16[256,1024]{1,0:T(8,128)(2,1)S(1)}, bf16[256,1024]{1,0:T(8,128)(2,1)S(1)}, u32[]{:S(2)}, u32[]{:S(2)}) collective-permute-start(bf16[256,1024]{1,0:T(8,128)(2,1)S(1)} %shard_map.166), channel_id=1, source_target_pairs={{0,8},{4,13},{8,2},{12,7},{5,12},{9,3},{16,24},{20,29},{24,18},{28... | collective-permute-start | bytes 1572872 | tf_op jit(solution)/shard_map/ppermute | solution.py:636
  160.4 0.7 collective-permute-start.32
  161.6 5.5 %collective-permute-done.31.refs_4_ = bf16[256,1024]{1,0:T(8,128)(2,1)S(1)} collective-permute-done((bf16[256,1024]{1,0:T(8,128)(2,1)S(1)}, bf16[256,1024]{1,0:T(8,128)(2,1)S(1)}, u32[]{:S(2)}, u32[]{:S(2)}) %collective-permute-start.31) | collective-permute-done | bytes 524320 | tf_op jit(solution)/shard_map/ppermute | solution.py:636
  167.1 1.1 shard_map.167
  168.3 1.4 collective-permute-done.33.recv_ref
  169.8 8.7 %collective-permute-start.34 = (bf16[64,1152]{1,0:T(8,128)(2,1)S(1)}, bf16[64,1152]{1,0:T(8,128)(2,1)S(1)}, u32[]{:S(2)}, u32[]{:S(2)}) collective-permute-start(bf16[64,1152]{1,0:T(8,128)(2,1)S(1)} %shard_map.168.refs_0_), channel_id=1, source_target_pairs={{0,2},{1,3},{2,0},{3,1},{4,6},{5,7},{6,4},{7,5},{8,10},{9,11},{10,... | collective-permute-start | bytes 442376 | tf_op jit(solution)/shard_map/ppermute | solution.py:539
  178.5 4.2 %collective-permute-done.34.refs_1_ = bf16[64,1152]{1,0:T(8,128)(2,1)S(1)} collective-permute-done((bf16[64,1152]{1,0:T(8,128)(2,1)S(1)}, bf16[64,1152]{1,0:T(8,128)(2,1)S(1)}, u32[]{:S(2)}, u32[]{:S(2)}) %collective-permute-start.34) | collective-permute-done | bytes 147488 | tf_op jit(solution)/shard_map/ppermute | solution.py:539
  182.8 3.7 %collective-permute-start.35 = (bf16[16,1152]{1,0:T(8,128)(2,1)S(1)}, bf16[16,1152]{1,0:T(8,128)(2,1)S(1)}, u32[]{:S(2)}, u32[]{:S(2)}) collective-permute-start(bf16[16,1152]{1,0:T(8,128)(2,1)S(1)} %get-tuple-element.56), channel_id=1, source_target_pairs={{0,4},{4,0},{8,12},{12,8},{1,5},{5,1},{9,13},{13,9},{2,6},{6,2},{1... | collective-permute-start | bytes 110600 | tf_op jit(solution)/shard_map/ppermute | solution.py:533
  186.5 4.6 %collective-permute-start.36 = (bf16[16,1152]{1,0:T(8,128)(2,1)S(1)}, bf16[16,1152]{1,0:T(8,128)(2,1)S(1)}, u32[]{:S(2)}, u32[]{:S(2)}) collective-permute-start(bf16[16,1152]{1,0:T(8,128)(2,1)S(1)} %get-tuple-element.57), channel_id=1, source_target_pairs={{0,8},{4,12},{8,0},{12,4},{1,9},{5,13},{9,1},{13,5},{2,10},{6,14},... | collective-permute-start | bytes 110600 | tf_op jit(solution)/shard_map/ppermute | solution.py:533
  191.2 2.3 %collective-permute-done.36.refs_2_ = bf16[16,1152]{1,0:T(8,128)(2,1)S(1)} collective-permute-done((bf16[16,1152]{1,0:T(8,128)(2,1)S(1)}, bf16[16,1152]{1,0:T(8,128)(2,1)S(1)}, u32[]{:S(2)}, u32[]{:S(2)}) %collective-permute-start.36) | collective-permute-done | bytes 36896 | tf_op jit(solution)/shard_map/ppermute | solution.py:533
  193.4 3.5 %collective-permute-done.37.refs_3_ = bf16[16,1152]{1,0:T(8,128)(2,1)S(1)} collective-permute-done((bf16[16,1152]{1,0:T(8,128)(2,1)S(1)}, bf16[16,1152]{1,0:T(8,128)(2,1)S(1)}, u32[]{:S(2)}, u32[]{:S(2)}) %collective-permute-start.37) | collective-permute-done | bytes 36896 | tf_op jit(solution)/shard_map/ppermute | solution.py:533
  196.9 1.5 shard_map.170
  198.5 0.9 collective-permute-start.41
  199.5 3.4 %collective-permute-start.42 = (bf16[16,1024]{1,0:T(8,128)(2,1)S(1)}, bf16[16,1024]{1,0:T(8,128)(2,1)S(1)}, u32[]{:S(2)}, u32[]{:S(2)}) collective-permute-start(bf16[16,1024]{1,0:T(8,128)(2,1)S(1)} %get-tuple-element.66), channel_id=1, source_target_pairs={{0,12},{4,8},{8,4},{12,0},{1,13},{5,9},{9,5},{13,1},{2,14},{6,10},... | collective-permute-start | bytes 98312 | tf_op jit(solution)/shard_map/ppermute | solution.py:533
  203.4 1.8 collective-permute-done.42.refs_3_
  205.5 4.7 %collective-permute-done.43.refs_1_ = bf16[64,1024]{1,0:T(8,128)(2,1)S(1)} collective-permute-done((bf16[64,1024]{1,0:T(8,128)(2,1)S(1)}, bf16[64,1024]{1,0:T(8,128)(2,1)S(1)}, u32[]{:S(2)}, u32[]{:S(2)}) %collective-permute-start.43) | collective-permute-done | bytes 131104 | tf_op jit(solution)/shard_map/ppermute | solution.py:539
  210.3 1.3 collective-permute-done.44.other_ref
  211.7 1.8 shard_map.173
  (87 shorter events, 8.2 us)
Async XLA Ops:
  0.0 1.2 copy-start.2
  1.2 0.8 copy-start.10
  2.1 0.8 copy-start.14
  2.8 0.7 copy-start.18
  5.3 19.1 %collective-permute-start = (bf16[144,512]{1,0:T(8,128)(2,1)S(1)}, bf16[144,512]{1,0:T(8,128)(2,1)S(1)}, u32[]{:S(2)}, u32[]{:S(2)}) collective-permute-start(bf16[144,512]{1,0:T(8,128)(2,1)S(1)} %get-tuple-element.42), channel_id=1, source_target_pairs={{0,4},{4,0},{8,12},{1,5},{5,1},{9,13},{2,6},{6,2},{10,14},{3,7},{7... | collective-permute-start | bytes 442376 | tf_op jit(solution)/shard_map/ppermute | solution.py:533
  10.3 14.1 %collective-permute-start.1 = (bf16[144,512]{1,0:T(8,128)(2,1)S(1)}, bf16[144,512]{1,0:T(8,128)(2,1)S(1)}, u32[]{:S(2)}, u32[]{:S(2)}) collective-permute-start(bf16[144,512]{1,0:T(8,128)(2,1)S(1)} %get-tuple-element.43), channel_id=1, source_target_pairs={{0,8},{4,12},{8,0},{1,9},{5,13},{9,1},{2,10},{6,14},{10,2},{3,11},... | collective-permute-start | bytes 442376 | tf_op jit(solution)/shard_map/ppermute | solution.py:533
  14.8 9.6 %collective-permute-start.2 = (bf16[144,512]{1,0:T(8,128)(2,1)S(1)}, bf16[144,512]{1,0:T(8,128)(2,1)S(1)}, u32[]{:S(2)}, u32[]{:S(2)}) collective-permute-start(bf16[144,512]{1,0:T(8,128)(2,1)S(1)} %get-tuple-element.44), channel_id=1, source_target_pairs={{0,12},{4,8},{8,4},{1,13},{5,9},{9,5},{2,14},{6,10},{10,6},{3,15},... | collective-permute-start | bytes 442376 | tf_op jit(solution)/shard_map/ppermute | solution.py:533
  16.1 2.2 %copy-start = (bf16[2048,1024]{1,0:T(8,128)(2,1)S(1)}, bf16[2048,1024]{1,0:T(8,128)(2,1)}, u32[]{:S(2)}) copy-start(bf16[2048,1024]{1,0:T(8,128)(2,1)} %refs_4_.3) | copy-start | bytes 12582916
  18.5 30.0 %copy-start.3 = (bf16[256,2048]{1,0:T(8,128)(2,1)S(1)}, bf16[256,2048]{1,0:T(8,128)(2,1)}, u32[]{:S(2)}) copy-start(bf16[256,2048]{1,0:T(8,128)(2,1)} %x_ref.5) | copy-start | bytes 3145732
  18.5 30.0 %copy-start.9 = (bf16[256,128]{1,0:T(8,128)(2,1)S(1)}, bf16[256,128]{1,0:T(8,128)(2,1)}, u32[]{:S(2)}) copy-start(bf16[256,128]{1,0:T(8,128)(2,1)} %read_ref.7) | copy-start | bytes 196612
  18.5 30.0 %copy-start.11 = (bf16[256,128]{1,0:T(8,128)(2,1)S(1)}, bf16[256,128]{1,0:T(8,128)(2,1)}, u32[]{:S(2)}) copy-start(bf16[256,128]{1,0:T(8,128)(2,1)} %write_ref.5) | copy-start | bytes 196612
  18.5 56.7 %collective-permute-start.21 = (bf16[256,1024]{1,0:T(8,128)(2,1)S(1)}, bf16[256,1024]{1,0:T(8,128)(2,1)S(1)}, u32[]{:S(2)}, u32[]{:S(2)}) collective-permute-start(bf16[256,1024]{1,0:T(8,128)(2,1)S(1)} %get-tuple-element.49), channel_id=1, source_target_pairs={{0,4},{12,8},{1,5},{13,9},{2,6},{14,10},{3,7},{15,11},{16,20},{28,... | collective-permute-start | bytes 1572872 | tf_op jit(solution)/shard_map/ppermute | solution.py:547
  23.1 29.2 %collective-permute-start.20 = (bf16[128,1024]{1,0:T(8,128)(2,1)S(1)}, bf16[128,1024]{1,0:T(8,128)(2,1)S(1)}, u32[]{:S(2)}, u32[]{:S(2)}) collective-permute-start(bf16[128,1024]{1,0:T(8,128)(2,1)S(1)} %cut.2), channel_id=1, source_target_pairs={{0,4},{12,8},{1,5},{13,9},{2,6},{14,10},{3,7},{15,11},{16,20},{28,... | collective-permute-start | bytes 786440 | tf_op jit(solution)/shard_map/ppermute | solution.py:547
  24.7 18.1 %collective-permute-start.3 = (bf16[128,512]{1,0:T(8,128)(2,1)S(1)}, bf16[128,512]{1,0:T(8,128)(2,1)S(1)}, u32[]{:S(2)}, u32[]{:S(2)}) collective-permute-start(bf16[128,512]{1,0:T(8,128)(2,1)S(1)} %get-tuple-element.46), channel_id=1, source_target_pairs={{0,4},{8,12},{12,8},{1,5},{9,13},{13,9},{2,6},{10,14},{14,10},{3,7... | collective-permute-start | bytes 393224 | tf_op jit(solution)/shard_map/ppermute | solution.py:533
  29.0 18.2 %collective-permute-start.4 = (bf16[128,512]{1,0:T(8,128)(2,1)S(1)}, bf16[128,512]{1,0:T(8,128)(2,1)S(1)}, u32[]{:S(2)}, u32[]{:S(2)}) collective-permute-start(bf16[128,512]{1,0:T(8,128)(2,1)S(1)} %get-tuple-element.47), channel_id=1, source_target_pairs={{0,8},{4,12},{12,4},{1,9},{5,13},{13,5},{2,10},{6,14},{14,6},{3,11... | collective-permute-start | bytes 393224 | tf_op jit(solution)/shard_map/ppermute | solution.py:533
  32.8 17.3 %collective-permute-start.5 = (bf16[128,512]{1,0:T(8,128)(2,1)S(1)}, bf16[128,512]{1,0:T(8,128)(2,1)S(1)}, u32[]{:S(2)}, u32[]{:S(2)}) collective-permute-start(bf16[128,512]{1,0:T(8,128)(2,1)S(1)} %get-tuple-element.48), channel_id=1, source_target_pairs={{0,12},{4,8},{8,4},{1,13},{5,9},{9,5},{2,14},{6,10},{10,6},{3,15},... | collective-permute-start | bytes 393224 | tf_op jit(solution)/shard_map/ppermute | solution.py:533
  42.8 35.5 %collective-permute-start.23 = (bf16[256,1024]{1,0:T(8,128)(2,1)S(1)}, bf16[256,1024]{1,0:T(8,128)(2,1)S(1)}, u32[]{:S(2)}, u32[]{:S(2)}) collective-permute-start(bf16[256,1024]{1,0:T(8,128)(2,1)S(1)} %get-tuple-element.51), channel_id=1, source_target_pairs={{0,4},{12,8},{1,5},{13,9},{2,6},{14,10},{3,7},{15,11},{16,20},{28,... | collective-permute-start | bytes 1572872 | tf_op jit(solution)/shard_map/ppermute | solution.py:547
  47.2 32.5 %collective-permute-start.24 = (bf16[256,1024]{1,0:T(8,128)(2,1)S(1)}, bf16[256,1024]{1,0:T(8,128)(2,1)S(1)}, u32[]{:S(2)}, u32[]{:S(2)}) collective-permute-start(bf16[256,1024]{1,0:T(8,128)(2,1)S(1)} %get-tuple-element.52), channel_id=1, source_target_pairs={{0,4},{12,8},{1,5},{13,9},{2,6},{14,10},{3,7},{15,11},{16,20},{28,... | collective-permute-start | bytes 1572872 | tf_op jit(solution)/shard_map/ppermute | solution.py:547
  48.6 2.9 %copy-start.4 = (bf16[256,2048]{1,0:T(8,128)(2,1)S(1)}, bf16[256,2048]{1,0:T(8,128)(2,1)}, u32[]{:S(2)}) copy-start(bf16[256,2048]{1,0:T(8,128)(2,1)} %gate_ref.3) | copy-start | bytes 3145732
  48.6 2.9 %copy-start.13 = (f32[2048]{0:T(1024)S(1)}, f32[2048]{0:T(1024)}, u32[]{:S(2)}) copy-start(f32[2048]{0:T(1024)} %param.22) | copy-start | bytes 24580
  50.1 24.4 %collective-permute-start.22 = (bf16[128,1024]{1,0:T(8,128)(2,1)S(1)}, bf16[128,1024]{1,0:T(8,128)(2,1)S(1)}, u32[]{:S(2)}, u32[]{:S(2)}) collective-permute-start(bf16[128,1024]{1,0:T(8,128)(2,1)S(1)} %get-tuple-element.50), channel_id=1, source_target_pairs={{0,4},{12,8},{1,5},{13,9},{2,6},{14,10},{3,7},{15,11},{16,20},{28,... | collective-permute-start | bytes 786440 | tf_op jit(solution)/shard_map/ppermute | solution.py:547
  52.3 41.7 %collective-permute-start.6 = (bf16[256,1024]{1,0:T(8,128)(2,1)S(1)}, bf16[256,1024]{1,0:T(8,128)(2,1)S(1)}, u32[]{:S(2)}, u32[]{:S(2)}) collective-permute-start(bf16[256,1024]{1,0:T(8,128)(2,1)S(1)} %shard_map.158.refs_2_.refs_0_), channel_id=1, source_target_pairs={{4,0},{8,4},{12,8},{5,1},{9,5},{13,9},{6,2},{10,6},{14,10},{7,3},{... | collective-permute-start | bytes 1572872 | tf_op jit(solution)/shard_map/ppermute | solution.py:611
  74.5 14.7 %collective-permute-start.25 = (bf16[128,1024]{1,0:T(8,128)(2,1)S(1)}, bf16[128,1024]{1,0:T(8,128)(2,1)S(1)}, u32[]{:S(2)}, u32[]{:S(2)}) collective-permute-start(bf16[128,1024]{1,0:T(8,128)(2,1)S(1)} %collective-permute-done.20.refs_5_), channel_id=1, source_target_pairs={{4,20},{8,24},{20,4},{24,8},{5,21},{9,25},{21,5},{25,9},{6,22},{10... | collective-permute-start | bytes 786440 | tf_op jit(solution)/shard_map/ppermute | solution.py:552
  75.2 18.0 %collective-permute-start.27 = (bf16[128,1024]{1,0:T(8,128)(2,1)S(1)}, bf16[128,1024]{1,0:T(8,128)(2,1)S(1)}, u32[]{:S(2)}, u32[]{:S(2)}) collective-permute-start(bf16[128,1024]{1,0:T(8,128)(2,1)S(1)} %collective-permute-done.22.refs_7_), channel_id=1, source_target_pairs={{4,20},{8,24},{20,4},{24,8},{5,21},{9,25},{21,5},{25,9},{6,22},{10... | collective-permute-start | bytes 786440 | tf_op jit(solution)/shard_map/ppermute | solution.py:552
  77.4 34.6 %copy-start.1 = (bf16[2048,1024]{1,0:T(8,128)(2,1)S(1)}, bf16[2048,1024]{1,0:T(8,128)(2,1)}, u32[]{:S(2)}) copy-start(bf16[2048,1024]{1,0:T(8,128)(2,1)} %refs_4_.3) | copy-start | bytes 12582916
  78.3 18.7 %collective-permute-start.7 = (bf16[256,1024]{1,0:T(8,128)(2,1)S(1)}, bf16[256,1024]{1,0:T(8,128)(2,1)S(1)}, u32[]{:S(2)}, u32[]{:S(2)}) collective-permute-start(bf16[256,1024]{1,0:T(8,128)(2,1)S(1)} %shard_map.160.refs_3_.refs_1_), channel_id=1, source_target_pairs={{4,0},{8,4},{12,8},{5,1},{9,5},{13,9},{6,2},{10,6},{14,10},{7,3},{... | collective-permute-start | bytes 1572872 | tf_op jit(solution)/shard_map/ppermute | solution.py:611
  79.7 21.8 %collective-permute-start.8 = (bf16[256,1024]{1,0:T(8,128)(2,1)S(1)}, bf16[256,1024]{1,0:T(8,128)(2,1)S(1)}, u32[]{:S(2)}, u32[]{:S(2)}) collective-permute-start(bf16[256,1024]{1,0:T(8,128)(2,1)S(1)} %shard_map.158.refs_2_.refs_0_), channel_id=1, source_target_pairs={{0,4},{4,8},{8,12},{1,5},{5,9},{9,13},{2,6},{6,10},{10,14},{3,7},{... | collective-permute-start | bytes 1572872 | tf_op jit(solution)/shard_map/ppermute | solution.py:611
  89.3 20.1 %collective-permute-start.9 = (bf16[256,1024]{1,0:T(8,128)(2,1)S(1)}, bf16[256,1024]{1,0:T(8,128)(2,1)S(1)}, u32[]{:S(2)}, u32[]{:S(2)}) collective-permute-start(bf16[256,1024]{1,0:T(8,128)(2,1)S(1)} %shard_map.160.refs_3_.refs_1_), channel_id=1, source_target_pairs={{0,4},{4,8},{8,12},{1,5},{5,9},{9,13},{2,6},{6,10},{10,14},{3,7},{... | collective-permute-start | bytes 1572872 | tf_op jit(solution)/shard_map/ppermute | solution.py:611
  93.2 17.4 %collective-permute-start.26 = (bf16[256,1024]{1,0:T(8,128)(2,1)S(1)}, bf16[256,1024]{1,0:T(8,128)(2,1)S(1)}, u32[]{:S(2)}, u32[]{:S(2)}) collective-permute-start(bf16[256,1024]{1,0:T(8,128)(2,1)S(1)} %collective-permute-done.21.refs_6_), channel_id=1, source_target_pairs={{4,20},{8,24},{20,4},{24,8},{5,21},{9,25},{21,5},{25,9},{6,22},{10... | collective-permute-start | bytes 1572872 | tf_op jit(solution)/shard_map/ppermute | solution.py:552
  93.9 17.4 %collective-permute-start.28 = (bf16[256,1024]{1,0:T(8,128)(2,1)S(1)}, bf16[256,1024]{1,0:T(8,128)(2,1)S(1)}, u32[]{:S(2)}, u32[]{:S(2)}) collective-permute-start(bf16[256,1024]{1,0:T(8,128)(2,1)S(1)} %collective-permute-done.23.refs_8_), channel_id=1, source_target_pairs={{4,20},{8,24},{20,4},{24,8},{5,21},{9,25},{21,5},{25,9},{6,22},{10... | collective-permute-start | bytes 1572872 | tf_op jit(solution)/shard_map/ppermute | solution.py:552
  96.9 16.5 %collective-permute-start.29 = (bf16[256,1024]{1,0:T(8,128)(2,1)S(1)}, bf16[256,1024]{1,0:T(8,128)(2,1)S(1)}, u32[]{:S(2)}, u32[]{:S(2)}) collective-permute-start(bf16[256,1024]{1,0:T(8,128)(2,1)S(1)} %collective-permute-done.24.refs_9_), channel_id=1, source_target_pairs={{4,20},{8,24},{20,4},{24,8},{5,21},{9,25},{21,5},{25,9},{6,22},{10... | collective-permute-start | bytes 1572872 | tf_op jit(solution)/shard_map/ppermute | solution.py:552
  101.5 14.4 %collective-permute-start.16 = (bf16[256,1024]{1,0:T(8,128)(2,1)S(1)}, bf16[256,1024]{1,0:T(8,128)(2,1)S(1)}, u32[]{:S(2)}, u32[]{:S(2)}) collective-permute-start(bf16[256,1024]{1,0:T(8,128)(2,1)S(1)} %collective-permute-done.6.refs_0_.refs_2_), channel_id=1, source_target_pairs={{4,0},{8,4},{5,1},{9,5},{6,2},{10,6},{7,3},{11,7},{20,16},{24,20},... | collective-permute-start | bytes 1572872 | tf_op jit(solution)/shard_map/ppermute | solution.py:611
  109.4 15.5 %collective-permute-start.17 = (bf16[256,1024]{1,0:T(8,128)(2,1)S(1)}, bf16[256,1024]{1,0:T(8,128)(2,1)S(1)}, u32[]{:S(2)}, u32[]{:S(2)}) collective-permute-start(bf16[256,1024]{1,0:T(8,128)(2,1)S(1)} %collective-permute-done.7.refs_1_.refs_3_), channel_id=1, source_target_pairs={{4,0},{8,4},{5,1},{9,5},{6,2},{10,6},{7,3},{11,7},{20,16},{24,20},... | collective-permute-start | bytes 1572872 | tf_op jit(solution)/shard_map/ppermute | solution.py:611
  110.7 14.2 %collective-permute-start.18 = (bf16[256,1024]{1,0:T(8,128)(2,1)S(1)}, bf16[256,1024]{1,0:T(8,128)(2,1)S(1)}, u32[]{:S(2)}, u32[]{:S(2)}) collective-permute-start(bf16[256,1024]{1,0:T(8,128)(2,1)S(1)} %collective-permute-done.8.refs_4_), channel_id=1, source_target_pairs={{4,8},{8,12},{5,9},{9,13},{6,10},{10,14},{7,11},{11,15},{20,24},{2... | collective-permute-start | bytes 1572872 | tf_op jit(solution)/shard_map/ppermute | solution.py:611
  111.4 13.5 %collective-permute-start.19 = (bf16[256,1024]{1,0:T(8,128)(2,1)S(1)}, bf16[256,1024]{1,0:T(8,128)(2,1)S(1)}, u32[]{:S(2)}, u32[]{:S(2)}) collective-permute-start(bf16[256,1024]{1,0:T(8,128)(2,1)S(1)} %collective-permute-done.9.refs_5_), channel_id=1, source_target_pairs={{4,8},{8,12},{5,9},{9,13},{6,10},{10,14},{7,11},{11,15},{20,24},{2... | collective-permute-start | bytes 1572872 | tf_op jit(solution)/shard_map/ppermute | solution.py:611
  113.4 13.2 %collective-permute-start.10 = (bf16[256,1024]{1,0:T(8,128)(2,1)S(1)}, bf16[256,1024]{1,0:T(8,128)(2,1)S(1)}, u32[]{:S(2)}, u32[]{:S(2)}) collective-permute-start(bf16[256,1024]{1,0:T(8,128)(2,1)S(1)} %shard_map.161), channel_id=1, source_target_pairs={{0,1},{1,0},{2,3},{3,2},{4,5},{5,4},{6,7},{7,6},{8,9},{9,8},{10,11... | collective-permute-start | bytes 1572872 | tf_op jit(solution)/shard_map/ppermute | solution.py:650
  115.9 14.4 %collective-permute-start.13 = (bf16[256,1024]{1,0:T(8,128)(2,1)S(1)}, bf16[256,1024]{1,0:T(8,128)(2,1)S(1)}, u32[]{:S(2)}, u32[]{:S(2)}) collective-permute-start(bf16[256,1024]{1,0:T(8,128)(2,1)S(1)} %shard_map.163.own_ref), channel_id=1, source_target_pairs={{5,4},{7,6},{9,8},{11,10},{21,20},{23,22},{25,24},{27,26}} | collective-permute-start | bytes 1572872 | tf_op jit(solution)/shard_map/ppermute | solution.py:657
  126.5 18.7 %collective-permute-start.30 = (bf16[256,1024]{1,0:T(8,128)(2,1)S(1)}, bf16[256,1024]{1,0:T(8,128)(2,1)S(1)}, u32[]{:S(2)}, u32[]{:S(2)}) collective-permute-start(bf16[256,1024]{1,0:T(8,128)(2,1)S(1)} %shard_map.165), channel_id=1, source_target_pairs={{0,1},{1,0},{2,3},{3,2},{4,5},{5,4},{6,7},{7,6},{8,9},{9,8},{10,11... | collective-permute-start | bytes 1572872 | tf_op jit(solution)/shard_map/ppermute | solution.py:662
  126.6 4.5 %copy-start.5 = (bf16[2,1024,672]{1,2,0:T(8,128)(2,1)S(1)}, bf16[2,1024,672]{1,2,0:T(8,128)(2,1)}, u32[]{:S(2)}) copy-start(bf16[2,1024,672]{1,2,0:T(8,128)(2,1)} %param.27) | copy-start | bytes 8257540
  126.6 4.5 %copy-start.6 = (bf16[2,672,1024]{2,1,0:T(8,128)(2,1)S(1)}, bf16[2,672,1024]{2,1,0:T(8,128)(2,1)}, u32[]{:S(2)}) copy-start(bf16[2,672,1024]{2,1,0:T(8,128)(2,1)} %refs_1_.1) | copy-start | bytes 8257540
  128.2 18.6 %collective-permute-start.11 = (bf16[256,1024]{1,0:T(8,128)(2,1)S(1)}, bf16[256,1024]{1,0:T(8,128)(2,1)S(1)}, u32[]{:S(2)}, u32[]{:S(2)}) collective-permute-start(bf16[256,1024]{1,0:T(8,128)(2,1)S(1)} %shard_map.162), channel_id=1, source_target_pairs={{0,0},{1,4},{4,5},{5,1},{8,10},{9,6},{12,15},{13,11},{16,16},{17,2... | collective-permute-start | bytes 1572872 | tf_op jit(solution)/shard_map/ppermute | solution.py:636
  129.0 18.5 %collective-permute-start.12 = (bf16[256,1024]{1,0:T(8,128)(2,1)S(1)}, bf16[256,1024]{1,0:T(8,128)(2,1)S(1)}, u32[]{:S(2)}, u32[]{:S(2)}) collective-permute-start(bf16[256,1024]{1,0:T(8,128)(2,1)S(1)} %shard_map.162), channel_id=1, source_target_pairs={{2,0},{3,4},{6,5},{7,1},{10,10},{11,6},{14,15},{15,11},{18,16},{19... | collective-permute-start | bytes 1572872 | tf_op jit(solution)/shard_map/ppermute | solution.py:636
  130.4 30.0 %collective-permute-start.14 = (bf16[256,1024]{1,0:T(8,128)(2,1)S(1)}, bf16[256,1024]{1,0:T(8,128)(2,1)S(1)}, u32[]{:S(2)}, u32[]{:S(2)}) collective-permute-start(bf16[256,1024]{1,0:T(8,128)(2,1)S(1)} %shard_map.164), channel_id=1, source_target_pairs={{4,9},{8,14},{20,25},{24,30}} | collective-permute-start | bytes 1572872 | tf_op jit(solution)/shard_map/ppermute | solution.py:636
  131.9 59.2 %collective-permute-start.38 = (bf16[1,672,1024]{2,1,0:T(8,128)(2,1)S(1)}, bf16[1,672,1024]{2,1,0:T(8,128)(2,1)S(1)}, u32[]{:S(2)}, u32[]{:S(2)}) collective-permute-start(bf16[1,672,1024]{2,1,0:T(8,128)(2,1)S(1)} %get-tuple-element.61), channel_id=1, source_target_pairs={{0,1},{1,0},{2,3},{3,2},{4,5},{5,4},{6,7},{7,6},{8,9},{9,8},{10,11... | collective-permute-start | bytes 4128776 | tf_op jit(solution)/shard_map/ppermute | solution.py:595
  145.2 15.9 %copy-start.15 = (s32[256,22]{0,1:T(8,128)S(1)}, s32[256,22]{0,1:T(8,128)}, u32[]{:S(2)}) copy-start(s32[256,22]{0,1:T(8,128)} %param.30) | copy-start | bytes 67588
  145.2 15.9 %copy-start.16 = (s32[256,22]{0,1:T(8,128)S(1)}, s32[256,22]{0,1:T(8,128)}, u32[]{:S(2)}) copy-start(s32[256,22]{0,1:T(8,128)} %param.31) | copy-start | bytes 67588
  145.2 21.9 %copy-start.7 = (bf16[1024,1024]{1,0:T(8,128)(2,1)S(1)}, bf16[1024,1024]{1,0:T(8,128)(2,1)}, u32[]{:S(2)}) copy-start(bf16[1024,1024]{1,0:T(8,128)(2,1)} %down_ref.1) | copy-start | bytes 6291460
  145.2 21.9 %copy-start.12 = (bf16[256,1024]{1,0:T(8,128)(2,1)S(1)}, bf16[256,1024]{1,0:T(8,128)(2,1)}, u32[]{:S(2)}) copy-start(bf16[256,1024]{1,0:T(8,128)(2,1)} %resin_ref.1) | copy-start | bytes 1572868
  145.2 21.9 %copy-start.17 = (f32[1024]{0:T(1024)S(1)}, f32[1024]{0:T(1024)}, u32[]{:S(2)}) copy-start(f32[1024]{0:T(1024)} %param.25) | copy-start | bytes 12292
  145.2 45.9 %collective-permute-start.39 = (bf16[1,672,1024]{2,1,0:T(8,128)(2,1)S(1)}, bf16[1,672,1024]{2,1,0:T(8,128)(2,1)S(1)}, u32[]{:S(2)}, u32[]{:S(2)}) collective-permute-start(bf16[1,672,1024]{2,1,0:T(8,128)(2,1)S(1)} %get-tuple-element.62), channel_id=1, source_target_pairs={{0,1},{1,0},{2,3},{3,2},{4,5},{5,4},{6,7},{7,6},{8,9},{9,8},{10,11... | collective-permute-start | bytes 4128776 | tf_op jit(solution)/shard_map/ppermute | solution.py:595
  146.8 14.8 %collective-permute-start.15 = (bf16[256,1024]{1,0:T(8,128)(2,1)S(1)}, bf16[256,1024]{1,0:T(8,128)(2,1)S(1)}, u32[]{:S(2)}, u32[]{:S(2)}) collective-permute-start(bf16[256,1024]{1,0:T(8,128)(2,1)S(1)} %shard_map.164), channel_id=1, source_target_pairs={{6,9},{10,14},{22,25},{26,30}} | collective-permute-start | bytes 1572872 | tf_op jit(solution)/shard_map/ppermute | solution.py:636
  147.5 19.6 %collective-permute-start.31 = (bf16[256,1024]{1,0:T(8,128)(2,1)S(1)}, bf16[256,1024]{1,0:T(8,128)(2,1)S(1)}, u32[]{:S(2)}, u32[]{:S(2)}) collective-permute-start(bf16[256,1024]{1,0:T(8,128)(2,1)S(1)} %shard_map.166), channel_id=1, source_target_pairs={{0,8},{4,13},{8,2},{12,7},{5,12},{9,3},{16,24},{20,29},{24,18},{28... | collective-permute-start | bytes 1572872 | tf_op jit(solution)/shard_map/ppermute | solution.py:636
  160.4 6.7 %collective-permute-start.32 = (bf16[256,1024]{1,0:T(8,128)(2,1)S(1)}, bf16[256,1024]{1,0:T(8,128)(2,1)S(1)}, u32[]{:S(2)}, u32[]{:S(2)}) collective-permute-start(bf16[256,1024]{1,0:T(8,128)(2,1)S(1)} %shard_map.166), channel_id=1, source_target_pairs={{2,8},{6,13},{10,2},{14,7},{7,12},{11,3},{18,24},{22,29},{26,18},{... | collective-permute-start | bytes 1572872 | tf_op jit(solution)/shard_map/ppermute | solution.py:636
  168.2 1.4 collective-permute-start.33
  169.8 12.8 %collective-permute-start.34 = (bf16[64,1152]{1,0:T(8,128)(2,1)S(1)}, bf16[64,1152]{1,0:T(8,128)(2,1)S(1)}, u32[]{:S(2)}, u32[]{:S(2)}) collective-permute-start(bf16[64,1152]{1,0:T(8,128)(2,1)S(1)} %shard_map.168.refs_0_), channel_id=1, source_target_pairs={{0,2},{1,3},{2,0},{3,1},{4,6},{5,7},{6,4},{7,5},{8,10},{9,11},{10,... | collective-permute-start | bytes 442376 | tf_op jit(solution)/shard_map/ppermute | solution.py:539
  182.8 8.3 %collective-permute-start.35 = (bf16[16,1152]{1,0:T(8,128)(2,1)S(1)}, bf16[16,1152]{1,0:T(8,128)(2,1)S(1)}, u32[]{:S(2)}, u32[]{:S(2)}) collective-permute-start(bf16[16,1152]{1,0:T(8,128)(2,1)S(1)} %get-tuple-element.56), channel_id=1, source_target_pairs={{0,4},{4,0},{8,12},{12,8},{1,5},{5,1},{9,13},{13,9},{2,6},{6,2},{1... | collective-permute-start | bytes 110600 | tf_op jit(solution)/shard_map/ppermute | solution.py:533
  186.5 6.9 %collective-permute-start.36 = (bf16[16,1152]{1,0:T(8,128)(2,1)S(1)}, bf16[16,1152]{1,0:T(8,128)(2,1)S(1)}, u32[]{:S(2)}, u32[]{:S(2)}) collective-permute-start(bf16[16,1152]{1,0:T(8,128)(2,1)S(1)} %get-tuple-element.57), channel_id=1, source_target_pairs={{0,8},{4,12},{8,0},{12,4},{1,9},{5,13},{9,1},{13,5},{2,10},{6,14},... | collective-permute-start | bytes 110600 | tf_op jit(solution)/shard_map/ppermute | solution.py:533
  191.1 5.8 %collective-permute-start.37 = (bf16[16,1152]{1,0:T(8,128)(2,1)S(1)}, bf16[16,1152]{1,0:T(8,128)(2,1)S(1)}, u32[]{:S(2)}, u32[]{:S(2)}) collective-permute-start(bf16[16,1152]{1,0:T(8,128)(2,1)S(1)} %get-tuple-element.58), channel_id=1, source_target_pairs={{0,12},{4,8},{8,4},{12,0},{1,13},{5,9},{9,5},{13,1},{2,14},{6,10},... | collective-permute-start | bytes 110600 | tf_op jit(solution)/shard_map/ppermute | solution.py:533
  196.9 14.8 %copy-start.8 = (bf16[1024,1024]{1,0:T(8,128)(2,1)S(1)}, bf16[1024,1024]{1,0:T(8,128)(2,1)}, u32[]{:S(2)}) copy-start(bf16[1024,1024]{1,0:T(8,128)(2,1)} %up_ref.1) | copy-start | bytes 6291460
  198.4 4.5 %collective-permute-start.40 = (bf16[16,1024]{1,0:T(8,128)(2,1)S(1)}, bf16[16,1024]{1,0:T(8,128)(2,1)S(1)}, u32[]{:S(2)}, u32[]{:S(2)}) collective-permute-start(bf16[16,1024]{1,0:T(8,128)(2,1)S(1)} %get-tuple-element.64), channel_id=1, source_target_pairs={{0,4},{4,0},{8,12},{12,8},{1,5},{5,1},{9,13},{13,9},{2,6},{6,2},{1... | collective-permute-start | bytes 98312 | tf_op jit(solution)/shard_map/ppermute | solution.py:533
  198.5 4.9 %collective-permute-start.41 = (bf16[16,1024]{1,0:T(8,128)(2,1)S(1)}, bf16[16,1024]{1,0:T(8,128)(2,1)S(1)}, u32[]{:S(2)}, u32[]{:S(2)}) collective-permute-start(bf16[16,1024]{1,0:T(8,128)(2,1)S(1)} %get-tuple-element.65), channel_id=1, source_target_pairs={{0,8},{4,12},{8,0},{12,4},{1,9},{5,13},{9,1},{13,5},{2,10},{6,14},... | collective-permute-start | bytes 98312 | tf_op jit(solution)/shard_map/ppermute | solution.py:533
  199.5 5.7 %collective-permute-start.42 = (bf16[16,1024]{1,0:T(8,128)(2,1)S(1)}, bf16[16,1024]{1,0:T(8,128)(2,1)S(1)}, u32[]{:S(2)}, u32[]{:S(2)}) collective-permute-start(bf16[16,1024]{1,0:T(8,128)(2,1)S(1)} %get-tuple-element.66), channel_id=1, source_target_pairs={{0,12},{4,8},{8,4},{12,0},{1,13},{5,9},{9,5},{13,1},{2,14},{6,10},... | collective-permute-start | bytes 98312 | tf_op jit(solution)/shard_map/ppermute | solution.py:533
  205.2 5.0 %collective-permute-start.43 = (bf16[64,1024]{1,0:T(8,128)(2,1)S(1)}, bf16[64,1024]{1,0:T(8,128)(2,1)S(1)}, u32[]{:S(2)}, u32[]{:S(2)}) collective-permute-start(bf16[64,1024]{1,0:T(8,128)(2,1)S(1)} %shard_map.171.refs_0_), channel_id=1, source_target_pairs={{0,2},{1,3},{2,0},{3,1},{4,6},{5,7},{6,4},{7,5},{8,10},{9,11},{10,... | collective-permute-start | bytes 393224 | tf_op jit(solution)/shard_map/ppermute | solution.py:539
  210.3 1.4 collective-permute-start.44

commit v2 on v1

--- a/solution.py
+++ b/solution.py
@@ -64,7 +64,7 @@
 
 def plan_of(rows, shares):
     units = rows // shares // LANES
-    sizes = (1, 2, 1, 2, 2)
+    sizes = (1, 2, 2, 2, 1)
     if units % sum(sizes) == 0:
         return tuple(size * units // sum(sizes) * LANES for size in sizes)
     return (LANES,) * units
@@ -227,37 +227,27 @@
     store_parts(total, outs)
 
 
-def final_kernel(choice, options, groups, far_core, shares, chunks, fold, parts, *refs):
+def far_kernel(choice, options, groups, shares, chunks, *refs):
     cands, refs = refs[: options * groups], refs[options * groups :]
-    w_ref, refs = refs[0], refs[1:]
-    far, refs = refs[: shares * chunks], refs[shares * chunks :]
-    if fold:
-        add_ref, refs = refs[0], refs[1:]
-    outs, a, acc = refs[:parts], refs[parts], refs[parts + 1]
+    *far, out_ref, a = refs
     place = lax.axis_index("ctx") * 2 + lax.rem(lax.axis_index("heads"), 2)
     load_rows(choice, place, options, groups, cands, a)
-    core = lax.rem(lax.axis_index("heads"), 2)
-    plan = [far[j].shape[0] for j in range(chunks)]
-
-    @pl.when(core == far_core)
-    def _():
-        total = None
-        for k in range(shares):
-            share = lax.axis_index("groups") ^ k
-            for j in range(chunks):
-                start = pl.multiple_of(share * sum(plan) + sum(plan[:j]), LANES)
-                part = dot(a[:, pl.ds(start, plan[j])], far[k * chunks + j][...])
-                total = part if total is None else total + part
-        acc[...] = total
-
-    @pl.when(core != far_core)
-    def _():
-        acc[...] = dot(a[...], w_ref[...])
-
-    total = acc[...]
-    if fold:
-        total = total + add_ref[...].astype(F32)
-    store_parts(total, outs)
+    plan = [ref.shape[0] for ref in far[: chunks - 1]]
+    plan.append(far[chunks - 1].shape[0] // shares)
+    total = None
+    for k in range(shares):
+        share = lax.axis_index("groups") ^ k
+        for j in range(chunks):
+            start = pl.multiple_of(share * sum(plan) + sum(plan[:j]), LANES)
+            if j == chunks - 1:
+                weight = far[j][k * plan[j] : (k + 1) * plan[j], :]
+            elif k == 0:
+                weight = far[j][...]
+            else:
+                weight = far[chunks + (k - 1) * (chunks - 1) + j][...]
+            part = dot(a[:, pl.ds(start, plan[j])], weight)
+            total = part if total is None else total + part
+    out_ref[...] = total.astype(BF)
 
 
 def project(choice, cands, weight, add, parts):
@@ -274,19 +264,14 @@
     )
 
 
-def project_final(choice, cands, weight, far, far_core, add, parts):
+def project_far(choice, cands, far):
     options, groups = len(cands), len(cands[0])
     rows, grp = cands[0][0].shape
-    args = [a for cand in cands for a in cand] + [weight] + [a for share in far for a in share]
-    if add is not None:
-        args.append(add)
     return call(
-        functools.partial(
-            final_kernel, choice, options, groups, far_core, len(far), len(far[0]), add is not None, parts
-        ),
-        args,
-        [sds((rows // parts, weight.shape[1]))] * parts,
-        [pltpu.VMEM((rows, groups * grp), BF), pltpu.VMEM((rows, weight.shape[1]), F32)],
+        functools.partial(far_kernel, choice, options, groups, len(far), len(far[0])),
+        [a for cand in cands for a in cand] + [a for share in far for a in share],
+        [sds((rows, far[0][0].shape[1]))],
+        [pltpu.VMEM((rows, groups * grp), BF)],
     )
 
 
@@ -301,13 +286,14 @@
 
 def cut_kernel(plan, picks, w_ref, *refs):
     outs, sem = refs[:-1], refs[-1]
-    share = lax.axis_index("groups") * sum(plan)
     copies = []
-    for i, (j, out) in enumerate(zip(picks, outs)):
-        start = pl.multiple_of(share + sum(plan[:j]), LANES)
-        copies.append(
-            pltpu.make_async_copy(w_ref.at[pl.ds(start, plan[j]), :], out, sem.at[i])
-        )
+    for j, out in zip(picks, outs):
+        for k in range(out.shape[0] // plan[j]):
+            share = (lax.axis_index("groups") ^ k) * sum(plan)
+            start = pl.multiple_of(share + sum(plan[:j]), LANES)
+            source = w_ref.at[pl.ds(start, plan[j]), :]
+            target = out.at[pl.ds(k * plan[j], plan[j]), :]
+            copies.append(pltpu.make_async_copy(source, target, sem.at[len(copies)]))
     for copy in copies:
         copy.start()
     for copy in copies:
@@ -315,12 +301,14 @@
 
 
 def cut(weight, space, plan, picks):
+    shares = weight.shape[0] // sum(plan)
+    sizes = [plan[j] * (shares if j == len(plan) - 1 else 1) for j in picks]
     return pl.pallas_call(
         functools.partial(cut_kernel, plan, picks),
         in_specs=[pl.BlockSpec(memory_space=space)],
         out_specs=[VM] * len(picks),
-        out_shape=[sds((plan[j], weight.shape[1])) for j in picks],
-        scratch_shapes=[pltpu.SemaphoreType.DMA((len(picks),))],
+        out_shape=[sds((size, weight.shape[1])) for size in sizes],
+        scratch_shapes=[pltpu.SemaphoreType.DMA((shares * len(picks),))],
         compiler_params=pltpu.CompilerParams(vmem_limit_bytes=LIMIT),
         name="cut",
     )(pltpu.with_memory_space_constraint(weight, space))
@@ -417,8 +405,8 @@
 
 def expert_kernel(n, per, features, *refs):
     ins = refs[:n]
-    up_ref, down_ref, up_other_ref, down_other_ref = refs[n : n + 4]
-    outs = refs[n + 4 :]
+    kept_ref, taken_ref = refs[n : n + 2]
+    outs = refs[n + 2 :]
     lat = outs[0].shape[1]
     contract = (((1,), (1,)), ((), ()))
     for j in range(per):
@@ -426,10 +414,8 @@
         square = rows[:, lat : lat + 1].astype(F32) + rows[:, lat + 1 : lat + 2].astype(F32)
         rows = (rows[:, :lat].astype(F32) * lax.rsqrt(square / features + EPS)).astype(BF)
         result = None
-        for up, down in (
-            (up_ref[j], down_ref[j]),
-            (up_other_ref[j], down_other_ref[j]),
-        ):
+        for ref in (kept_ref, taken_ref):
+            up, down = ref[j], ref[per + j]
             hidden = lax.dot_general(rows, up, contract, preferred_element_type=F32)
             hidden = jnp.maximum(hidden, 0.0)
             part = dot((hidden * hidden).astype(BF), down)
@@ -439,16 +425,14 @@
             outs[k][j * CAP : (j + 1) * CAP, :] = result[k * CAP : (k + 1) * CAP, :]
 
 
-def share_kernel(per, *refs):
-    count = (len(refs) - 1) // 3
-    ins, outs, sem = refs[:count], refs[count : 3 * count], refs[3 * count]
+def share_kernel(per, up_ref, down_ref, kept_ref, given_ref, sem):
     core = lax.rem(lax.axis_index("heads"), 2)
     copies = []
-    for i, ref in enumerate(ins):
-        for k, start in enumerate((core * per, (1 - core) * per)):
+    for i, ref in enumerate((up_ref, down_ref)):
+        for k, (start, out) in enumerate(((core * per, kept_ref), ((1 - core) * per, given_ref))):
             copies.append(
                 pltpu.make_async_copy(
-                    ref.at[pl.ds(start, per)], outs[i + k * count], sem.at[i + k * count]
+                    ref.at[pl.ds(start, per)], out.at[pl.ds(i * per, per)], sem.at[2 * i + k]
                 )
             )
     for copy in copies:
@@ -457,17 +441,16 @@
         copy.wait()
 
 
-def share_experts(per, *arrays):
-    outs = pl.pallas_call(
+def share_experts(per, up, down):
+    return pl.pallas_call(
         functools.partial(share_kernel, per),
-        in_specs=[pl.BlockSpec(memory_space=pl.ANY)] * len(arrays),
-        out_specs=[VM] * (2 * len(arrays)),
-        out_shape=[sds((per, *a.shape[1:])) for a in arrays] * 2,
-        scratch_shapes=[pltpu.SemaphoreType.DMA((2 * len(arrays),))],
+        in_specs=[pl.BlockSpec(memory_space=pl.ANY)] * 2,
+        out_specs=[VM] * 2,
+        out_shape=[sds((2 * per, *up.shape[1:]))] * 2,
+        scratch_shapes=[pltpu.SemaphoreType.DMA((4,))],
         compiler_params=pltpu.CompilerParams(vmem_limit_bytes=LIMIT),
         name="share",
-    )(*arrays)
-    return outs[: len(arrays)], outs[len(arrays) :]
+    )(up, down)
 
 
 def returned_kernel(n, *refs):
@@ -545,7 +528,7 @@
     far = [[] for _ in range(ny)]
     for j, chunk in enumerate(chunks):
         far[0].append(lax.ppermute(chunk, "ctx", [(0, 1), (n - 1, n - 2)]))
-        for k in range(1, ny):
+        for k in range(1, ny if j < len(plan) - 1 else 1):
             perm = []
             for y in range(ny):
                 perm += [(y * n + c, (y ^ k) * n + c) for c in (1, n - 2)]
@@ -592,7 +575,7 @@
         )
 
     kept, given = share_experts(per, jnp.swapaxes(expert_up, 1, 2), expert_down)
-    taken = [lax.ppermute(a, "heads", swap) for a in given]
+    taken = lax.ppermute(given, "heads", swap)
 
     table_of = tasks(n)
     blocks = {("O", 0): normed}
@@ -651,17 +634,17 @@
         choice, cands = options(lambda k: 2 * p + k)
         (held,) = project(choice, cands, out_weight, recv, 1)
         rest(held, entries_of(lambda k: 2 * p + k, (0, 1)))
-    choice, cands = options(lambda k: n - 2)
-    (own,) = project(choice, cands, out_weight, None, 1)
-    perm = [(c * nh + i, c * nh + i - 1) for c in range(1, n - 1) for i in range(1, nh, 2)]
-    recv = lax.ppermute(own, both, perm)
+    for i, keeper in ((n - 2, 0), (n - 1, 1)):
+        choice, cands = options(lambda k: i)
+        (own,) = project(choice, cands, out_weight, None, 1)
+        recv = lax.ppermute(own, "heads", swap)
+        (held,) = fold(own, recv, 1)
+        rest(held, entries_of(lambda k: i, (keeper,)))
+    choice, cands = options(lambda k: n - 1)
+    (own,) = project_far(choice, cands, far)
+    recv = lax.ppermute(own, "heads", swap)
     (held,) = fold(own, recv, 1)
-    rest(held, entries_of(lambda k: n - 2, (0,)))
-    choice, cands = options(lambda k: n - 1)
-    (sent,) = project_final(choice, cands, out_weight, far, 0, None, 1)
-    recv = lax.ppermute(sent, "heads", swap)
-    (held,) = project_final(choice, cands, out_weight, far, 1, recv, 1)
-    rest(held, entries_of(lambda k: n - 1, (0,)) + [(1, 1, 0, n - 1), (n - 2, 1, n - 1, 0)])
+    rest(held, [(1, 0, 0, n - 1), (n - 2, 0, n - 1, 0)])
 
     wide = lat + SQL
     residual, same, apart = call(
@@ -679,7 +662,7 @@
     )
     sends = call(
         functools.partial(expert_kernel, n, per, float(feats * nh)),
-        [*exchange(sends), *kept, *taken],
+        [*exchange(sends), kept, taken],
         [sds((per * CAP, lat))] * n,
     )
     (mine,) = call(functools.partial(returned_kernel, n), exchange(sends), [sds((slots // 2, lat))])

time: 214 us -> 225 us (1.051)
  waiting for transfers between devices: 74.9 us -> 81.8 us
  starting transfers between devices: 111 us -> 114 us
    ppermute x5, waiting for transfers between devices: 21 us -> 1.85 us  [local(): far[0].append(lax.ppermute(chunk, 'ctx', [(0, 1), (n - 1, n - 2)]))]
    ppermute x12, waiting for transfers between devices: 14.6 us -> 28.7 us  [exchange(): out.append(lax.ppermute(arrays[k], 'ctx', perm))]
    ppermute x6 -> x8, starting transfers between devices: 17.1 us -> 6.45 us  [rest(): got.append(lax.ppermute(held, both, perm))]
    ppermute x3 -> x4, starting transfers between devices: 14 us -> 23.5 us  [the longest x1 14.2 us: local(): taken = lax.ppermute(given, 'heads', swap)]
    ppermute x1, starting transfers between devices: 0.07 us -> 8.69 us  [local(): recv = lax.ppermute(apart, 'heads', swap)]
    ppermute x6 -> x8, waiting for transfers between devices: 5.56 us -> 12.5 us  [rest(): got.append(lax.ppermute(held, both, perm))]
    ppermute x8, waiting for transfers between devices: 22.1 us -> 29 us  [local(): out.append(lax.ppermute(a, 'ctx', perm))]
    ppermute x8, starting transfers between devices: 20.1 us -> 16.7 us  [local(): out.append(lax.ppermute(a, 'ctx', perm))]
  transfers between devices with their start and end apart: 45 -> 46, of which waited for: 16 -> 16; matrix products, arithmetic and copies ran while one was open for 0% -> 0% of each run, Pallas kernels for 7% -> 7%
where the time goes in v2:
time: 225 us; the launch traced here: 224 us
  starting transfers between devices  114 us (51%)
  waiting for transfers between devices  81.8 us (36%)
  Pallas kernels  21.2 us (9%)
  local copies, waits for them, and re-layouts  5.74 us (3%)
    ppermute x12, starting transfers between devices, exchange(): out.append(lax.ppermute(arrays[k], 'ctx', perm))  33.4 us
    ppermute x8, waiting for transfers between devices, local(): out.append(lax.ppermute(a, 'ctx', perm))  29 us
    ppermute x12, waiting for transfers between devices, exchange(): out.append(lax.ppermute(arrays[k], 'ctx', perm))  28.7 us
    pallas_call x22, Pallas kernels, call(): pl.pallas_call(body, in_specs=[VM] * len(args), out_specs=[VM] * len(outs...  19.3 us
    ppermute x8, starting transfers between devices, local(): out.append(lax.ppermute(a, 'ctx', perm))  16.7 us
    ppermute x1, starting transfers between devices, local(): taken = lax.ppermute(given, 'heads', swap)  14.2 us
    ppermute x5, starting transfers between devices, local(): far[0].append(lax.ppermute(chunk, 'ctx', [(0, 1), (n - 1, n - 2)]))  12.7 us
    ppermute x8, waiting for transfers between devices, rest(): got.append(lax.ppermute(held, both, perm))  12.5 us
  transfers between devices with their start and end apart: 46, of which 16 were waited for; matrix products, arithmetic and copies ran while one was open for 0% of the time, Pallas kernels for 7%

profile of v2, /device:TPU:0, one launch (start us, length us, event | category | flops | bytes accessed | tf_op | source)
XLA Modules:
  0.0 224.0 jit_solution(8273798686195253685)
XLA Ops:
  0.0 1.2 copy-done.2
  1.2 0.8 copy-done.10
  2.1 0.8 copy-done.14
  3.5 1.9 shard_map.155
  5.3 5.0 %collective-permute-start = (bf16[144,512]{1,0:T(8,128)(2,1)S(1)}, bf16[144,512]{1,0:T(8,128)(2,1)S(1)}, u32[]{:S(2)}, u32[]{:S(2)}) collective-permute-start(bf16[144,512]{1,0:T(8,128)(2,1)S(1)} %get-tuple-element.40), channel_id=1, source_target_pairs={{0,4},{4,0},{8,12},{1,5},{5,1},{9,13},{2,6},{6,2},{10,14},{3,7},{7... | collective-permute-start | bytes 442376 | tf_op jit(solution)/shard_map/ppermute | solution.py:516
  10.3 4.5 %collective-permute-start.1 = (bf16[144,512]{1,0:T(8,128)(2,1)S(1)}, bf16[144,512]{1,0:T(8,128)(2,1)S(1)}, u32[]{:S(2)}, u32[]{:S(2)}) collective-permute-start(bf16[144,512]{1,0:T(8,128)(2,1)S(1)} %get-tuple-element.41), channel_id=1, source_target_pairs={{0,8},{4,12},{8,0},{1,9},{5,13},{9,1},{2,10},{6,14},{10,2},{3,11},... | collective-permute-start | bytes 442376 | tf_op jit(solution)/shard_map/ppermute | solution.py:516
  14.8 1.3 collective-permute-start.2
  16.2 2.2 copy-done
  18.6 3.6 %collective-permute-start.24 = (bf16[256,1024]{1,0:T(8,128)(2,1)S(1)}, bf16[256,1024]{1,0:T(8,128)(2,1)S(1)}, u32[]{:S(2)}, u32[]{:S(2)}) collective-permute-start(bf16[256,1024]{1,0:T(8,128)(2,1)S(1)} %get-tuple-element.47), channel_id=1, source_target_pairs={{0,4},{12,8},{1,5},{13,9},{2,6},{14,10},{3,7},{15,11},{16,20},{28,... | collective-permute-start | bytes 1572872 | tf_op jit(solution)/shard_map/ppermute | solution.py:530
  22.4 6.5 %collective-permute-start.3 = (bf16[128,512]{1,0:T(8,128)(2,1)S(1)}, bf16[128,512]{1,0:T(8,128)(2,1)S(1)}, u32[]{:S(2)}, u32[]{:S(2)}) collective-permute-start(bf16[128,512]{1,0:T(8,128)(2,1)S(1)} %get-tuple-element.44), channel_id=1, source_target_pairs={{0,4},{8,12},{12,8},{1,5},{9,13},{13,9},{2,6},{10,14},{14,10},{3,7... | collective-permute-start | bytes 393224 | tf_op jit(solution)/shard_map/ppermute | solution.py:516
  29.0 1.3 collective-permute-start.25
  30.3 3.8 %collective-permute-start.4 = (bf16[128,512]{1,0:T(8,128)(2,1)S(1)}, bf16[128,512]{1,0:T(8,128)(2,1)S(1)}, u32[]{:S(2)}, u32[]{:S(2)}) collective-permute-start(bf16[128,512]{1,0:T(8,128)(2,1)S(1)} %get-tuple-element.45), channel_id=1, source_target_pairs={{0,8},{4,12},{12,4},{1,9},{5,13},{13,5},{2,10},{6,14},{14,6},{3,11... | collective-permute-start | bytes 393224 | tf_op jit(solution)/shard_map/ppermute | solution.py:516
  34.1 4.6 %collective-permute-start.26 = (bf16[256,1024]{1,0:T(8,128)(2,1)S(1)}, bf16[256,1024]{1,0:T(8,128)(2,1)S(1)}, u32[]{:S(2)}, u32[]{:S(2)}) collective-permute-start(bf16[256,1024]{1,0:T(8,128)(2,1)S(1)} %get-tuple-element.49), channel_id=1, source_target_pairs={{0,4},{12,8},{1,5},{13,9},{2,6},{14,10},{3,7},{15,11},{16,20},{28,... | collective-permute-start | bytes 1572872 | tf_op jit(solution)/shard_map/ppermute | solution.py:530
  38.7 1.0 cut.2
  39.7 1.9 collective-permute-start.23
  41.6 9.6 %collective-permute-done.4.refs_2_ = bf16[128,512]{1,0:T(8,128)(2,1)S(1)} collective-permute-done((bf16[128,512]{1,0:T(8,128)(2,1)S(1)}, bf16[128,512]{1,0:T(8,128)(2,1)S(1)}, u32[]{:S(2)}, u32[]{:S(2)}) %collective-permute-start.4) | collective-permute-done | bytes 131104 | tf_op jit(solution)/shard_map/ppermute | solution.py:516
  51.3 3.3 %collective-permute-start.5 = (bf16[128,512]{1,0:T(8,128)(2,1)S(1)}, bf16[128,512]{1,0:T(8,128)(2,1)S(1)}, u32[]{:S(2)}, u32[]{:S(2)}) collective-permute-start(bf16[128,512]{1,0:T(8,128)(2,1)S(1)} %get-tuple-element.46), channel_id=1, source_target_pairs={{0,12},{4,8},{8,4},{1,13},{5,9},{9,5},{2,14},{6,10},{10,6},{3,15},... | collective-permute-start | bytes 393224 | tf_op jit(solution)/shard_map/ppermute | solution.py:516
  54.7 1.5 shard_map.159.base_ref
  56.2 1.5 shard_map.156.base_ref
  57.7 11.4 %collective-permute-done.5.refs_3_ = bf16[128,512]{1,0:T(8,128)(2,1)S(1)} collective-permute-done((bf16[128,512]{1,0:T(8,128)(2,1)S(1)}, bf16[128,512]{1,0:T(8,128)(2,1)S(1)}, u32[]{:S(2)}, u32[]{:S(2)}) %collective-permute-start.5) | collective-permute-done | bytes 131104 | tf_op jit(solution)/shard_map/ppermute | solution.py:516
  69.2 1.3 collective-permute-start.27
  70.5 0.8 shard_map.160.refs_3_.refs_1_
  71.3 0.8 shard_map.158.refs_2_.refs_0_
  72.1 1.4 collective-permute-start.7
  73.5 1.3 collective-permute-start.6
  74.9 5.2 %collective-permute-start.9 = (bf16[256,1024]{1,0:T(8,128)(2,1)S(1)}, bf16[256,1024]{1,0:T(8,128)(2,1)S(1)}, u32[]{:S(2)}, u32[]{:S(2)}) collective-permute-start(bf16[256,1024]{1,0:T(8,128)(2,1)S(1)} %shard_map.160.refs_3_.refs_1_), channel_id=1, source_target_pairs={{0,4},{4,8},{8,12},{1,5},{5,9},{9,13},{2,6},{6,10},{10,14},{3,7},{... | collective-permute-start | bytes 1572872 | tf_op jit(solution)/shard_map/ppermute | solution.py:594
  80.8 1.8 collective-permute-done.27.refs_8_
  82.6 4.8 %collective-permute-start.8 = (bf16[256,1024]{1,0:T(8,128)(2,1)S(1)}, bf16[256,1024]{1,0:T(8,128)(2,1)S(1)}, u32[]{:S(2)}, u32[]{:S(2)}) collective-permute-start(bf16[256,1024]{1,0:T(8,128)(2,1)S(1)} %shard_map.158.refs_2_.refs_0_), channel_id=1, source_target_pairs={{0,4},{4,8},{8,12},{1,5},{5,9},{9,13},{2,6},{6,10},{10,14},{3,7},{... | collective-permute-start | bytes 1572872 | tf_op jit(solution)/shard_map/ppermute | solution.py:594
  88.2 0.7 collective-permute-done.7.refs_1_.refs_3_
  89.6 7.5 %collective-permute-done.6.refs_0_.refs_2_ = bf16[256,1024]{1,0:T(8,128)(2,1)S(1)} collective-permute-done((bf16[256,1024]{1,0:T(8,128)(2,1)S(1)}, bf16[256,1024]{1,0:T(8,128)(2,1)S(1)}, u32[]{:S(2)}, u32[]{:S(2)}) %collective-permute-start.6) | collective-permute-done | bytes 524320 | tf_op jit(solution)/shard_map/ppermute | solution.py:594
  97.9 0.8 share.1
  98.6 14.2 %collective-permute-start.40 = (bf16[2,672,1024]{2,1,0:T(8,128)(2,1)S(1)}, bf16[2,672,1024]{2,1,0:T(8,128)(2,1)S(1)}, u32[]{:S(2)}, u32[]{:S(2)}) collective-permute-start(bf16[2,672,1024]{2,1,0:T(8,128)(2,1)S(1)} %get-tuple-element.58), channel_id=1, source_target_pairs={{0,1},{1,0},{2,3},{3,2},{4,5},{5,4},{6,7},{7,6},{8,9},{9,8},{10,11... | collective-permute-start | bytes 8257544 | tf_op jit(solution)/shard_map/ppermute | solution.py:578
  112.8 1.3 collective-permute-start.17
  114.1 1.3 collective-permute-start.16
  116.9 1.2 shard_map.163.own_ref
  118.1 1.3 shard_map.161
  119.5 10.0 %collective-permute-done.17.refs_1_ = bf16[256,1024]{1,0:T(8,128)(2,1)S(1)} collective-permute-done((bf16[256,1024]{1,0:T(8,128)(2,1)S(1)}, bf16[256,1024]{1,0:T(8,128)(2,1)S(1)}, u32[]{:S(2)}, u32[]{:S(2)}) %collective-permute-start.17) | collective-permute-done | bytes 524320 | tf_op jit(solution)/shard_map/ppermute | solution.py:594
  129.5 10.6 %collective-permute-done.16.refs_0_ = bf16[256,1024]{1,0:T(8,128)(2,1)S(1)} collective-permute-done((bf16[256,1024]{1,0:T(8,128)(2,1)S(1)}, bf16[256,1024]{1,0:T(8,128)(2,1)S(1)}, u32[]{:S(2)}, u32[]{:S(2)}) %collective-permute-start.16) | collective-permute-done | bytes 524320 | tf_op jit(solution)/shard_map/ppermute | solution.py:594
  140.2 1.6 shard_map.167.own_ref
  141.8 8.9 %collective-permute-start.32 = (bf16[256,1024]{1,0:T(8,128)(2,1)S(1)}, bf16[256,1024]{1,0:T(8,128)(2,1)S(1)}, u32[]{:S(2)}, u32[]{:S(2)}) collective-permute-start(bf16[256,1024]{1,0:T(8,128)(2,1)S(1)} %shard_map.167.own_ref), channel_id=1, source_target_pairs={{0,1},{1,0},{2,3},{3,2},{4,5},{5,4},{6,7},{7,6},{8,9},{9,8},{10,11... | collective-permute-start | bytes 1572872 | tf_op jit(solution)/shard_map/ppermute | solution.py:645
  150.7 1.3 shard_map.165.own_ref
  152.6 0.9 collective-permute-start.14
  154.2 1.3 shard_map.162
  155.6 0.8 collective-permute-start.11
  156.5 1.3 collective-permute-start.12
  160.2 12.5 %collective-permute-done.12.refs_1_ = bf16[256,1024]{1,0:T(8,128)(2,1)S(1)} collective-permute-done((bf16[256,1024]{1,0:T(8,128)(2,1)S(1)}, bf16[256,1024]{1,0:T(8,128)(2,1)S(1)}, u32[]{:S(2)}, u32[]{:S(2)}) %collective-permute-start.12) | collective-permute-done | bytes 524320 | tf_op jit(solution)/shard_map/ppermute | solution.py:619
  173.9 1.2 shard_map.169
  175.1 8.7 %collective-permute-start.35 = (bf16[64,1152]{1,0:T(8,128)(2,1)S(1)}, bf16[64,1152]{1,0:T(8,128)(2,1)S(1)}, u32[]{:S(2)}, u32[]{:S(2)}) collective-permute-start(bf16[64,1152]{1,0:T(8,128)(2,1)S(1)} %get-tuple-element.52), channel_id=1, source_target_pairs={{0,1},{1,0},{2,3},{3,2},{4,5},{5,4},{6,7},{7,6},{8,9},{9,8},{10,11... | collective-permute-start | bytes 442376 | tf_op jit(solution)/shard_map/ppermute | solution.py:655
  183.8 1.0 collective-permute-done.35.recv_ref
  185.0 8.3 %collective-permute-start.36 = (bf16[64,1152]{1,0:T(8,128)(2,1)S(1)}, bf16[64,1152]{1,0:T(8,128)(2,1)S(1)}, u32[]{:S(2)}, u32[]{:S(2)}) collective-permute-start(bf16[64,1152]{1,0:T(8,128)(2,1)S(1)} %shard_map.170.refs_0_), channel_id=1, source_target_pairs={{0,2},{1,3},{2,0},{3,1},{4,6},{5,7},{6,4},{7,5},{8,10},{9,11},{10,... | collective-permute-start | bytes 442376 | tf_op jit(solution)/shard_map/ppermute | solution.py:522
  193.3 4.2 %collective-permute-done.36.refs_1_ = bf16[64,1152]{1,0:T(8,128)(2,1)S(1)} collective-permute-done((bf16[64,1152]{1,0:T(8,128)(2,1)S(1)}, bf16[64,1152]{1,0:T(8,128)(2,1)S(1)}, u32[]{:S(2)}, u32[]{:S(2)}) %collective-permute-start.36) | collective-permute-done | bytes 147488 | tf_op jit(solution)/shard_map/ppermute | solution.py:522
  197.7 1.4 collective-permute-start.38
  199.1 2.9 %collective-permute-start.39 = (bf16[16,1152]{1,0:T(8,128)(2,1)S(1)}, bf16[16,1152]{1,0:T(8,128)(2,1)S(1)}, u32[]{:S(2)}, u32[]{:S(2)}) collective-permute-start(bf16[16,1152]{1,0:T(8,128)(2,1)S(1)} %get-tuple-element.56), channel_id=1, source_target_pairs={{0,12},{4,8},{8,4},{12,0},{1,13},{5,9},{9,5},{13,1},{2,14},{6,10},... | collective-permute-start | bytes 110600 | tf_op jit(solution)/shard_map/ppermute | solution.py:516
  202.1 1.0 collective-permute-done.38.refs_2_
  203.1 1.8 collective-permute-done.39.refs_3_
  204.9 1.5 shard_map.172
  206.5 3.5 %collective-permute-start.42 = (bf16[16,1024]{1,0:T(8,128)(2,1)S(1)}, bf16[16,1024]{1,0:T(8,128)(2,1)S(1)}, u32[]{:S(2)}, u32[]{:S(2)}) collective-permute-start(bf16[16,1024]{1,0:T(8,128)(2,1)S(1)} %get-tuple-element.61), channel_id=1, source_target_pairs={{0,8},{4,12},{8,0},{12,4},{1,9},{5,13},{9,1},{13,5},{2,10},{6,14},... | collective-permute-start | bytes 98312 | tf_op jit(solution)/shard_map/ppermute | solution.py:516
  210.0 0.9 collective-permute-start.43
  210.9 1.3 collective-permute-done.42.refs_2_
  212.2 3.5 %collective-permute-done.43.refs_3_ = bf16[16,1024]{1,0:T(8,128)(2,1)S(1)} collective-permute-done((bf16[16,1024]{1,0:T(8,128)(2,1)S(1)}, bf16[16,1024]{1,0:T(8,128)(2,1)S(1)}, u32[]{:S(2)}, u32[]{:S(2)}) %collective-permute-start.43) | collective-permute-done | bytes 32800 | tf_op jit(solution)/shard_map/ppermute | solution.py:516
  215.7 1.8 collective-permute-start.44
  217.5 3.2 %collective-permute-done.44.refs_1_ = bf16[64,1024]{1,0:T(8,128)(2,1)S(1)} collective-permute-done((bf16[64,1024]{1,0:T(8,128)(2,1)S(1)}, bf16[64,1024]{1,0:T(8,128)(2,1)S(1)}, u32[]{:S(2)}, u32[]{:S(2)}) %collective-permute-start.44) | collective-permute-done | bytes 131104 | tf_op jit(solution)/shard_map/ppermute | solution.py:522
  220.9 1.3 collective-permute-done.45.other_ref
  222.2 1.8 shard_map.175
  (91 shorter events, 10.7 us)
Async XLA Ops:
  0.0 1.2 copy-start.2
  1.2 0.8 copy-start.10
  2.1 0.8 copy-start.14
  5.3 16.8 %collective-permute-start = (bf16[144,512]{1,0:T(8,128)(2,1)S(1)}, bf16[144,512]{1,0:T(8,128)(2,1)S(1)}, u32[]{:S(2)}, u32[]{:S(2)}) collective-permute-start(bf16[144,512]{1,0:T(8,128)(2,1)S(1)} %get-tuple-element.40), channel_id=1, source_target_pairs={{0,4},{4,0},{8,12},{1,5},{5,1},{9,13},{2,6},{6,2},{10,14},{3,7},{7... | collective-permute-start | bytes 442376 | tf_op jit(solution)/shard_map/ppermute | solution.py:516
  10.3 11.9 %collective-permute-start.1 = (bf16[144,512]{1,0:T(8,128)(2,1)S(1)}, bf16[144,512]{1,0:T(8,128)(2,1)S(1)}, u32[]{:S(2)}, u32[]{:S(2)}) collective-permute-start(bf16[144,512]{1,0:T(8,128)(2,1)S(1)} %get-tuple-element.41), channel_id=1, source_target_pairs={{0,8},{4,12},{8,0},{1,9},{5,13},{9,1},{2,10},{6,14},{10,2},{3,11},... | collective-permute-start | bytes 442376 | tf_op jit(solution)/shard_map/ppermute | solution.py:516
  14.8 7.3 %collective-permute-start.2 = (bf16[144,512]{1,0:T(8,128)(2,1)S(1)}, bf16[144,512]{1,0:T(8,128)(2,1)S(1)}, u32[]{:S(2)}, u32[]{:S(2)}) collective-permute-start(bf16[144,512]{1,0:T(8,128)(2,1)S(1)} %get-tuple-element.42), channel_id=1, source_target_pairs={{0,12},{4,8},{8,4},{1,13},{5,9},{9,5},{2,14},{6,10},{10,6},{3,15},... | collective-permute-start | bytes 442376 | tf_op jit(solution)/shard_map/ppermute | solution.py:516
  16.1 2.2 copy-start
  18.6 36.1 %copy-start.3 = (bf16[256,2048]{1,0:T(8,128)(2,1)S(1)}, bf16[256,2048]{1,0:T(8,128)(2,1)}, u32[]{:S(2)}) copy-start(bf16[256,2048]{1,0:T(8,128)(2,1)} %x_ref.5) | copy-start | bytes 3145732
  18.6 36.1 %copy-start.9 = (bf16[256,128]{1,0:T(8,128)(2,1)S(1)}, bf16[256,128]{1,0:T(8,128)(2,1)}, u32[]{:S(2)}) copy-start(bf16[256,128]{1,0:T(8,128)(2,1)} %read_ref.7) | copy-start | bytes 196612
  18.6 36.1 %copy-start.11 = (bf16[256,128]{1,0:T(8,128)(2,1)S(1)}, bf16[256,128]{1,0:T(8,128)(2,1)}, u32[]{:S(2)}) copy-start(bf16[256,128]{1,0:T(8,128)(2,1)} %write_ref.5) | copy-start | bytes 196612
  18.6 54.9 %collective-permute-start.24 = (bf16[256,1024]{1,0:T(8,128)(2,1)S(1)}, bf16[256,1024]{1,0:T(8,128)(2,1)S(1)}, u32[]{:S(2)}, u32[]{:S(2)}) collective-permute-start(bf16[256,1024]{1,0:T(8,128)(2,1)S(1)} %get-tuple-element.47), channel_id=1, source_target_pairs={{0,4},{12,8},{1,5},{13,9},{2,6},{14,10},{3,7},{15,11},{16,20},{28,... | collective-permute-start | bytes 1572872 | tf_op jit(solution)/shard_map/ppermute | solution.py:530
  22.4 17.3 %collective-permute-start.3 = (bf16[128,512]{1,0:T(8,128)(2,1)S(1)}, bf16[128,512]{1,0:T(8,128)(2,1)S(1)}, u32[]{:S(2)}, u32[]{:S(2)}) collective-permute-start(bf16[128,512]{1,0:T(8,128)(2,1)S(1)} %get-tuple-element.44), channel_id=1, source_target_pairs={{0,4},{8,12},{12,8},{1,5},{9,13},{13,9},{2,6},{10,14},{14,10},{3,7... | collective-permute-start | bytes 393224 | tf_op jit(solution)/shard_map/ppermute | solution.py:516
  29.0 45.9 %collective-permute-start.25 = (bf16[256,1024]{1,0:T(8,128)(2,1)S(1)}, bf16[256,1024]{1,0:T(8,128)(2,1)S(1)}, u32[]{:S(2)}, u32[]{:S(2)}) collective-permute-start(bf16[256,1024]{1,0:T(8,128)(2,1)S(1)} %get-tuple-element.48), channel_id=1, source_target_pairs={{0,4},{12,8},{1,5},{13,9},{2,6},{14,10},{3,7},{15,11},{16,20},{28,... | collective-permute-start | bytes 1572872 | tf_op jit(solution)/shard_map/ppermute | solution.py:530
  30.3 21.0 %collective-permute-start.4 = (bf16[128,512]{1,0:T(8,128)(2,1)S(1)}, bf16[128,512]{1,0:T(8,128)(2,1)S(1)}, u32[]{:S(2)}, u32[]{:S(2)}) collective-permute-start(bf16[128,512]{1,0:T(8,128)(2,1)S(1)} %get-tuple-element.45), channel_id=1, source_target_pairs={{0,8},{4,12},{12,4},{1,9},{5,13},{13,5},{2,10},{6,14},{14,6},{3,11... | collective-permute-start | bytes 393224 | tf_op jit(solution)/shard_map/ppermute | solution.py:516
  34.1 46.0 %collective-permute-start.26 = (bf16[256,1024]{1,0:T(8,128)(2,1)S(1)}, bf16[256,1024]{1,0:T(8,128)(2,1)S(1)}, u32[]{:S(2)}, u32[]{:S(2)}) collective-permute-start(bf16[256,1024]{1,0:T(8,128)(2,1)S(1)} %get-tuple-element.49), channel_id=1, source_target_pairs={{0,4},{12,8},{1,5},{13,9},{2,6},{14,10},{3,7},{15,11},{16,20},{28,... | collective-permute-start | bytes 1572872 | tf_op jit(solution)/shard_map/ppermute | solution.py:530
  39.7 32.4 %collective-permute-start.23 = (bf16[128,1024]{1,0:T(8,128)(2,1)S(1)}, bf16[128,1024]{1,0:T(8,128)(2,1)S(1)}, u32[]{:S(2)}, u32[]{:S(2)}) collective-permute-start(bf16[128,1024]{1,0:T(8,128)(2,1)S(1)} %cut.2), channel_id=1, source_target_pairs={{0,4},{12,8},{1,5},{13,9},{2,6},{14,10},{3,7},{15,11},{16,20},{28,... | collective-permute-start | bytes 786440 | tf_op jit(solution)/shard_map/ppermute | solution.py:530
  51.3 17.9 %collective-permute-start.5 = (bf16[128,512]{1,0:T(8,128)(2,1)S(1)}, bf16[128,512]{1,0:T(8,128)(2,1)S(1)}, u32[]{:S(2)}, u32[]{:S(2)}) collective-permute-start(bf16[128,512]{1,0:T(8,128)(2,1)S(1)} %get-tuple-element.46), channel_id=1, source_target_pairs={{0,12},{4,8},{8,4},{1,13},{5,9},{9,5},{2,14},{6,10},{10,6},{3,15},... | collective-permute-start | bytes 393224 | tf_op jit(solution)/shard_map/ppermute | solution.py:516
  56.2 14.3 %copy-start.4 = (bf16[256,2048]{1,0:T(8,128)(2,1)S(1)}, bf16[256,2048]{1,0:T(8,128)(2,1)}, u32[]{:S(2)}) copy-start(bf16[256,2048]{1,0:T(8,128)(2,1)} %gate_ref.3) | copy-start | bytes 3145732
  56.2 14.3 %copy-start.13 = (f32[2048]{0:T(1024)S(1)}, f32[2048]{0:T(1024)}, u32[]{:S(2)}) copy-start(f32[2048]{0:T(1024)} %param.22) | copy-start | bytes 24580
  69.2 13.4 %collective-permute-start.27 = (bf16[256,1024]{1,0:T(8,128)(2,1)S(1)}, bf16[256,1024]{1,0:T(8,128)(2,1)S(1)}, u32[]{:S(2)}, u32[]{:S(2)}) collective-permute-start(bf16[256,1024]{1,0:T(8,128)(2,1)S(1)} %get-tuple-element.50), channel_id=1, source_target_pairs={{0,4},{12,8},{1,5},{13,9},{2,6},{14,10},{3,7},{15,11},{16,20},{28,... | collective-permute-start | bytes 1572872 | tf_op jit(solution)/shard_map/ppermute | solution.py:530
  70.5 27.3 %copy-start.6 = (bf16[2,672,1024]{2,1,0:T(8,128)(2,1)S(1)}, bf16[2,672,1024]{2,1,0:T(8,128)(2,1)}, u32[]{:S(2)}) copy-start(bf16[2,672,1024]{2,1,0:T(8,128)(2,1)} %down_ref.3) | copy-start | bytes 8257540
  71.3 26.5 %copy-start.5 = (bf16[2,1024,672]{1,2,0:T(8,128)(2,1)S(1)}, bf16[2,1024,672]{1,2,0:T(8,128)(2,1)}, u32[]{:S(2)}) copy-start(bf16[2,1024,672]{1,2,0:T(8,128)(2,1)} %param.27) | copy-start | bytes 8257540
  72.1 16.8 %collective-permute-start.7 = (bf16[256,1024]{1,0:T(8,128)(2,1)S(1)}, bf16[256,1024]{1,0:T(8,128)(2,1)S(1)}, u32[]{:S(2)}, u32[]{:S(2)}) collective-permute-start(bf16[256,1024]{1,0:T(8,128)(2,1)S(1)} %shard_map.160.refs_3_.refs_1_), channel_id=1, source_target_pairs={{4,0},{8,4},{12,8},{5,1},{9,5},{13,9},{6,2},{10,6},{14,10},{7,3},{... | collective-permute-start | bytes 1572872 | tf_op jit(solution)/shard_map/ppermute | solution.py:594
  73.5 23.6 %collective-permute-start.6 = (bf16[256,1024]{1,0:T(8,128)(2,1)S(1)}, bf16[256,1024]{1,0:T(8,128)(2,1)S(1)}, u32[]{:S(2)}, u32[]{:S(2)}) collective-permute-start(bf16[256,1024]{1,0:T(8,128)(2,1)S(1)} %shard_map.158.refs_2_.refs_0_), channel_id=1, source_target_pairs={{4,0},{8,4},{12,8},{5,1},{9,5},{13,9},{6,2},{10,6},{14,10},{7,3},{... | collective-permute-start | bytes 1572872 | tf_op jit(solution)/shard_map/ppermute | solution.py:594
  74.9 23.8 %collective-permute-start.9 = (bf16[256,1024]{1,0:T(8,128)(2,1)S(1)}, bf16[256,1024]{1,0:T(8,128)(2,1)S(1)}, u32[]{:S(2)}, u32[]{:S(2)}) collective-permute-start(bf16[256,1024]{1,0:T(8,128)(2,1)S(1)} %shard_map.160.refs_3_.refs_1_), channel_id=1, source_target_pairs={{0,4},{4,8},{8,12},{1,5},{5,9},{9,13},{2,6},{6,10},{10,14},{3,7},{... | collective-permute-start | bytes 1572872 | tf_op jit(solution)/shard_map/ppermute | solution.py:594
  80.1 7.4 %collective-permute-start.28 = (bf16[128,1024]{1,0:T(8,128)(2,1)S(1)}, bf16[128,1024]{1,0:T(8,128)(2,1)S(1)}, u32[]{:S(2)}, u32[]{:S(2)}) collective-permute-start(bf16[128,1024]{1,0:T(8,128)(2,1)S(1)} %collective-permute-done.23.refs_4_), channel_id=1, source_target_pairs={{4,20},{8,24},{20,4},{24,8},{5,21},{9,25},{21,5},{25,9},{6,22},{10... | collective-permute-start | bytes 786440 | tf_op jit(solution)/shard_map/ppermute | solution.py:535
  82.6 30.2 %collective-permute-start.8 = (bf16[256,1024]{1,0:T(8,128)(2,1)S(1)}, bf16[256,1024]{1,0:T(8,128)(2,1)S(1)}, u32[]{:S(2)}, u32[]{:S(2)}) collective-permute-start(bf16[256,1024]{1,0:T(8,128)(2,1)S(1)} %shard_map.158.refs_2_.refs_0_), channel_id=1, source_target_pairs={{0,4},{4,8},{8,12},{1,5},{5,9},{9,13},{2,6},{6,10},{10,14},{3,7},{... | collective-permute-start | bytes 1572872 | tf_op jit(solution)/shard_map/ppermute | solution.py:594
  87.5 26.7 %collective-permute-start.29 = (bf16[256,1024]{1,0:T(8,128)(2,1)S(1)}, bf16[256,1024]{1,0:T(8,128)(2,1)S(1)}, u32[]{:S(2)}, u32[]{:S(2)}) collective-permute-start(bf16[256,1024]{1,0:T(8,128)(2,1)S(1)} %collective-permute-done.24.refs_5_), channel_id=1, source_target_pairs={{4,20},{8,24},{20,4},{24,8},{5,21},{9,25},{21,5},{25,9},{6,22},{10... | collective-permute-start | bytes 1572872 | tf_op jit(solution)/shard_map/ppermute | solution.py:535
  88.9 26.5 %collective-permute-start.30 = (bf16[256,1024]{1,0:T(8,128)(2,1)S(1)}, bf16[256,1024]{1,0:T(8,128)(2,1)S(1)}, u32[]{:S(2)}, u32[]{:S(2)}) collective-permute-start(bf16[256,1024]{1,0:T(8,128)(2,1)S(1)} %collective-permute-done.25.refs_6_), channel_id=1, source_target_pairs={{4,20},{8,24},{20,4},{24,8},{5,21},{9,25},{21,5},{25,9},{6,22},{10... | collective-permute-start | bytes 1572872 | tf_op jit(solution)/shard_map/ppermute | solution.py:535
  97.1 19.0 %collective-permute-start.31 = (bf16[256,1024]{1,0:T(8,128)(2,1)S(1)}, bf16[256,1024]{1,0:T(8,128)(2,1)S(1)}, u32[]{:S(2)}, u32[]{:S(2)}) collective-permute-start(bf16[256,1024]{1,0:T(8,128)(2,1)S(1)} %collective-permute-done.26.refs_7_), channel_id=1, source_target_pairs={{4,20},{8,24},{20,4},{24,8},{5,21},{9,25},{21,5},{25,9},{6,22},{10... | collective-permute-start | bytes 1572872 | tf_op jit(solution)/shard_map/ppermute | solution.py:535
  97.9 19.0 %copy-start.1 = (bf16[2048,1024]{1,0:T(8,128)(2,1)S(1)}, bf16[2048,1024]{1,0:T(8,128)(2,1)}, u32[]{:S(2)}) copy-start(bf16[2048,1024]{1,0:T(8,128)(2,1)} %w_ref.3) | copy-start | bytes 12582916
  98.6 106.2 %collective-permute-start.40 = (bf16[2,672,1024]{2,1,0:T(8,128)(2,1)S(1)}, bf16[2,672,1024]{2,1,0:T(8,128)(2,1)S(1)}, u32[]{:S(2)}, u32[]{:S(2)}) collective-permute-start(bf16[2,672,1024]{2,1,0:T(8,128)(2,1)S(1)} %get-tuple-element.58), channel_id=1, source_target_pairs={{0,1},{1,0},{2,3},{3,2},{4,5},{5,4},{6,7},{7,6},{8,9},{9,8},{10,11... | collective-permute-start | bytes 8257544 | tf_op jit(solution)/shard_map/ppermute | solution.py:578
  112.8 16.7 %collective-permute-start.17 = (bf16[256,1024]{1,0:T(8,128)(2,1)S(1)}, bf16[256,1024]{1,0:T(8,128)(2,1)S(1)}, u32[]{:S(2)}, u32[]{:S(2)}) collective-permute-start(bf16[256,1024]{1,0:T(8,128)(2,1)S(1)} %collective-permute-done.7.refs_1_.refs_3_), channel_id=1, source_target_pairs={{4,0},{8,4},{5,1},{9,5},{6,2},{10,6},{7,3},{11,7},{20,16},{24,20},... | collective-permute-start | bytes 1572872 | tf_op jit(solution)/shard_map/ppermute | solution.py:594
  114.1 26.0 %collective-permute-start.16 = (bf16[256,1024]{1,0:T(8,128)(2,1)S(1)}, bf16[256,1024]{1,0:T(8,128)(2,1)S(1)}, u32[]{:S(2)}, u32[]{:S(2)}) collective-permute-start(bf16[256,1024]{1,0:T(8,128)(2,1)S(1)} %collective-permute-done.6.refs_0_.refs_2_), channel_id=1, source_target_pairs={{4,0},{8,4},{5,1},{9,5},{6,2},{10,6},{7,3},{11,7},{20,16},{24,20},... | collective-permute-start | bytes 1572872 | tf_op jit(solution)/shard_map/ppermute | solution.py:594
  115.5 24.7 %collective-permute-start.19 = (bf16[256,1024]{1,0:T(8,128)(2,1)S(1)}, bf16[256,1024]{1,0:T(8,128)(2,1)S(1)}, u32[]{:S(2)}, u32[]{:S(2)}) collective-permute-start(bf16[256,1024]{1,0:T(8,128)(2,1)S(1)} %collective-permute-done.9.refs_5_), channel_id=1, source_target_pairs={{4,8},{8,12},{5,9},{9,13},{6,10},{10,14},{7,11},{11,15},{20,24},{2... | collective-permute-start | bytes 1572872 | tf_op jit(solution)/shard_map/ppermute | solution.py:594
  116.2 24.0 %collective-permute-start.18 = (bf16[256,1024]{1,0:T(8,128)(2,1)S(1)}, bf16[256,1024]{1,0:T(8,128)(2,1)S(1)}, u32[]{:S(2)}, u32[]{:S(2)}) collective-permute-start(bf16[256,1024]{1,0:T(8,128)(2,1)S(1)} %collective-permute-done.8.refs_4_), channel_id=1, source_target_pairs={{4,8},{8,12},{5,9},{9,13},{6,10},{10,14},{7,11},{11,15},{20,24},{2... | collective-permute-start | bytes 1572872 | tf_op jit(solution)/shard_map/ppermute | solution.py:594
  129.5 23.0 %collective-permute-start.13 = (bf16[256,1024]{1,0:T(8,128)(2,1)S(1)}, bf16[256,1024]{1,0:T(8,128)(2,1)S(1)}, u32[]{:S(2)}, u32[]{:S(2)}) collective-permute-start(bf16[256,1024]{1,0:T(8,128)(2,1)S(1)} %shard_map.163.own_ref), channel_id=1, source_target_pairs={{0,1},{1,0},{2,3},{3,2},{4,5},{5,4},{6,7},{7,6},{8,9},{9,8},{10,11... | collective-permute-start | bytes 1572872 | tf_op jit(solution)/shard_map/ppermute | solution.py:640
  140.2 13.4 %collective-permute-start.10 = (bf16[256,1024]{1,0:T(8,128)(2,1)S(1)}, bf16[256,1024]{1,0:T(8,128)(2,1)S(1)}, u32[]{:S(2)}, u32[]{:S(2)}) collective-permute-start(bf16[256,1024]{1,0:T(8,128)(2,1)S(1)} %shard_map.161), channel_id=1, source_target_pairs={{0,1},{1,0},{2,3},{3,2},{4,5},{5,4},{6,7},{7,6},{8,9},{9,8},{10,11... | collective-permute-start | bytes 1572872 | tf_op jit(solution)/shard_map/ppermute | solution.py:633
  141.8 13.8 %collective-permute-start.32 = (bf16[256,1024]{1,0:T(8,128)(2,1)S(1)}, bf16[256,1024]{1,0:T(8,128)(2,1)S(1)}, u32[]{:S(2)}, u32[]{:S(2)}) collective-permute-start(bf16[256,1024]{1,0:T(8,128)(2,1)S(1)} %shard_map.167.own_ref), channel_id=1, source_target_pairs={{0,1},{1,0},{2,3},{3,2},{4,5},{5,4},{6,7},{7,6},{8,9},{9,8},{10,11... | collective-permute-start | bytes 1572872 | tf_op jit(solution)/shard_map/ppermute | solution.py:645
  152.1 4.4 %collective-permute-start.20 = (bf16[256,1024]{1,0:T(8,128)(2,1)S(1)}, bf16[256,1024]{1,0:T(8,128)(2,1)S(1)}, u32[]{:S(2)}, u32[]{:S(2)}) collective-permute-start(bf16[256,1024]{1,0:T(8,128)(2,1)S(1)} %shard_map.165.own_ref), channel_id=1, source_target_pairs={{0,1},{1,0},{2,3},{3,2},{4,5},{5,4},{6,7},{7,6},{8,9},{9,8},{10,11... | collective-permute-start | bytes 1572872 | tf_op jit(solution)/shard_map/ppermute | solution.py:640
  152.6 5.4 %collective-permute-start.14 = (bf16[256,1024]{1,0:T(8,128)(2,1)S(1)}, bf16[256,1024]{1,0:T(8,128)(2,1)S(1)}, u32[]{:S(2)}, u32[]{:S(2)}) collective-permute-start(bf16[256,1024]{1,0:T(8,128)(2,1)S(1)} %shard_map.164), channel_id=1, source_target_pairs={{4,9},{8,14},{20,25},{24,30}} | collective-permute-start | bytes 1572872 | tf_op jit(solution)/shard_map/ppermute | solution.py:619
  153.5 5.3 %collective-permute-start.15 = (bf16[256,1024]{1,0:T(8,128)(2,1)S(1)}, bf16[256,1024]{1,0:T(8,128)(2,1)S(1)}, u32[]{:S(2)}, u32[]{:S(2)}) collective-permute-start(bf16[256,1024]{1,0:T(8,128)(2,1)S(1)} %shard_map.164), channel_id=1, source_target_pairs={{6,9},{10,14},{22,25},{26,30}} | collective-permute-start | bytes 1572872 | tf_op jit(solution)/shard_map/ppermute | solution.py:619
  155.6 17.8 %copy-start.15 = (s32[256,22]{0,1:T(8,128)S(1)}, s32[256,22]{0,1:T(8,128)}, u32[]{:S(2)}) copy-start(s32[256,22]{0,1:T(8,128)} %param.30) | copy-start | bytes 67588
  155.6 17.8 %copy-start.16 = (s32[256,22]{0,1:T(8,128)S(1)}, s32[256,22]{0,1:T(8,128)}, u32[]{:S(2)}) copy-start(s32[256,22]{0,1:T(8,128)} %param.31) | copy-start | bytes 67588
  155.6 18.2 %copy-start.7 = (bf16[1024,1024]{1,0:T(8,128)(2,1)S(1)}, bf16[1024,1024]{1,0:T(8,128)(2,1)}, u32[]{:S(2)}) copy-start(bf16[1024,1024]{1,0:T(8,128)(2,1)} %down_ref.2) | copy-start | bytes 6291460
  155.6 18.2 %copy-start.12 = (bf16[256,1024]{1,0:T(8,128)(2,1)S(1)}, bf16[256,1024]{1,0:T(8,128)(2,1)}, u32[]{:S(2)}) copy-start(bf16[256,1024]{1,0:T(8,128)(2,1)} %resin_ref.1) | copy-start | bytes 1572868
  155.6 18.2 %copy-start.17 = (f32[1024]{0:T(1024)S(1)}, f32[1024]{0:T(1024)}, u32[]{:S(2)}) copy-start(f32[1024]{0:T(1024)} %param.25) | copy-start | bytes 12292
  155.6 3.8 %collective-permute-start.11 = (bf16[256,1024]{1,0:T(8,128)(2,1)S(1)}, bf16[256,1024]{1,0:T(8,128)(2,1)S(1)}, u32[]{:S(2)}, u32[]{:S(2)}) collective-permute-start(bf16[256,1024]{1,0:T(8,128)(2,1)S(1)} %shard_map.162), channel_id=1, source_target_pairs={{0,0},{1,4},{4,5},{5,1},{8,10},{9,6},{12,15},{13,11},{16,16},{17,2... | collective-permute-start | bytes 1572872 | tf_op jit(solution)/shard_map/ppermute | solution.py:619
  156.5 16.2 %collective-permute-start.12 = (bf16[256,1024]{1,0:T(8,128)(2,1)S(1)}, bf16[256,1024]{1,0:T(8,128)(2,1)S(1)}, u32[]{:S(2)}, u32[]{:S(2)}) collective-permute-start(bf16[256,1024]{1,0:T(8,128)(2,1)S(1)} %shard_map.162), channel_id=1, source_target_pairs={{2,0},{3,4},{6,5},{7,1},{10,10},{11,6},{14,15},{15,11},{18,16},{19... | collective-permute-start | bytes 1572872 | tf_op jit(solution)/shard_map/ppermute | solution.py:619
  158.1 15.7 %collective-permute-start.33 = (bf16[256,1024]{1,0:T(8,128)(2,1)S(1)}, bf16[256,1024]{1,0:T(8,128)(2,1)S(1)}, u32[]{:S(2)}, u32[]{:S(2)}) collective-permute-start(bf16[256,1024]{1,0:T(8,128)(2,1)S(1)} %shard_map.168), channel_id=1, source_target_pairs={{4,12},{8,3},{20,28},{24,19}} | collective-permute-start | bytes 1572872 | tf_op jit(solution)/shard_map/ppermute | solution.py:619
  158.8 15.0 %collective-permute-start.34 = (bf16[256,1024]{1,0:T(8,128)(2,1)S(1)}, bf16[256,1024]{1,0:T(8,128)(2,1)S(1)}, u32[]{:S(2)}, u32[]{:S(2)}) collective-permute-start(bf16[256,1024]{1,0:T(8,128)(2,1)S(1)} %shard_map.168), channel_id=1, source_target_pairs={{6,12},{10,3},{22,28},{26,19}} | collective-permute-start | bytes 1572872 | tf_op jit(solution)/shard_map/ppermute | solution.py:619
  159.5 14.3 %collective-permute-start.21 = (bf16[256,1024]{1,0:T(8,128)(2,1)S(1)}, bf16[256,1024]{1,0:T(8,128)(2,1)S(1)}, u32[]{:S(2)}, u32[]{:S(2)}) collective-permute-start(bf16[256,1024]{1,0:T(8,128)(2,1)S(1)} %shard_map.166), channel_id=1, source_target_pairs={{1,8},{5,13},{9,2},{13,7},{17,24},{21,29},{25,18},{29,23}} | collective-permute-start | bytes 1572872 | tf_op jit(solution)/shard_map/ppermute | solution.py:619
  172.7 1.1 collective-permute-start.22
  175.1 9.7 %collective-permute-start.35 = (bf16[64,1152]{1,0:T(8,128)(2,1)S(1)}, bf16[64,1152]{1,0:T(8,128)(2,1)S(1)}, u32[]{:S(2)}, u32[]{:S(2)}) collective-permute-start(bf16[64,1152]{1,0:T(8,128)(2,1)S(1)} %get-tuple-element.52), channel_id=1, source_target_pairs={{0,1},{1,0},{2,3},{3,2},{4,5},{5,4},{6,7},{7,6},{8,9},{9,8},{10,11... | collective-permute-start | bytes 442376 | tf_op jit(solution)/shard_map/ppermute | solution.py:655
  185.0 12.4 %collective-permute-start.36 = (bf16[64,1152]{1,0:T(8,128)(2,1)S(1)}, bf16[64,1152]{1,0:T(8,128)(2,1)S(1)}, u32[]{:S(2)}, u32[]{:S(2)}) collective-permute-start(bf16[64,1152]{1,0:T(8,128)(2,1)S(1)} %shard_map.170.refs_0_), channel_id=1, source_target_pairs={{0,2},{1,3},{2,0},{3,1},{4,6},{5,7},{6,4},{7,5},{8,10},{9,11},{10,... | collective-permute-start | bytes 442376 | tf_op jit(solution)/shard_map/ppermute | solution.py:522
  197.6 4.5 %collective-permute-start.37 = (bf16[16,1152]{1,0:T(8,128)(2,1)S(1)}, bf16[16,1152]{1,0:T(8,128)(2,1)S(1)}, u32[]{:S(2)}, u32[]{:S(2)}) collective-permute-start(bf16[16,1152]{1,0:T(8,128)(2,1)S(1)} %get-tuple-element.54), channel_id=1, source_target_pairs={{0,4},{4,0},{8,12},{12,8},{1,5},{5,1},{9,13},{13,9},{2,6},{6,2},{1... | collective-permute-start | bytes 110600 | tf_op jit(solution)/shard_map/ppermute | solution.py:516
  197.7 5.4 %collective-permute-start.38 = (bf16[16,1152]{1,0:T(8,128)(2,1)S(1)}, bf16[16,1152]{1,0:T(8,128)(2,1)S(1)}, u32[]{:S(2)}, u32[]{:S(2)}) collective-permute-start(bf16[16,1152]{1,0:T(8,128)(2,1)S(1)} %get-tuple-element.55), channel_id=1, source_target_pairs={{0,8},{4,12},{8,0},{12,4},{1,9},{5,13},{9,1},{13,5},{2,10},{6,14},... | collective-permute-start | bytes 110600 | tf_op jit(solution)/shard_map/ppermute | solution.py:516
  199.1 5.8 %collective-permute-start.39 = (bf16[16,1152]{1,0:T(8,128)(2,1)S(1)}, bf16[16,1152]{1,0:T(8,128)(2,1)S(1)}, u32[]{:S(2)}, u32[]{:S(2)}) collective-permute-start(bf16[16,1152]{1,0:T(8,128)(2,1)S(1)} %get-tuple-element.56), channel_id=1, source_target_pairs={{0,12},{4,8},{8,4},{12,0},{1,13},{5,9},{9,5},{13,1},{2,14},{6,10},... | collective-permute-start | bytes 110600 | tf_op jit(solution)/shard_map/ppermute | solution.py:516
  204.9 17.3 %copy-start.8 = (bf16[1024,1024]{1,0:T(8,128)(2,1)S(1)}, bf16[1024,1024]{1,0:T(8,128)(2,1)}, u32[]{:S(2)}) copy-start(bf16[1024,1024]{1,0:T(8,128)(2,1)} %up_ref.1) | copy-start | bytes 6291460
  206.4 4.5 %collective-permute-start.41 = (bf16[16,1024]{1,0:T(8,128)(2,1)S(1)}, bf16[16,1024]{1,0:T(8,128)(2,1)S(1)}, u32[]{:S(2)}, u32[]{:S(2)}) collective-permute-start(bf16[16,1024]{1,0:T(8,128)(2,1)S(1)} %get-tuple-element.60), channel_id=1, source_target_pairs={{0,4},{4,0},{8,12},{12,8},{1,5},{5,1},{9,13},{13,9},{2,6},{6,2},{1... | collective-permute-start | bytes 98312 | tf_op jit(solution)/shard_map/ppermute | solution.py:516
  206.5 5.7 %collective-permute-start.42 = (bf16[16,1024]{1,0:T(8,128)(2,1)S(1)}, bf16[16,1024]{1,0:T(8,128)(2,1)S(1)}, u32[]{:S(2)}, u32[]{:S(2)}) collective-permute-start(bf16[16,1024]{1,0:T(8,128)(2,1)S(1)} %get-tuple-element.61), channel_id=1, source_target_pairs={{0,8},{4,12},{8,0},{12,4},{1,9},{5,13},{9,1},{13,5},{2,10},{6,14},... | collective-permute-start | bytes 98312 | tf_op jit(solution)/shard_map/ppermute | solution.py:516
  210.0 5.7 %collective-permute-start.43 = (bf16[16,1024]{1,0:T(8,128)(2,1)S(1)}, bf16[16,1024]{1,0:T(8,128)(2,1)S(1)}, u32[]{:S(2)}, u32[]{:S(2)}) collective-permute-start(bf16[16,1024]{1,0:T(8,128)(2,1)S(1)} %get-tuple-element.62), channel_id=1, source_target_pairs={{0,12},{4,8},{8,4},{12,0},{1,13},{5,9},{9,5},{13,1},{2,14},{6,10},... | collective-permute-start | bytes 98312 | tf_op jit(solution)/shard_map/ppermute | solution.py:516
  215.7 5.0 %collective-permute-start.44 = (bf16[64,1024]{1,0:T(8,128)(2,1)S(1)}, bf16[64,1024]{1,0:T(8,128)(2,1)S(1)}, u32[]{:S(2)}, u32[]{:S(2)}) collective-permute-start(bf16[64,1024]{1,0:T(8,128)(2,1)S(1)} %shard_map.173.refs_0_), channel_id=1, source_target_pairs={{0,2},{1,3},{2,0},{3,1},{4,6},{5,7},{6,4},{7,5},{8,10},{9,11},{10,... | collective-permute-start | bytes 393224 | tf_op jit(solution)/shard_map/ppermute | solution.py:522
  220.8 1.4 collective-permute-start.45
  (1 other events, 0.7 us)

commit v3 on v2

--- a/solution.py
+++ b/solution.py
@@ -524,7 +524,7 @@
 
     plan = plan_of(out_weight.shape[0], ny)
     chunks = cut(out_weight, pltpu.HBM, plan, range(1))
-    chunks = chunks + cut(out_weight, pl.ANY, plan, range(1, len(plan)))
+    chunks = chunks + cut(out_weight, pltpu.HBM, plan, range(1, len(plan)))
     far = [[] for _ in range(ny)]
     for j, chunk in enumerate(chunks):
         far[0].append(lax.ppermute(chunk, "ctx", [(0, 1), (n - 1, n - 2)]))
@@ -642,7 +642,8 @@
         rest(held, entries_of(lambda k: i, (keeper,)))
     choice, cands = options(lambda k: n - 1)
     (own,) = project_far(choice, cands, far)
-    recv = lax.ppermute(own, "heads", swap)
+    perm = [(c * nh + i, c * nh + i - 1) for c in (1, n - 2) for i in range(1, nh, 2)]
+    recv = lax.ppermute(own, both, perm)
     (held,) = fold(own, recv, 1)
     rest(held, [(1, 0, 0, n - 1), (n - 2, 0, n - 1, 0)])
 

time: 225 us -> 229 us (1.018); the launches traced: 224 us -> 226 us
  starting transfers between devices: 114 us -> 121 us
  waiting for transfers between devices: 81.8 us -> 77.6 us
    ppermute x8, waiting for transfers between devices: 12.5 us -> 7.4 us  [rest(): got.append(lax.ppermute(held, both, perm))]
    ppermute x1, starting transfers between devices: 8.69 us -> 13.8 us  [local(): recv = lax.ppermute(apart, 'heads', swap)]
    unnamed x38 -> x36, local copies, waits for them, and re-layouts: 5.74 us -> 3.56 us
    ppermute x3 -> x2, starting transfers between devices: 9.36 us -> 10.3 us  [local(): recv = lax.ppermute(own, 'heads', swap)]
  transfers between devices with their start and end apart: 46 -> 46, of which waited for: 16 -> 16; matrix products, arithmetic and copies ran while one was open for 0% -> 0% of each run, Pallas kernels for 7% -> 8%
where the time goes in v3:
time: 229 us; the launch traced here: 226 us
  starting transfers between devices  121 us (53%)
  waiting for transfers between devices  77.6 us (34%)
  Pallas kernels  22.7 us (10%)
  local copies, waits for them, and re-layouts  3.56 us (2%)
    ppermute x12, starting transfers between devices, exchange(): out.append(lax.ppermute(arrays[k], 'ctx', perm))  34.2 us
    ppermute x8, waiting for transfers between devices, local(): out.append(lax.ppermute(a, 'ctx', perm))  29.6 us
    ppermute x12, waiting for transfers between devices, exchange(): out.append(lax.ppermute(arrays[k], 'ctx', perm))  28.7 us
    pallas_call x22, Pallas kernels, call(): pl.pallas_call(body, in_specs=[VM] * len(args), out_specs=[VM] * len(outs...  19.4 us
    ppermute x8, starting transfers between devices, local(): out.append(lax.ppermute(a, 'ctx', perm))  16.4 us
    ppermute x1, starting transfers between devices, local(): taken = lax.ppermute(given, 'heads', swap)  14.3 us
    ppermute x1, starting transfers between devices, local(): recv = lax.ppermute(apart, 'heads', swap)  13.8 us
    ppermute x5, starting transfers between devices, local(): far[0].append(lax.ppermute(chunk, 'ctx', [(0, 1), (n - 1, n - 2)]))  12.1 us
  transfers between devices with their start and end apart: 46, of which 16 were waited for; matrix products, arithmetic and copies ran while one was open for 0% of the time, Pallas kernels for 8%

profile of v3, /device:TPU:0, one launch (start us, length us, event | category | flops | bytes accessed | tf_op | source)
XLA Modules:
  0.0 225.7 jit_solution(8718510407332937705)
XLA Ops:
  0.0 1.2 copy-done.1
  1.2 0.8 copy-done.9
  2.1 0.8 copy-done.13
  3.5 1.9 shard_map.155
  5.4 5.0 %collective-permute-start = (bf16[144,512]{1,0:T(8,128)(2,1)S(1)}, bf16[144,512]{1,0:T(8,128)(2,1)S(1)}, u32[]{:S(2)}, u32[]{:S(2)}) collective-permute-start(bf16[144,512]{1,0:T(8,128)(2,1)S(1)} %get-tuple-element.40), channel_id=1, source_target_pairs={{0,4},{4,0},{8,12},{1,5},{5,1},{9,13},{2,6},{6,2},{10,14},{3,7},{7... | collective-permute-start | bytes 442376 | tf_op jit(solution)/shard_map/ppermute | solution.py:516
  10.3 4.5 %collective-permute-start.1 = (bf16[144,512]{1,0:T(8,128)(2,1)S(1)}, bf16[144,512]{1,0:T(8,128)(2,1)S(1)}, u32[]{:S(2)}, u32[]{:S(2)}) collective-permute-start(bf16[144,512]{1,0:T(8,128)(2,1)S(1)} %get-tuple-element.41), channel_id=1, source_target_pairs={{0,8},{4,12},{8,0},{1,9},{5,13},{9,1},{2,10},{6,14},{10,2},{3,11},... | collective-permute-start | bytes 442376 | tf_op jit(solution)/shard_map/ppermute | solution.py:516
  14.8 1.3 collective-permute-start.2
  16.2 1.6 cut.3
  17.8 3.6 %collective-permute-start.24 = (bf16[256,1024]{1,0:T(8,128)(2,1)S(1)}, bf16[256,1024]{1,0:T(8,128)(2,1)S(1)}, u32[]{:S(2)}, u32[]{:S(2)}) collective-permute-start(bf16[256,1024]{1,0:T(8,128)(2,1)S(1)} %get-tuple-element.47), channel_id=1, source_target_pairs={{0,4},{12,8},{1,5},{13,9},{2,6},{14,10},{3,7},{15,11},{16,20},{28,... | collective-permute-start | bytes 1572872 | tf_op jit(solution)/shard_map/ppermute | solution.py:530
  21.6 7.4 %collective-permute-start.3 = (bf16[128,512]{1,0:T(8,128)(2,1)S(1)}, bf16[128,512]{1,0:T(8,128)(2,1)S(1)}, u32[]{:S(2)}, u32[]{:S(2)}) collective-permute-start(bf16[128,512]{1,0:T(8,128)(2,1)S(1)} %get-tuple-element.44), channel_id=1, source_target_pairs={{0,4},{8,12},{12,8},{1,5},{9,13},{13,9},{2,6},{10,14},{14,10},{3,7... | collective-permute-start | bytes 393224 | tf_op jit(solution)/shard_map/ppermute | solution.py:516
  29.0 1.3 collective-permute-start.25
  30.3 3.8 %collective-permute-start.4 = (bf16[128,512]{1,0:T(8,128)(2,1)S(1)}, bf16[128,512]{1,0:T(8,128)(2,1)S(1)}, u32[]{:S(2)}, u32[]{:S(2)}) collective-permute-start(bf16[128,512]{1,0:T(8,128)(2,1)S(1)} %get-tuple-element.45), channel_id=1, source_target_pairs={{0,8},{4,12},{12,4},{1,9},{5,13},{13,5},{2,10},{6,14},{14,6},{3,11... | collective-permute-start | bytes 393224 | tf_op jit(solution)/shard_map/ppermute | solution.py:516
  34.1 4.6 %collective-permute-start.26 = (bf16[256,1024]{1,0:T(8,128)(2,1)S(1)}, bf16[256,1024]{1,0:T(8,128)(2,1)S(1)}, u32[]{:S(2)}, u32[]{:S(2)}) collective-permute-start(bf16[256,1024]{1,0:T(8,128)(2,1)S(1)} %get-tuple-element.49), channel_id=1, source_target_pairs={{0,4},{12,8},{1,5},{13,9},{2,6},{14,10},{3,7},{15,11},{16,20},{28,... | collective-permute-start | bytes 1572872 | tf_op jit(solution)/shard_map/ppermute | solution.py:530
  38.7 1.0 cut.2
  39.7 1.3 collective-permute-start.23
  41.0 9.4 %collective-permute-done.4.refs_2_ = bf16[128,512]{1,0:T(8,128)(2,1)S(1)} collective-permute-done((bf16[128,512]{1,0:T(8,128)(2,1)S(1)}, bf16[128,512]{1,0:T(8,128)(2,1)S(1)}, u32[]{:S(2)}, u32[]{:S(2)}) %collective-permute-start.4) | collective-permute-done | bytes 131104 | tf_op jit(solution)/shard_map/ppermute | solution.py:516
  50.5 3.3 %collective-permute-start.5 = (bf16[128,512]{1,0:T(8,128)(2,1)S(1)}, bf16[128,512]{1,0:T(8,128)(2,1)S(1)}, u32[]{:S(2)}, u32[]{:S(2)}) collective-permute-start(bf16[128,512]{1,0:T(8,128)(2,1)S(1)} %get-tuple-element.46), channel_id=1, source_target_pairs={{0,12},{4,8},{8,4},{1,13},{5,9},{9,5},{2,14},{6,10},{10,6},{3,15},... | collective-permute-start | bytes 393224 | tf_op jit(solution)/shard_map/ppermute | solution.py:516
  53.8 1.5 shard_map.159.base_ref
  55.4 1.5 shard_map.156.base_ref
  56.9 11.7 %collective-permute-done.5.refs_3_ = bf16[128,512]{1,0:T(8,128)(2,1)S(1)} collective-permute-done((bf16[128,512]{1,0:T(8,128)(2,1)S(1)}, bf16[128,512]{1,0:T(8,128)(2,1)S(1)}, u32[]{:S(2)}, u32[]{:S(2)}) %collective-permute-start.5) | collective-permute-done | bytes 131104 | tf_op jit(solution)/shard_map/ppermute | solution.py:516
  68.6 1.3 collective-permute-start.27
  70.0 0.8 shard_map.160.refs_3_.refs_1_
  70.8 0.8 shard_map.158.refs_2_.refs_0_
  71.6 1.3 collective-permute-start.7
  72.9 1.3 collective-permute-start.6
  74.2 5.2 %collective-permute-start.9 = (bf16[256,1024]{1,0:T(8,128)(2,1)S(1)}, bf16[256,1024]{1,0:T(8,128)(2,1)S(1)}, u32[]{:S(2)}, u32[]{:S(2)}) collective-permute-start(bf16[256,1024]{1,0:T(8,128)(2,1)S(1)} %shard_map.160.refs_3_.refs_1_), channel_id=1, source_target_pairs={{0,4},{4,8},{8,12},{1,5},{5,9},{9,13},{2,6},{6,10},{10,14},{3,7},{... | collective-permute-start | bytes 1572872 | tf_op jit(solution)/shard_map/ppermute | solution.py:594
  80.1 2.1 collective-permute-done.27.refs_8_
  82.2 4.6 %collective-permute-start.8 = (bf16[256,1024]{1,0:T(8,128)(2,1)S(1)}, bf16[256,1024]{1,0:T(8,128)(2,1)S(1)}, u32[]{:S(2)}, u32[]{:S(2)}) collective-permute-start(bf16[256,1024]{1,0:T(8,128)(2,1)S(1)} %shard_map.158.refs_2_.refs_0_), channel_id=1, source_target_pairs={{0,4},{4,8},{8,12},{1,5},{5,9},{9,13},{2,6},{6,10},{10,14},{3,7},{... | collective-permute-start | bytes 1572872 | tf_op jit(solution)/shard_map/ppermute | solution.py:594
  87.5 0.8 collective-permute-done.7.refs_1_.refs_3_
  89.0 8.2 %collective-permute-done.6.refs_0_.refs_2_ = bf16[256,1024]{1,0:T(8,128)(2,1)S(1)} collective-permute-done((bf16[256,1024]{1,0:T(8,128)(2,1)S(1)}, bf16[256,1024]{1,0:T(8,128)(2,1)S(1)}, u32[]{:S(2)}, u32[]{:S(2)}) %collective-permute-start.6) | collective-permute-done | bytes 524320 | tf_op jit(solution)/shard_map/ppermute | solution.py:594
  97.9 0.8 share.1
  98.6 14.3 %collective-permute-start.40 = (bf16[2,672,1024]{2,1,0:T(8,128)(2,1)S(1)}, bf16[2,672,1024]{2,1,0:T(8,128)(2,1)S(1)}, u32[]{:S(2)}, u32[]{:S(2)}) collective-permute-start(bf16[2,672,1024]{2,1,0:T(8,128)(2,1)S(1)} %get-tuple-element.58), channel_id=1, source_target_pairs={{0,1},{1,0},{2,3},{3,2},{4,5},{5,4},{6,7},{7,6},{8,9},{9,8},{10,11... | collective-permute-start | bytes 8257544 | tf_op jit(solution)/shard_map/ppermute | solution.py:578
  112.9 1.3 collective-permute-start.17
  114.2 1.3 collective-permute-start.16
  117.0 1.2 shard_map.163.own_ref
  118.2 1.3 shard_map.161
  119.6 10.0 %collective-permute-done.17.refs_1_ = bf16[256,1024]{1,0:T(8,128)(2,1)S(1)} collective-permute-done((bf16[256,1024]{1,0:T(8,128)(2,1)S(1)}, bf16[256,1024]{1,0:T(8,128)(2,1)S(1)}, u32[]{:S(2)}, u32[]{:S(2)}) %collective-permute-start.17) | collective-permute-done | bytes 524320 | tf_op jit(solution)/shard_map/ppermute | solution.py:594
  129.6 10.6 %collective-permute-done.16.refs_0_ = bf16[256,1024]{1,0:T(8,128)(2,1)S(1)} collective-permute-done((bf16[256,1024]{1,0:T(8,128)(2,1)S(1)}, bf16[256,1024]{1,0:T(8,128)(2,1)S(1)}, u32[]{:S(2)}, u32[]{:S(2)}) %collective-permute-start.16) | collective-permute-done | bytes 524320 | tf_op jit(solution)/shard_map/ppermute | solution.py:594
  140.3 1.6 shard_map.167.own_ref
  142.6 1.3 shard_map.165.own_ref
  143.9 10.3 %collective-permute-start.20 = (bf16[256,1024]{1,0:T(8,128)(2,1)S(1)}, bf16[256,1024]{1,0:T(8,128)(2,1)S(1)}, u32[]{:S(2)}, u32[]{:S(2)}) collective-permute-start(bf16[256,1024]{1,0:T(8,128)(2,1)S(1)} %shard_map.165.own_ref), channel_id=1, source_target_pairs={{0,1},{1,0},{2,3},{3,2},{4,5},{5,4},{6,7},{7,6},{8,9},{9,8},{10,11... | collective-permute-start | bytes 1572872 | tf_op jit(solution)/shard_map/ppermute | solution.py:640
  154.4 0.9 collective-permute-start.14
  156.0 1.3 shard_map.162
  157.4 0.8 collective-permute-start.11
  158.2 1.3 collective-permute-start.12
  161.9 7.4 %collective-permute-done.12.refs_1_ = bf16[256,1024]{1,0:T(8,128)(2,1)S(1)} collective-permute-done((bf16[256,1024]{1,0:T(8,128)(2,1)S(1)}, bf16[256,1024]{1,0:T(8,128)(2,1)S(1)}, u32[]{:S(2)}, u32[]{:S(2)}) %collective-permute-start.12) | collective-permute-done | bytes 524320 | tf_op jit(solution)/shard_map/ppermute | solution.py:619
  170.5 1.2 shard_map.169
  171.7 13.8 %collective-permute-start.35 = (bf16[64,1152]{1,0:T(8,128)(2,1)S(1)}, bf16[64,1152]{1,0:T(8,128)(2,1)S(1)}, u32[]{:S(2)}, u32[]{:S(2)}) collective-permute-start(bf16[64,1152]{1,0:T(8,128)(2,1)S(1)} %get-tuple-element.52), channel_id=1, source_target_pairs={{0,1},{1,0},{2,3},{3,2},{4,5},{5,4},{6,7},{7,6},{8,9},{9,8},{10,11... | collective-permute-start | bytes 442376 | tf_op jit(solution)/shard_map/ppermute | solution.py:656
  185.5 1.0 collective-permute-done.35.recv_ref
  186.7 8.3 %collective-permute-start.36 = (bf16[64,1152]{1,0:T(8,128)(2,1)S(1)}, bf16[64,1152]{1,0:T(8,128)(2,1)S(1)}, u32[]{:S(2)}, u32[]{:S(2)}) collective-permute-start(bf16[64,1152]{1,0:T(8,128)(2,1)S(1)} %shard_map.170.refs_0_), channel_id=1, source_target_pairs={{0,2},{1,3},{2,0},{3,1},{4,6},{5,7},{6,4},{7,5},{8,10},{9,11},{10,... | collective-permute-start | bytes 442376 | tf_op jit(solution)/shard_map/ppermute | solution.py:522
  195.0 4.2 %collective-permute-done.36.refs_1_ = bf16[64,1152]{1,0:T(8,128)(2,1)S(1)} collective-permute-done((bf16[64,1152]{1,0:T(8,128)(2,1)S(1)}, bf16[64,1152]{1,0:T(8,128)(2,1)S(1)}, u32[]{:S(2)}, u32[]{:S(2)}) %collective-permute-start.36) | collective-permute-done | bytes 147488 | tf_op jit(solution)/shard_map/ppermute | solution.py:522
  199.4 1.6 collective-permute-start.38
  201.0 2.7 %collective-permute-start.39 = (bf16[16,1152]{1,0:T(8,128)(2,1)S(1)}, bf16[16,1152]{1,0:T(8,128)(2,1)S(1)}, u32[]{:S(2)}, u32[]{:S(2)}) collective-permute-start(bf16[16,1152]{1,0:T(8,128)(2,1)S(1)} %get-tuple-element.56), channel_id=1, source_target_pairs={{0,12},{4,8},{8,4},{12,0},{1,13},{5,9},{9,5},{13,1},{2,14},{6,10},... | collective-permute-start | bytes 110600 | tf_op jit(solution)/shard_map/ppermute | solution.py:516
  203.8 1.0 collective-permute-done.38.refs_2_
  204.8 2.0 collective-permute-done.39.refs_3_
  206.8 1.5 shard_map.172
  208.4 3.3 %collective-permute-start.42 = (bf16[16,1024]{1,0:T(8,128)(2,1)S(1)}, bf16[16,1024]{1,0:T(8,128)(2,1)S(1)}, u32[]{:S(2)}, u32[]{:S(2)}) collective-permute-start(bf16[16,1024]{1,0:T(8,128)(2,1)S(1)} %get-tuple-element.61), channel_id=1, source_target_pairs={{0,8},{4,12},{8,0},{12,4},{1,9},{5,13},{9,1},{13,5},{2,10},{6,14},... | collective-permute-start | bytes 98312 | tf_op jit(solution)/shard_map/ppermute | solution.py:516
  211.7 1.1 collective-permute-start.43
  212.8 1.2 collective-permute-done.42.refs_2_
  213.9 3.5 %collective-permute-done.43.refs_3_ = bf16[16,1024]{1,0:T(8,128)(2,1)S(1)} collective-permute-done((bf16[16,1024]{1,0:T(8,128)(2,1)S(1)}, bf16[16,1024]{1,0:T(8,128)(2,1)S(1)}, u32[]{:S(2)}, u32[]{:S(2)}) %collective-permute-start.43) | collective-permute-done | bytes 32800 | tf_op jit(solution)/shard_map/ppermute | solution.py:516
  217.4 1.8 collective-permute-start.44
  219.2 3.2 %collective-permute-done.44.refs_1_ = bf16[64,1024]{1,0:T(8,128)(2,1)S(1)} collective-permute-done((bf16[64,1024]{1,0:T(8,128)(2,1)S(1)}, bf16[64,1024]{1,0:T(8,128)(2,1)S(1)}, u32[]{:S(2)}, u32[]{:S(2)}) %collective-permute-start.44) | collective-permute-done | bytes 131104 | tf_op jit(solution)/shard_map/ppermute | solution.py:522
  222.6 1.3 collective-permute-done.45.other_ref
  223.9 1.8 shard_map.175
  (89 shorter events, 10.7 us)
Async XLA Ops:
  0.0 1.2 copy-start.1
  1.2 0.8 copy-start.9
  2.1 0.8 copy-start.13
  2.8 0.7 copy-start.17
  5.4 16.0 %collective-permute-start = (bf16[144,512]{1,0:T(8,128)(2,1)S(1)}, bf16[144,512]{1,0:T(8,128)(2,1)S(1)}, u32[]{:S(2)}, u32[]{:S(2)}) collective-permute-start(bf16[144,512]{1,0:T(8,128)(2,1)S(1)} %get-tuple-element.40), channel_id=1, source_target_pairs={{0,4},{4,0},{8,12},{1,5},{5,1},{9,13},{2,6},{6,2},{10,14},{3,7},{7... | collective-permute-start | bytes 442376 | tf_op jit(solution)/shard_map/ppermute | solution.py:516
  10.3 11.0 %collective-permute-start.1 = (bf16[144,512]{1,0:T(8,128)(2,1)S(1)}, bf16[144,512]{1,0:T(8,128)(2,1)S(1)}, u32[]{:S(2)}, u32[]{:S(2)}) collective-permute-start(bf16[144,512]{1,0:T(8,128)(2,1)S(1)} %get-tuple-element.41), channel_id=1, source_target_pairs={{0,8},{4,12},{8,0},{1,9},{5,13},{9,1},{2,10},{6,14},{10,2},{3,11},... | collective-permute-start | bytes 442376 | tf_op jit(solution)/shard_map/ppermute | solution.py:516
  14.8 6.5 %collective-permute-start.2 = (bf16[144,512]{1,0:T(8,128)(2,1)S(1)}, bf16[144,512]{1,0:T(8,128)(2,1)S(1)}, u32[]{:S(2)}, u32[]{:S(2)}) collective-permute-start(bf16[144,512]{1,0:T(8,128)(2,1)S(1)} %get-tuple-element.42), channel_id=1, source_target_pairs={{0,12},{4,8},{8,4},{1,13},{5,9},{9,5},{2,14},{6,10},{10,6},{3,15},... | collective-permute-start | bytes 442376 | tf_op jit(solution)/shard_map/ppermute | solution.py:516
  17.7 36.1 %copy-start.2 = (bf16[256,2048]{1,0:T(8,128)(2,1)S(1)}, bf16[256,2048]{1,0:T(8,128)(2,1)}, u32[]{:S(2)}) copy-start(bf16[256,2048]{1,0:T(8,128)(2,1)} %x_ref.5) | copy-start | bytes 3145732
  17.8 36.1 %copy-start.8 = (bf16[256,128]{1,0:T(8,128)(2,1)S(1)}, bf16[256,128]{1,0:T(8,128)(2,1)}, u32[]{:S(2)}) copy-start(bf16[256,128]{1,0:T(8,128)(2,1)} %read_ref.7) | copy-start | bytes 196612
  17.8 36.1 %copy-start.10 = (bf16[256,128]{1,0:T(8,128)(2,1)S(1)}, bf16[256,128]{1,0:T(8,128)(2,1)}, u32[]{:S(2)}) copy-start(bf16[256,128]{1,0:T(8,128)(2,1)} %write_ref.5) | copy-start | bytes 196612
  17.8 55.1 %collective-permute-start.24 = (bf16[256,1024]{1,0:T(8,128)(2,1)S(1)}, bf16[256,1024]{1,0:T(8,128)(2,1)S(1)}, u32[]{:S(2)}, u32[]{:S(2)}) collective-permute-start(bf16[256,1024]{1,0:T(8,128)(2,1)S(1)} %get-tuple-element.47), channel_id=1, source_target_pairs={{0,4},{12,8},{1,5},{13,9},{2,6},{14,10},{3,7},{15,11},{16,20},{28,... | collective-permute-start | bytes 1572872 | tf_op jit(solution)/shard_map/ppermute | solution.py:530
  21.6 18.1 %collective-permute-start.3 = (bf16[128,512]{1,0:T(8,128)(2,1)S(1)}, bf16[128,512]{1,0:T(8,128)(2,1)S(1)}, u32[]{:S(2)}, u32[]{:S(2)}) collective-permute-start(bf16[128,512]{1,0:T(8,128)(2,1)S(1)} %get-tuple-element.44), channel_id=1, source_target_pairs={{0,4},{8,12},{12,8},{1,5},{9,13},{13,9},{2,6},{10,14},{14,10},{3,7... | collective-permute-start | bytes 393224 | tf_op jit(solution)/shard_map/ppermute | solution.py:516
  29.0 45.2 %collective-permute-start.25 = (bf16[256,1024]{1,0:T(8,128)(2,1)S(1)}, bf16[256,1024]{1,0:T(8,128)(2,1)S(1)}, u32[]{:S(2)}, u32[]{:S(2)}) collective-permute-start(bf16[256,1024]{1,0:T(8,128)(2,1)S(1)} %get-tuple-element.48), channel_id=1, source_target_pairs={{0,4},{12,8},{1,5},{13,9},{2,6},{14,10},{3,7},{15,11},{16,20},{28,... | collective-permute-start | bytes 1572872 | tf_op jit(solution)/shard_map/ppermute | solution.py:530
  30.3 20.2 %collective-permute-start.4 = (bf16[128,512]{1,0:T(8,128)(2,1)S(1)}, bf16[128,512]{1,0:T(8,128)(2,1)S(1)}, u32[]{:S(2)}, u32[]{:S(2)}) collective-permute-start(bf16[128,512]{1,0:T(8,128)(2,1)S(1)} %get-tuple-element.45), channel_id=1, source_target_pairs={{0,8},{4,12},{12,4},{1,9},{5,13},{13,5},{2,10},{6,14},{14,6},{3,11... | collective-permute-start | bytes 393224 | tf_op jit(solution)/shard_map/ppermute | solution.py:516
  34.1 45.3 %collective-permute-start.26 = (bf16[256,1024]{1,0:T(8,128)(2,1)S(1)}, bf16[256,1024]{1,0:T(8,128)(2,1)S(1)}, u32[]{:S(2)}, u32[]{:S(2)}) collective-permute-start(bf16[256,1024]{1,0:T(8,128)(2,1)S(1)} %get-tuple-element.49), channel_id=1, source_target_pairs={{0,4},{12,8},{1,5},{13,9},{2,6},{14,10},{3,7},{15,11},{16,20},{28,... | collective-permute-start | bytes 1572872 | tf_op jit(solution)/shard_map/ppermute | solution.py:530
  39.7 31.9 %collective-permute-start.23 = (bf16[128,1024]{1,0:T(8,128)(2,1)S(1)}, bf16[128,1024]{1,0:T(8,128)(2,1)S(1)}, u32[]{:S(2)}, u32[]{:S(2)}) collective-permute-start(bf16[128,1024]{1,0:T(8,128)(2,1)S(1)} %cut.2), channel_id=1, source_target_pairs={{0,4},{12,8},{1,5},{13,9},{2,6},{14,10},{3,7},{15,11},{16,20},{28,... | collective-permute-start | bytes 786440 | tf_op jit(solution)/shard_map/ppermute | solution.py:530
  50.5 18.1 %collective-permute-start.5 = (bf16[128,512]{1,0:T(8,128)(2,1)S(1)}, bf16[128,512]{1,0:T(8,128)(2,1)S(1)}, u32[]{:S(2)}, u32[]{:S(2)}) collective-permute-start(bf16[128,512]{1,0:T(8,128)(2,1)S(1)} %get-tuple-element.46), channel_id=1, source_target_pairs={{0,12},{4,8},{8,4},{1,13},{5,9},{9,5},{2,14},{6,10},{10,6},{3,15},... | collective-permute-start | bytes 393224 | tf_op jit(solution)/shard_map/ppermute | solution.py:516
  55.4 14.6 %copy-start.3 = (bf16[256,2048]{1,0:T(8,128)(2,1)S(1)}, bf16[256,2048]{1,0:T(8,128)(2,1)}, u32[]{:S(2)}) copy-start(bf16[256,2048]{1,0:T(8,128)(2,1)} %gate_ref.3) | copy-start | bytes 3145732
  55.4 14.6 %copy-start.12 = (f32[2048]{0:T(1024)S(1)}, f32[2048]{0:T(1024)}, u32[]{:S(2)}) copy-start(f32[2048]{0:T(1024)} %param.22) | copy-start | bytes 24580
  68.6 13.6 %collective-permute-start.27 = (bf16[256,1024]{1,0:T(8,128)(2,1)S(1)}, bf16[256,1024]{1,0:T(8,128)(2,1)S(1)}, u32[]{:S(2)}, u32[]{:S(2)}) collective-permute-start(bf16[256,1024]{1,0:T(8,128)(2,1)S(1)} %get-tuple-element.50), channel_id=1, source_target_pairs={{0,4},{12,8},{1,5},{13,9},{2,6},{14,10},{3,7},{15,11},{16,20},{28,... | collective-permute-start | bytes 1572872 | tf_op jit(solution)/shard_map/ppermute | solution.py:530
  69.9 27.9 %copy-start.5 = (bf16[2,672,1024]{2,1,0:T(8,128)(2,1)S(1)}, bf16[2,672,1024]{2,1,0:T(8,128)(2,1)}, u32[]{:S(2)}) copy-start(bf16[2,672,1024]{2,1,0:T(8,128)(2,1)} %down_ref.3) | copy-start | bytes 8257540
  70.8 27.1 %copy-start.4 = (bf16[2,1024,672]{1,2,0:T(8,128)(2,1)S(1)}, bf16[2,1024,672]{1,2,0:T(8,128)(2,1)}, u32[]{:S(2)}) copy-start(bf16[2,1024,672]{1,2,0:T(8,128)(2,1)} %param.27) | copy-start | bytes 8257540
  71.6 16.7 %collective-permute-start.7 = (bf16[256,1024]{1,0:T(8,128)(2,1)S(1)}, bf16[256,1024]{1,0:T(8,128)(2,1)S(1)}, u32[]{:S(2)}, u32[]{:S(2)}) collective-permute-start(bf16[256,1024]{1,0:T(8,128)(2,1)S(1)} %shard_map.160.refs_3_.refs_1_), channel_id=1, source_target_pairs={{4,0},{8,4},{12,8},{5,1},{9,5},{13,9},{6,2},{10,6},{14,10},{7,3},{... | collective-permute-start | bytes 1572872 | tf_op jit(solution)/shard_map/ppermute | solution.py:594
  72.9 24.2 %collective-permute-start.6 = (bf16[256,1024]{1,0:T(8,128)(2,1)S(1)}, bf16[256,1024]{1,0:T(8,128)(2,1)S(1)}, u32[]{:S(2)}, u32[]{:S(2)}) collective-permute-start(bf16[256,1024]{1,0:T(8,128)(2,1)S(1)} %shard_map.158.refs_2_.refs_0_), channel_id=1, source_target_pairs={{4,0},{8,4},{12,8},{5,1},{9,5},{13,9},{6,2},{10,6},{14,10},{7,3},{... | collective-permute-start | bytes 1572872 | tf_op jit(solution)/shard_map/ppermute | solution.py:594
  74.2 24.4 %collective-permute-start.9 = (bf16[256,1024]{1,0:T(8,128)(2,1)S(1)}, bf16[256,1024]{1,0:T(8,128)(2,1)S(1)}, u32[]{:S(2)}, u32[]{:S(2)}) collective-permute-start(bf16[256,1024]{1,0:T(8,128)(2,1)S(1)} %shard_map.160.refs_3_.refs_1_), channel_id=1, source_target_pairs={{0,4},{4,8},{8,12},{1,5},{5,9},{9,13},{2,6},{6,10},{10,14},{3,7},{... | collective-permute-start | bytes 1572872 | tf_op jit(solution)/shard_map/ppermute | solution.py:594
  79.4 7.4 %collective-permute-start.28 = (bf16[128,1024]{1,0:T(8,128)(2,1)S(1)}, bf16[128,1024]{1,0:T(8,128)(2,1)S(1)}, u32[]{:S(2)}, u32[]{:S(2)}) collective-permute-start(bf16[128,1024]{1,0:T(8,128)(2,1)S(1)} %collective-permute-done.23.refs_4_), channel_id=1, source_target_pairs={{4,20},{8,24},{20,4},{24,8},{5,21},{9,25},{21,5},{25,9},{6,22},{10... | collective-permute-start | bytes 786440 | tf_op jit(solution)/shard_map/ppermute | solution.py:535
  82.2 30.7 %collective-permute-start.8 = (bf16[256,1024]{1,0:T(8,128)(2,1)S(1)}, bf16[256,1024]{1,0:T(8,128)(2,1)S(1)}, u32[]{:S(2)}, u32[]{:S(2)}) collective-permute-start(bf16[256,1024]{1,0:T(8,128)(2,1)S(1)} %shard_map.158.refs_2_.refs_0_), channel_id=1, source_target_pairs={{0,4},{4,8},{8,12},{1,5},{5,9},{9,13},{2,6},{6,10},{10,14},{3,7},{... | collective-permute-start | bytes 1572872 | tf_op jit(solution)/shard_map/ppermute | solution.py:594
  86.8 27.4 %collective-permute-start.29 = (bf16[256,1024]{1,0:T(8,128)(2,1)S(1)}, bf16[256,1024]{1,0:T(8,128)(2,1)S(1)}, u32[]{:S(2)}, u32[]{:S(2)}) collective-permute-start(bf16[256,1024]{1,0:T(8,128)(2,1)S(1)} %collective-permute-done.24.refs_5_), channel_id=1, source_target_pairs={{4,20},{8,24},{20,4},{24,8},{5,21},{9,25},{21,5},{25,9},{6,22},{10... | collective-permute-start | bytes 1572872 | tf_op jit(solution)/shard_map/ppermute | solution.py:535
  88.3 27.3 %collective-permute-start.30 = (bf16[256,1024]{1,0:T(8,128)(2,1)S(1)}, bf16[256,1024]{1,0:T(8,128)(2,1)S(1)}, u32[]{:S(2)}, u32[]{:S(2)}) collective-permute-start(bf16[256,1024]{1,0:T(8,128)(2,1)S(1)} %collective-permute-done.25.refs_6_), channel_id=1, source_target_pairs={{4,20},{8,24},{20,4},{24,8},{5,21},{9,25},{21,5},{25,9},{6,22},{10... | collective-permute-start | bytes 1572872 | tf_op jit(solution)/shard_map/ppermute | solution.py:535
  97.1 19.1 %collective-permute-start.31 = (bf16[256,1024]{1,0:T(8,128)(2,1)S(1)}, bf16[256,1024]{1,0:T(8,128)(2,1)S(1)}, u32[]{:S(2)}, u32[]{:S(2)}) collective-permute-start(bf16[256,1024]{1,0:T(8,128)(2,1)S(1)} %collective-permute-done.26.refs_7_), channel_id=1, source_target_pairs={{4,20},{8,24},{20,4},{24,8},{5,21},{9,25},{21,5},{25,9},{6,22},{10... | collective-permute-start | bytes 1572872 | tf_op jit(solution)/shard_map/ppermute | solution.py:535
  97.9 19.1 %copy-start = (bf16[2048,1024]{1,0:T(8,128)(2,1)S(1)}, bf16[2048,1024]{1,0:T(8,128)(2,1)}, u32[]{:S(2)}) copy-start(bf16[2048,1024]{1,0:T(8,128)(2,1)} %w_ref.3) | copy-start | bytes 12582916
  98.6 108.1 %collective-permute-start.40 = (bf16[2,672,1024]{2,1,0:T(8,128)(2,1)S(1)}, bf16[2,672,1024]{2,1,0:T(8,128)(2,1)S(1)}, u32[]{:S(2)}, u32[]{:S(2)}) collective-permute-start(bf16[2,672,1024]{2,1,0:T(8,128)(2,1)S(1)} %get-tuple-element.58), channel_id=1, source_target_pairs={{0,1},{1,0},{2,3},{3,2},{4,5},{5,4},{6,7},{7,6},{8,9},{9,8},{10,11... | collective-permute-start | bytes 8257544 | tf_op jit(solution)/shard_map/ppermute | solution.py:578
  112.9 16.7 %collective-permute-start.17 = (bf16[256,1024]{1,0:T(8,128)(2,1)S(1)}, bf16[256,1024]{1,0:T(8,128)(2,1)S(1)}, u32[]{:S(2)}, u32[]{:S(2)}) collective-permute-start(bf16[256,1024]{1,0:T(8,128)(2,1)S(1)} %collective-permute-done.7.refs_1_.refs_3_), channel_id=1, source_target_pairs={{4,0},{8,4},{5,1},{9,5},{6,2},{10,6},{7,3},{11,7},{20,16},{24,20},... | collective-permute-start | bytes 1572872 | tf_op jit(solution)/shard_map/ppermute | solution.py:594
  114.2 26.0 %collective-permute-start.16 = (bf16[256,1024]{1,0:T(8,128)(2,1)S(1)}, bf16[256,1024]{1,0:T(8,128)(2,1)S(1)}, u32[]{:S(2)}, u32[]{:S(2)}) collective-permute-start(bf16[256,1024]{1,0:T(8,128)(2,1)S(1)} %collective-permute-done.6.refs_0_.refs_2_), channel_id=1, source_target_pairs={{4,0},{8,4},{5,1},{9,5},{6,2},{10,6},{7,3},{11,7},{20,16},{24,20},... | collective-permute-start | bytes 1572872 | tf_op jit(solution)/shard_map/ppermute | solution.py:594
  115.6 24.7 %collective-permute-start.19 = (bf16[256,1024]{1,0:T(8,128)(2,1)S(1)}, bf16[256,1024]{1,0:T(8,128)(2,1)S(1)}, u32[]{:S(2)}, u32[]{:S(2)}) collective-permute-start(bf16[256,1024]{1,0:T(8,128)(2,1)S(1)} %collective-permute-done.9.refs_5_), channel_id=1, source_target_pairs={{4,8},{8,12},{5,9},{9,13},{6,10},{10,14},{7,11},{11,15},{20,24},{2... | collective-permute-start | bytes 1572872 | tf_op jit(solution)/shard_map/ppermute | solution.py:594
  116.3 24.0 %collective-permute-start.18 = (bf16[256,1024]{1,0:T(8,128)(2,1)S(1)}, bf16[256,1024]{1,0:T(8,128)(2,1)S(1)}, u32[]{:S(2)}, u32[]{:S(2)}) collective-permute-start(bf16[256,1024]{1,0:T(8,128)(2,1)S(1)} %collective-permute-done.8.refs_4_), channel_id=1, source_target_pairs={{4,8},{8,12},{5,9},{9,13},{6,10},{10,14},{7,11},{11,15},{20,24},{2... | collective-permute-start | bytes 1572872 | tf_op jit(solution)/shard_map/ppermute | solution.py:594
  129.6 24.6 %collective-permute-start.13 = (bf16[256,1024]{1,0:T(8,128)(2,1)S(1)}, bf16[256,1024]{1,0:T(8,128)(2,1)S(1)}, u32[]{:S(2)}, u32[]{:S(2)}) collective-permute-start(bf16[256,1024]{1,0:T(8,128)(2,1)S(1)} %shard_map.163.own_ref), channel_id=1, source_target_pairs={{0,1},{1,0},{2,3},{3,2},{4,5},{5,4},{6,7},{7,6},{8,9},{9,8},{10,11... | collective-permute-start | bytes 1572872 | tf_op jit(solution)/shard_map/ppermute | solution.py:640
  140.2 15.0 %collective-permute-start.10 = (bf16[256,1024]{1,0:T(8,128)(2,1)S(1)}, bf16[256,1024]{1,0:T(8,128)(2,1)S(1)}, u32[]{:S(2)}, u32[]{:S(2)}) collective-permute-start(bf16[256,1024]{1,0:T(8,128)(2,1)S(1)} %shard_map.161), channel_id=1, source_target_pairs={{0,1},{1,0},{2,3},{3,2},{4,5},{5,4},{6,7},{7,6},{8,9},{9,8},{10,11... | collective-permute-start | bytes 1572872 | tf_op jit(solution)/shard_map/ppermute | solution.py:633
  141.9 15.5 %collective-permute-start.32 = (bf16[256,1024]{1,0:T(8,128)(2,1)S(1)}, bf16[256,1024]{1,0:T(8,128)(2,1)S(1)}, u32[]{:S(2)}, u32[]{:S(2)}) collective-permute-start(bf16[256,1024]{1,0:T(8,128)(2,1)S(1)} %shard_map.167.own_ref), channel_id=1, source_target_pairs={{5,4},{7,6},{9,8},{11,10},{21,20},{23,22},{25,24},{27,26}} | collective-permute-start | bytes 1572872 | tf_op jit(solution)/shard_map/ppermute | solution.py:646
  143.9 14.3 %collective-permute-start.20 = (bf16[256,1024]{1,0:T(8,128)(2,1)S(1)}, bf16[256,1024]{1,0:T(8,128)(2,1)S(1)}, u32[]{:S(2)}, u32[]{:S(2)}) collective-permute-start(bf16[256,1024]{1,0:T(8,128)(2,1)S(1)} %shard_map.165.own_ref), channel_id=1, source_target_pairs={{0,1},{1,0},{2,3},{3,2},{4,5},{5,4},{6,7},{7,6},{8,9},{9,8},{10,11... | collective-permute-start | bytes 1572872 | tf_op jit(solution)/shard_map/ppermute | solution.py:640
  154.4 5.4 %collective-permute-start.14 = (bf16[256,1024]{1,0:T(8,128)(2,1)S(1)}, bf16[256,1024]{1,0:T(8,128)(2,1)S(1)}, u32[]{:S(2)}, u32[]{:S(2)}) collective-permute-start(bf16[256,1024]{1,0:T(8,128)(2,1)S(1)} %shard_map.164), channel_id=1, source_target_pairs={{4,9},{8,14},{20,25},{24,30}} | collective-permute-start | bytes 1572872 | tf_op jit(solution)/shard_map/ppermute | solution.py:619
  155.3 5.3 %collective-permute-start.15 = (bf16[256,1024]{1,0:T(8,128)(2,1)S(1)}, bf16[256,1024]{1,0:T(8,128)(2,1)S(1)}, u32[]{:S(2)}, u32[]{:S(2)}) collective-permute-start(bf16[256,1024]{1,0:T(8,128)(2,1)S(1)} %shard_map.164), channel_id=1, source_target_pairs={{6,9},{10,14},{22,25},{26,30}} | collective-permute-start | bytes 1572872 | tf_op jit(solution)/shard_map/ppermute | solution.py:619
  157.3 12.7 %copy-start.14 = (s32[256,22]{0,1:T(8,128)S(1)}, s32[256,22]{0,1:T(8,128)}, u32[]{:S(2)}) copy-start(s32[256,22]{0,1:T(8,128)} %param.30) | copy-start | bytes 67588
  157.3 12.7 %copy-start.15 = (s32[256,22]{0,1:T(8,128)S(1)}, s32[256,22]{0,1:T(8,128)}, u32[]{:S(2)}) copy-start(s32[256,22]{0,1:T(8,128)} %param.31) | copy-start | bytes 67588
  157.3 13.1 %copy-start.6 = (bf16[1024,1024]{1,0:T(8,128)(2,1)S(1)}, bf16[1024,1024]{1,0:T(8,128)(2,1)}, u32[]{:S(2)}) copy-start(bf16[1024,1024]{1,0:T(8,128)(2,1)} %down_ref.2) | copy-start | bytes 6291460
  157.4 13.1 %copy-start.11 = (bf16[256,1024]{1,0:T(8,128)(2,1)S(1)}, bf16[256,1024]{1,0:T(8,128)(2,1)}, u32[]{:S(2)}) copy-start(bf16[256,1024]{1,0:T(8,128)(2,1)} %resin_ref.1) | copy-start | bytes 1572868
  157.4 13.1 %copy-start.16 = (f32[1024]{0:T(1024)S(1)}, f32[1024]{0:T(1024)}, u32[]{:S(2)}) copy-start(f32[1024]{0:T(1024)} %param.25) | copy-start | bytes 12292
  157.4 3.8 %collective-permute-start.11 = (bf16[256,1024]{1,0:T(8,128)(2,1)S(1)}, bf16[256,1024]{1,0:T(8,128)(2,1)S(1)}, u32[]{:S(2)}, u32[]{:S(2)}) collective-permute-start(bf16[256,1024]{1,0:T(8,128)(2,1)S(1)} %shard_map.162), channel_id=1, source_target_pairs={{0,0},{1,4},{4,5},{5,1},{8,10},{9,6},{12,15},{13,11},{16,16},{17,2... | collective-permute-start | bytes 1572872 | tf_op jit(solution)/shard_map/ppermute | solution.py:619
  158.2 11.1 %collective-permute-start.12 = (bf16[256,1024]{1,0:T(8,128)(2,1)S(1)}, bf16[256,1024]{1,0:T(8,128)(2,1)S(1)}, u32[]{:S(2)}, u32[]{:S(2)}) collective-permute-start(bf16[256,1024]{1,0:T(8,128)(2,1)S(1)} %shard_map.162), channel_id=1, source_target_pairs={{2,0},{3,4},{6,5},{7,1},{10,10},{11,6},{14,15},{15,11},{18,16},{19... | collective-permute-start | bytes 1572872 | tf_op jit(solution)/shard_map/ppermute | solution.py:619
  159.8 10.6 %collective-permute-start.33 = (bf16[256,1024]{1,0:T(8,128)(2,1)S(1)}, bf16[256,1024]{1,0:T(8,128)(2,1)S(1)}, u32[]{:S(2)}, u32[]{:S(2)}) collective-permute-start(bf16[256,1024]{1,0:T(8,128)(2,1)S(1)} %shard_map.168), channel_id=1, source_target_pairs={{4,12},{8,3},{20,28},{24,19}} | collective-permute-start | bytes 1572872 | tf_op jit(solution)/shard_map/ppermute | solution.py:619
  160.5 9.9 %collective-permute-start.34 = (bf16[256,1024]{1,0:T(8,128)(2,1)S(1)}, bf16[256,1024]{1,0:T(8,128)(2,1)S(1)}, u32[]{:S(2)}, u32[]{:S(2)}) collective-permute-start(bf16[256,1024]{1,0:T(8,128)(2,1)S(1)} %shard_map.168), channel_id=1, source_target_pairs={{6,12},{10,3},{22,28},{26,19}} | collective-permute-start | bytes 1572872 | tf_op jit(solution)/shard_map/ppermute | solution.py:619
  161.2 9.2 %collective-permute-start.21 = (bf16[256,1024]{1,0:T(8,128)(2,1)S(1)}, bf16[256,1024]{1,0:T(8,128)(2,1)S(1)}, u32[]{:S(2)}, u32[]{:S(2)}) collective-permute-start(bf16[256,1024]{1,0:T(8,128)(2,1)S(1)} %shard_map.166), channel_id=1, source_target_pairs={{1,8},{5,13},{9,2},{13,7},{17,24},{21,29},{25,18},{29,23}} | collective-permute-start | bytes 1572872 | tf_op jit(solution)/shard_map/ppermute | solution.py:619
  169.3 1.1 collective-permute-start.22
  171.7 14.8 %collective-permute-start.35 = (bf16[64,1152]{1,0:T(8,128)(2,1)S(1)}, bf16[64,1152]{1,0:T(8,128)(2,1)S(1)}, u32[]{:S(2)}, u32[]{:S(2)}) collective-permute-start(bf16[64,1152]{1,0:T(8,128)(2,1)S(1)} %get-tuple-element.52), channel_id=1, source_target_pairs={{0,1},{1,0},{2,3},{3,2},{4,5},{5,4},{6,7},{7,6},{8,9},{9,8},{10,11... | collective-permute-start | bytes 442376 | tf_op jit(solution)/shard_map/ppermute | solution.py:656
  186.7 12.4 %collective-permute-start.36 = (bf16[64,1152]{1,0:T(8,128)(2,1)S(1)}, bf16[64,1152]{1,0:T(8,128)(2,1)S(1)}, u32[]{:S(2)}, u32[]{:S(2)}) collective-permute-start(bf16[64,1152]{1,0:T(8,128)(2,1)S(1)} %shard_map.170.refs_0_), channel_id=1, source_target_pairs={{0,2},{1,3},{2,0},{3,1},{4,6},{5,7},{6,4},{7,5},{8,10},{9,11},{10,... | collective-permute-start | bytes 442376 | tf_op jit(solution)/shard_map/ppermute | solution.py:522
  199.3 4.5 %collective-permute-start.37 = (bf16[16,1152]{1,0:T(8,128)(2,1)S(1)}, bf16[16,1152]{1,0:T(8,128)(2,1)S(1)}, u32[]{:S(2)}, u32[]{:S(2)}) collective-permute-start(bf16[16,1152]{1,0:T(8,128)(2,1)S(1)} %get-tuple-element.54), channel_id=1, source_target_pairs={{0,4},{4,0},{8,12},{12,8},{1,5},{5,1},{9,13},{13,9},{2,6},{6,2},{1... | collective-permute-start | bytes 110600 | tf_op jit(solution)/shard_map/ppermute | solution.py:516
  199.4 5.4 %collective-permute-start.38 = (bf16[16,1152]{1,0:T(8,128)(2,1)S(1)}, bf16[16,1152]{1,0:T(8,128)(2,1)S(1)}, u32[]{:S(2)}, u32[]{:S(2)}) collective-permute-start(bf16[16,1152]{1,0:T(8,128)(2,1)S(1)} %get-tuple-element.55), channel_id=1, source_target_pairs={{0,8},{4,12},{8,0},{12,4},{1,9},{5,13},{9,1},{13,5},{2,10},{6,14},... | collective-permute-start | bytes 110600 | tf_op jit(solution)/shard_map/ppermute | solution.py:516
  201.0 5.8 %collective-permute-start.39 = (bf16[16,1152]{1,0:T(8,128)(2,1)S(1)}, bf16[16,1152]{1,0:T(8,128)(2,1)S(1)}, u32[]{:S(2)}, u32[]{:S(2)}) collective-permute-start(bf16[16,1152]{1,0:T(8,128)(2,1)S(1)} %get-tuple-element.56), channel_id=1, source_target_pairs={{0,12},{4,8},{8,4},{12,0},{1,13},{5,9},{9,5},{13,1},{2,14},{6,10},... | collective-permute-start | bytes 110600 | tf_op jit(solution)/shard_map/ppermute | solution.py:516
  206.8 17.1 %copy-start.7 = (bf16[1024,1024]{1,0:T(8,128)(2,1)S(1)}, bf16[1024,1024]{1,0:T(8,128)(2,1)}, u32[]{:S(2)}) copy-start(bf16[1024,1024]{1,0:T(8,128)(2,1)} %up_ref.1) | copy-start | bytes 6291460
  208.3 4.5 %collective-permute-start.41 = (bf16[16,1024]{1,0:T(8,128)(2,1)S(1)}, bf16[16,1024]{1,0:T(8,128)(2,1)S(1)}, u32[]{:S(2)}, u32[]{:S(2)}) collective-permute-start(bf16[16,1024]{1,0:T(8,128)(2,1)S(1)} %get-tuple-element.60), channel_id=1, source_target_pairs={{0,4},{4,0},{8,12},{12,8},{1,5},{5,1},{9,13},{13,9},{2,6},{6,2},{1... | collective-permute-start | bytes 98312 | tf_op jit(solution)/shard_map/ppermute | solution.py:516
  208.4 5.5 %collective-permute-start.42 = (bf16[16,1024]{1,0:T(8,128)(2,1)S(1)}, bf16[16,1024]{1,0:T(8,128)(2,1)S(1)}, u32[]{:S(2)}, u32[]{:S(2)}) collective-permute-start(bf16[16,1024]{1,0:T(8,128)(2,1)S(1)} %get-tuple-element.61), channel_id=1, source_target_pairs={{0,8},{4,12},{8,0},{12,4},{1,9},{5,13},{9,1},{13,5},{2,10},{6,14},... | collective-permute-start | bytes 98312 | tf_op jit(solution)/shard_map/ppermute | solution.py:516
  211.7 5.7 %collective-permute-start.43 = (bf16[16,1024]{1,0:T(8,128)(2,1)S(1)}, bf16[16,1024]{1,0:T(8,128)(2,1)S(1)}, u32[]{:S(2)}, u32[]{:S(2)}) collective-permute-start(bf16[16,1024]{1,0:T(8,128)(2,1)S(1)} %get-tuple-element.62), channel_id=1, source_target_pairs={{0,12},{4,8},{8,4},{12,0},{1,13},{5,9},{9,5},{13,1},{2,14},{6,10},... | collective-permute-start | bytes 98312 | tf_op jit(solution)/shard_map/ppermute | solution.py:516
  217.4 5.0 %collective-permute-start.44 = (bf16[64,1024]{1,0:T(8,128)(2,1)S(1)}, bf16[64,1024]{1,0:T(8,128)(2,1)S(1)}, u32[]{:S(2)}, u32[]{:S(2)}) collective-permute-start(bf16[64,1024]{1,0:T(8,128)(2,1)S(1)} %shard_map.173.refs_0_), channel_id=1, source_target_pairs={{0,2},{1,3},{2,0},{3,1},{4,6},{5,7},{6,4},{7,5},{8,10},{9,11},{10,... | collective-permute-start | bytes 393224 | tf_op jit(solution)/shard_map/ppermute | solution.py:522
  222.5 1.4 collective-permute-start.45
